TPU v7x, 256 devices: a whole 4x4x8 slice. The times are simulated.
256 devices in a mesh: probe: 4 (over x), space: 64 (over y, z, core).
Axes of the slice: x: 4, y: 4, z: 8, core: 2. Of those that a mesh axis runs over, the one named last changes fastest.
Arguments:
- courant_field: float32 [128, 32, 256], P('space'), may hold values from 0.05 to 0.3
- probe_fields: float32 [16, 128, 32, 256], P('probe', 'space'), may hold values from -6 to 6
- prior_weight: float32 [128, 32, 256], P('space'), may hold values from 0.5 to 5
- source_cells: int32 [4096], P('space'), may hold values from 0 to 1048575, as said below
- source_strength: float32 [4096], P('space'), may hold values from -6 to 6
- wavelet: float32 [8], replicated, may hold values from -4 to 4
- receiver_cells: int32 [4096], P('space'), may hold values from 0 to 1048575, as said below
- receiver_weight: float32 [4096], P('space'), may hold values from 1 to 10
Outputs:
- hessian_fields: float32 [16, 128, 32, 256], P('probe', 'space')
- basis: float32 [16, 128, 32, 256], P('probe', 'space')
Inputs may be any that keep to these rules, and one draw needn't show every extreme that they name: `source_cells`: entries k * 64 to (k + 1) * 64 - 1 are cells of the k-th slab of 2 planes along the first dimension; cells may repeat. `receiver_cells`: entries k * 64 to (k + 1) * 64 - 1 are cells of the k-th slab of 2 planes along the first dimension; cells may repeat.
All inputs are finite; a program needn't handle non-finite values.
Results may differ from a plain program's by a relative error of at most 0.0019.
Values sent between devices are 32-bit elements; how exact they have to be, the bound alone decides.
No kernel may reach another device: no remote copies, remote signals or barrier semaphores. Data moves between devices by JAX's collectives and lax.ppermute only.
A program may use at most 64 MiB of HBM per device.

v0:
```python
import jax
import jax.numpy as jnp
from jax import lax
from jax.sharding import PartitionSpec as P


def extended(block, sides, width):
    for axis, dim in sides:
        count = lax.axis_size(axis)
        forward = [(i, i + 1) for i in range(count - 1)]
        backward = [(target, source) for source, target in forward]
        low = lax.ppermute(
            lax.slice_in_dim(block, block.shape[dim] - width, None, axis=dim), axis, forward
        )
        high = lax.ppermute(lax.slice_in_dim(block, 0, width, axis=dim), axis, backward)
        block = jnp.concatenate([low, block, high], axis=dim)
    return block


def laplace_local(padded, center):
    side = jnp.pad(center, ((0, 0), (0, 0), (1, 1), (1, 1)))
    total = padded[:, 2:] + padded[:, :-2]
    total = total + side[:, :, 2:, 1:-1] + side[:, :, :-2, 1:-1]
    total = total + side[:, :, 1:-1, 2:] + side[:, :, 1:-1, :-2]
    return total - 6.0 * center


def inject(values, local_cells, field_shape):
    flat = jnp.zeros(
        (field_shape[0], field_shape[1] * field_shape[2] * field_shape[3]), jnp.float32
    )
    return flat.at[:, local_cells].add(values).reshape(field_shape)


def inner_rows(rows):
    return lax.dot_general(
        rows,
        rows,
        (((1,), (1,)), ((), ())),
        precision=lax.Precision.HIGHEST,
        preferred_element_type=jnp.float32,
    )


def shards(
    courant_field,
    probe_fields,
    prior_weight,
    source_cells,
    source_strength,
    wavelet,
    receiver_cells,
    receiver_weight,
):
    field_shape = probe_fields.shape
    groups = field_shape[0]
    cells = field_shape[1] * field_shape[2] * field_shape[3]
    steps_total = wavelet.shape[0]
    offset = lax.axis_index("space") * cells
    source_local = source_cells - offset
    receiver_local = receiver_cells - offset
    source_field = (
        jnp.zeros((cells,), jnp.float32)
        .at[source_local]
        .add(source_strength)
        .reshape(field_shape[1:])
    )
    state_prev = jnp.zeros((groups + 1,) + field_shape[1:], jnp.float32)
    state_now = jnp.concatenate(
        [(wavelet[0] * source_field)[None], jnp.zeros(field_shape, jnp.float32)], 0
    )
    drives = [None]
    records = [None]
    for step in range(1, steps_total):
        padded = extended(state_now, (("space", 1),), 1)
        bent = laplace_local(padded, state_now)
        drive = courant_field * bent[0]
        forcing = jnp.concatenate(
            [(wavelet[step] * source_field)[None], probe_fields * drive[None]], 0
        )
        state_next = 2.0 * state_now - state_prev + courant_field * bent + forcing
        drives.append(drive)
        records.append(jnp.take(state_next[1:].reshape(groups, cells), receiver_local, axis=1))
        state_prev, state_now = (state_now, state_next)
    adjoint_next = inject(receiver_weight * records[steps_total - 1], receiver_local, field_shape)
    adjoint_after = jnp.zeros(field_shape, jnp.float32)
    hessian = prior_weight * probe_fields + drives[steps_total - 1] * adjoint_next
    for level in range(steps_total - 1, 1, -1):
        scaled = courant_field * adjoint_next
        padded = extended(scaled, (("space", 1),), 1)
        injected = inject(receiver_weight * records[level - 1], receiver_local, field_shape)
        adjoint_now = 2.0 * adjoint_next - adjoint_after + laplace_local(padded, scaled) + injected
        hessian = hessian + drives[level - 1] * adjoint_now
        adjoint_after, adjoint_next = (adjoint_next, adjoint_now)
    flat = hessian.reshape(groups, cells)
    total_cells = cells * lax.axis_size("space")
    rows = lax.all_gather(flat, "probe", axis=0, tiled=True)
    gram = lax.psum(inner_rows(rows), "space") / total_cells
    lower = jnp.linalg.cholesky(gram)
    solved = lax.linalg.triangular_solve(lower, rows, left_side=True, lower=True)
    mine = lax.dynamic_slice_in_dim(solved, lax.axis_index("probe") * groups, groups, 0)
    return (hessian, mine.reshape(field_shape))


def solution(mesh):
    in_specs = (
        P("space", None, None),
        P("probe", "space", None, None),
        P("space", None, None),
        P("space"),
        P("space"),
        P(),
        P("space"),
        P("space"),
    )
    out_specs = (P("probe", "space", None, None), P("probe", "space", None, None))
    return jax.shard_map(shards, mesh=mesh, in_specs=in_specs, out_specs=out_specs, check_vma=False)
```

profile of v0, /device:TPU:1, one launch (start us, length us, event | category | flops | bytes accessed | tf_op | source)
XLA Modules:
  0.0 435.4 jit_solution(6910389396807057819)
XLA Ops:
  10.6 5.0 %broadcast_multiply_fusion.13 = (f32[16384]{0:T(1024)S(1)}, f32[16384]{0:T(1024)S(1)}, f32[16384]{0:T(1024)S(1)}, f32[16384]{0:T(1024)S(1)}, f32[16384]{0:T(1024...) fusion(f32[16384]{0:T(1024)S(1)} %scatter_custom_fusion, f32[]{:T(128)} %bitcast.14, f32[]{:T(128)} %bitcast.11, ...), kind=kLoop, calls=%fused_computation.264 | loop fusion | flops 131072 | bytes 589856 | tf_op jit(solution)/shard_map/mul | solution.py:79
  15.7 4.9 %collective-permute-start.1 = (f32[5,1,32,256]{3,2,1,0:T(8,128)S(1)}, f32[5,1,32,256]{3,2,1,0:T(8,128)S(1)}, u32[]{:S(2)}, u32[]{:S(2)}) collective-permute-start(f32[5,1,32,256]{3,2,1,0:T(8,128)S(1)} %get-tuple-element.51), channel_id=1, source_target_pairs={{0,1},{1,2},{2,3},{3,4},{4,5},{5,6},{6,7},{7,8},{8,9},{9,10},{10,1... | collective-permute-start | bytes 491528 | tf_op jit(solution)/shard_map/ppermute | solution.py:12
  22.8 4.4 %collective-permute-done = f32[5,1,32,256]{3,2,1,0:T(8,128)S(1)} collective-permute-done((f32[5,1,32,256]{3,2,1,0:T(8,128)S(1)}, f32[5,1,32,256]{3,2,1,0:T(8,128)S(1)}, u32[]{:S(2)}, u32[]{:S(2)}) %collective-permute-start) | collective-permute-done | bytes 163872 | tf_op jit(solution)/shard_map/ppermute | solution.py:15
  34.8 4.5 %collective-permute-done.2 = f32[5,1,32,256]{3,2,1,0:T(8,128)S(1)} collective-permute-done((f32[5,1,32,256]{3,2,1,0:T(8,128)S(1)}, f32[5,1,32,256]{3,2,1,0:T(8,128)S(1)}, u32[]{:S(2)}, u32[]{:S(2)}) %collective-permute-start.2) | collective-permute-done | bytes 163872 | tf_op jit(solution)/shard_map/ppermute | solution.py:15
  46.9 4.5 %collective-permute-done.4 = f32[5,1,32,256]{3,2,1,0:T(8,128)S(1)} collective-permute-done((f32[5,1,32,256]{3,2,1,0:T(8,128)S(1)}, f32[5,1,32,256]{3,2,1,0:T(8,128)S(1)}, u32[]{:S(2)}, u32[]{:S(2)}) %collective-permute-start.4) | collective-permute-done | bytes 163872 | tf_op jit(solution)/shard_map/ppermute | solution.py:15
  56.4 6.9 %collective-permute-done.6 = f32[5,1,32,256]{3,2,1,0:T(8,128)S(1)} collective-permute-done((f32[5,1,32,256]{3,2,1,0:T(8,128)S(1)}, f32[5,1,32,256]{3,2,1,0:T(8,128)S(1)}, u32[]{:S(2)}, u32[]{:S(2)}) %collective-permute-start.6) | collective-permute-done | bytes 163872 | tf_op jit(solution)/shard_map/ppermute | solution.py:15
  68.3 5.4 %collective-permute-done.8 = f32[5,1,32,256]{3,2,1,0:T(8,128)S(1)} collective-permute-done((f32[5,1,32,256]{3,2,1,0:T(8,128)S(1)}, f32[5,1,32,256]{3,2,1,0:T(8,128)S(1)}, u32[]{:S(2)}, u32[]{:S(2)}) %collective-permute-start.8) | collective-permute-done | bytes 163872 | tf_op jit(solution)/shard_map/ppermute | solution.py:15
  78.7 5.4 %collective-permute-done.10 = f32[5,1,32,256]{3,2,1,0:T(8,128)S(1)} collective-permute-done((f32[5,1,32,256]{3,2,1,0:T(8,128)S(1)}, f32[5,1,32,256]{3,2,1,0:T(8,128)S(1)}, u32[]{:S(2)}, u32[]{:S(2)}) %collective-permute-start.10) | collective-permute-done | bytes 163872 | tf_op jit(solution)/shard_map/ppermute | solution.py:15
  89.7 5.4 %collective-permute-done.12 = f32[5,1,32,256]{3,2,1,0:T(8,128)S(1)} collective-permute-done((f32[5,1,32,256]{3,2,1,0:T(8,128)S(1)}, f32[5,1,32,256]{3,2,1,0:T(8,128)S(1)}, u32[]{:S(2)}, u32[]{:S(2)}) %collective-permute-start.12) | collective-permute-done | bytes 163872 | tf_op jit(solution)/shard_map/ppermute | solution.py:15
  95.5 4.7 %copy.29 = f32[4,2,32,256]{0,3,2,1:T(8,128)} copy(f32[4,2,32,256]{3,2,1,0:T(8,128)S(1)} %get-tuple-element.15) | data formatting | bytes 524288 | tf_op jit(solution)/shard_map/slice | solution.py:83
  100.2 5.5 %scatter_custom_fusion.1 = f32[4,16384]{0,1:T(8,128)} fusion(s32[64]{0:T(128)S(1)} %get-tuple-element.14, f32[]{:T(128)} %constant.69.clone.1, f32[]{:T(128)} %constant.78.clone.1, f32[64]{0:T(128)S(1)} %copy-done.10, pred[64]{0:T(512)(128)(4,1)S(1)} %get-tuple-element.13, f32[4,16384]{0,1:T(8,128)} %bitcast.125, s32[1024]{0:T(1024)S(1)} %pad_clamp_fusion), kind=kCustom, calls=%fused_computation.27 | custom fusion | flops 768 | bytes 529416 | tf_op jit(solution)/shard_map/scatter-add | solution.py:32
  105.7 5.2 %copy.30 = f32[4,2,32,256]{3,2,1,0:T(8,128)S(1)} copy(f32[4,2,32,256]{0,3,2,1:T(8,128)} %bitcast.126) | data formatting | bytes 524288 | tf_op jit(solution)/shard_map/reshape | solution.py:32
  116.0 4.7 %copy.33 = f32[4,2,32,256]{0,3,2,1:T(8,128)} copy(f32[4,2,32,256]{3,2,1,0:T(8,128)S(1)} %get-tuple-element.16) | data formatting | bytes 524288 | tf_op jit(solution)/shard_map/slice | solution.py:83
  120.8 5.5 %scatter_custom_fusion.2 = f32[4,16384]{0,1:T(8,128)} fusion(s32[64]{0:T(128)S(1)} %get-tuple-element.14, f32[]{:T(128)} %constant.69.clone.1, f32[]{:T(128)} %constant.78.clone.1, f32[64]{0:T(128)S(1)} %copy-done.10, pred[64]{0:T(512)(128)(4,1)S(1)} %get-tuple-element.13, f32[4,16384]{0,1:T(8,128)} %bitcast.127, s32[1024]{0:T(1024)S(1)} %pad_clamp_fusion), kind=kCustom, calls=%fused_computation.25 | custom fusion | flops 768 | bytes 529416 | tf_op jit(solution)/shard_map/scatter-add | solution.py:32
  126.3 5.2 %copy.34 = f32[4,2,32,256]{3,2,1,0:T(8,128)S(1)} copy(f32[4,2,32,256]{0,3,2,1:T(8,128)} %bitcast.128) | data formatting | bytes 524288 | tf_op jit(solution)/shard_map/reshape | solution.py:32
  139.9 4.7 %copy.36 = f32[4,2,32,256]{0,3,2,1:T(8,128)} copy(f32[4,2,32,256]{3,2,1,0:T(8,128)S(1)} %get-tuple-element.17) | data formatting | bytes 524288 | tf_op jit(solution)/shard_map/slice | solution.py:83
  144.6 5.5 %scatter_custom_fusion.3 = f32[4,16384]{0,1:T(8,128)} fusion(s32[64]{0:T(128)S(1)} %get-tuple-element.14, f32[]{:T(128)} %constant.69.clone.1, f32[]{:T(128)} %constant.78.clone.1, f32[64]{0:T(128)S(1)} %copy-done.10, pred[64]{0:T(512)(128)(4,1)S(1)} %get-tuple-element.13, f32[4,16384]{0,1:T(8,128)} %bitcast.129, s32[1024]{0:T(1024)S(1)} %pad_clamp_fusion), kind=kCustom, calls=%fused_computation.23 | custom fusion | flops 768 | bytes 529416 | tf_op jit(solution)/shard_map/scatter-add | solution.py:32
  150.2 5.2 %copy.37 = f32[4,2,32,256]{3,2,1,0:T(8,128)S(1)} copy(f32[4,2,32,256]{0,3,2,1:T(8,128)} %bitcast.130) | data formatting | bytes 524288 | tf_op jit(solution)/shard_map/reshape | solution.py:32
  163.0 4.7 %copy.38 = f32[4,2,32,256]{0,3,2,1:T(8,128)} copy(f32[4,2,32,256]{3,2,1,0:T(8,128)S(1)} %slice.584) | data formatting | bytes 524288 | tf_op jit(solution)/shard_map/slice | solution.py:83
  167.7 5.5 %scatter_custom_fusion.4 = f32[4,16384]{0,1:T(8,128)} fusion(s32[64]{0:T(128)S(1)} %get-tuple-element.14, f32[]{:T(128)} %constant.69.clone.1, f32[]{:T(128)} %constant.78.clone.1, f32[64]{0:T(128)S(1)} %copy-done.10, pred[64]{0:T(512)(128)(4,1)S(1)} %get-tuple-element.13, f32[4,16384]{0,1:T(8,128)} %bitcast.131, s32[1024]{0:T(1024)S(1)} %pad_clamp_fusion), kind=kCustom, calls=%fused_computation.21 | custom fusion | flops 768 | bytes 529416 | tf_op jit(solution)/shard_map/scatter-add | solution.py:32
  173.2 5.2 %copy.39 = f32[4,2,32,256]{3,2,1,0:T(8,128)S(1)} copy(f32[4,2,32,256]{0,3,2,1:T(8,128)} %bitcast.132) | data formatting | bytes 524288 | tf_op jit(solution)/shard_map/reshape | solution.py:32
  186.0 4.7 %copy.40 = f32[4,2,32,256]{0,3,2,1:T(8,128)} copy(f32[4,2,32,256]{3,2,1,0:T(8,128)S(1)} %slice.587) | data formatting | bytes 524288 | tf_op jit(solution)/shard_map/slice | solution.py:83
  190.7 5.5 %scatter_custom_fusion.5 = f32[4,16384]{0,1:T(8,128)} fusion(s32[64]{0:T(128)S(1)} %get-tuple-element.14, f32[]{:T(128)} %constant.69.clone.1, f32[]{:T(128)} %constant.78.clone.1, f32[64]{0:T(128)S(1)} %copy-done.10, pred[64]{0:T(512)(128)(4,1)S(1)} %get-tuple-element.13, f32[4,16384]{0,1:T(8,128)} %bitcast.133, s32[1024]{0:T(1024)S(1)} %pad_clamp_fusion), kind=kCustom, calls=%fused_computation.19 | custom fusion | flops 768 | bytes 529416 | tf_op jit(solution)/shard_map/scatter-add | solution.py:32
  196.3 5.2 %copy.41 = f32[4,2,32,256]{3,2,1,0:T(8,128)S(1)} copy(f32[4,2,32,256]{0,3,2,1:T(8,128)} %bitcast.134) | data formatting | bytes 524288 | tf_op jit(solution)/shard_map/reshape | solution.py:32
  208.3 4.7 %copy.42 = f32[4,2,32,256]{0,3,2,1:T(8,128)} copy(f32[4,2,32,256]{3,2,1,0:T(8,128)S(1)} %slice.590) | data formatting | bytes 524288 | tf_op jit(solution)/shard_map/slice | solution.py:83
  213.1 5.5 %scatter_custom_fusion.6 = f32[4,16384]{0,1:T(8,128)} fusion(s32[64]{0:T(128)S(1)} %get-tuple-element.14, f32[]{:T(128)} %constant.69.clone.1, f32[]{:T(128)} %constant.78.clone.1, f32[64]{0:T(128)S(1)} %copy-done.10, pred[64]{0:T(512)(128)(4,1)S(1)} %get-tuple-element.13, f32[4,16384]{0,1:T(8,128)} %bitcast.135, s32[1024]{0:T(1024)S(1)} %pad_clamp_fusion), kind=kCustom, calls=%fused_computation.17 | custom fusion | flops 768 | bytes 529416 | tf_op jit(solution)/shard_map/scatter-add | solution.py:32
  218.6 5.2 %copy.43 = f32[4,2,32,256]{3,2,1,0:T(8,128)S(1)} copy(f32[4,2,32,256]{0,3,2,1:T(8,128)} %bitcast.136) | data formatting | bytes 524288 | tf_op jit(solution)/shard_map/reshape | solution.py:32
  230.9 4.7 %copy.44 = f32[4,2,32,256]{0,3,2,1:T(8,128)} copy(f32[4,2,32,256]{3,2,1,0:T(8,128)S(1)} %slice.593) | data formatting | bytes 524288 | tf_op jit(solution)/shard_map/slice | solution.py:83
  235.7 5.5 %scatter_custom_fusion.7 = f32[4,16384]{0,1:T(8,128)} fusion(s32[64]{0:T(128)S(1)} %get-tuple-element.14, f32[]{:T(128)} %constant.69.clone.1, f32[]{:T(128)} %constant.78.clone.1, f32[64]{0:T(128)S(1)} %copy-done.10, pred[64]{0:T(512)(128)(4,1)S(1)} %get-tuple-element.13, f32[4,16384]{0,1:T(8,128)} %bitcast.123, s32[1024]{0:T(1024)S(1)} %pad_clamp_fusion), kind=kCustom, calls=%fused_computation.15 | custom fusion | flops 768 | bytes 529416 | tf_op jit(solution)/shard_map/scatter-add | solution.py:32
  241.2 5.3 %copy.45 = f32[4,2,32,256]{3,2,1,0:T(8,128)S(1)} copy(f32[4,2,32,256]{0,3,2,1:T(8,128)} %bitcast.124) | data formatting | bytes 524288 | tf_op jit(solution)/shard_map/reshape | solution.py:32
  249.4 41.3 %all-gather.3.cloned.1.call-done = f32[4,4,16384]{2,1,0:T(4,128)} async-done(((f32[1,4,16384]{2,1,0:T(4,128)}), f32[4,4,16384]{2,1,0:T(4,128)}) %all-gather.3.cloned.1.call-update) | async-done | bytes 1048592 | tf_op jit(solution)/shard_map/all_gather | solution.py:97
  293.8 128.7 %psum.7 = f32[16,16]{0,1:T(8,128)S(1)} all-reduce(f32[16,16]{0,1:T(8,128)S(1)} %fusion.185), channel_id=1, replica_groups=mesh['probe'=4,'space'=64] {'space'}, use_global_device_ids=true, to_apply=%region_8.10 | all-reduce | flops 256 | bytes 2048 | tf_op jit(solution)/shard_map/psum | solution.py:98
  (150 shorter events, 95.5 us)
Async XLA Ops:
  7.2 44.4 %copy-start = (f32[2,32,256]{2,1,0:T(8,128)S(1)}, f32[2,32,256]{2,1,0:T(8,128)}, u32[]{:S(2)}) copy-start(f32[2,32,256]{2,1,0:T(8,128)} %param.10) | copy-start | bytes 196612
  7.2 44.4 %copy-start.1 = (f32[4,2,32,256]{3,2,1,0:T(8,128)S(1)}, f32[4,2,32,256]{3,2,1,0:T(8,128)}, u32[]{:S(2)}) copy-start(f32[4,2,32,256]{3,2,1,0:T(8,128)} %param.11) | copy-start | bytes 786436
  7.2 283.5 %all-gather.3.cloned.1.call-start = ((), (), s32[]{:S(2)}) async-start(), calls=%async_computation | async-start | bytes 1310720 | tf_op jit(solution)/shard_map/all_gather | solution.py:97
  15.7 7.2 %collective-permute-start.1 = (f32[5,1,32,256]{3,2,1,0:T(8,128)S(1)}, f32[5,1,32,256]{3,2,1,0:T(8,128)S(1)}, u32[]{:S(2)}, u32[]{:S(2)}) collective-permute-start(f32[5,1,32,256]{3,2,1,0:T(8,128)S(1)} %get-tuple-element.51), channel_id=1, source_target_pairs={{0,1},{1,2},{2,3},{3,4},{4,5},{5,6},{6,7},{7,8},{8,9},{9,10},{10,1... | collective-permute-start | bytes 491528 | tf_op jit(solution)/shard_map/ppermute | solution.py:12
  20.6 6.6 %collective-permute-start = (f32[5,1,32,256]{3,2,1,0:T(8,128)S(1)}, f32[5,1,32,256]{3,2,1,0:T(8,128)S(1)}, u32[]{:S(2)}, u32[]{:S(2)}) collective-permute-start(f32[5,1,32,256]{3,2,1,0:T(8,128)S(1)} %get-tuple-element.50), channel_id=1, source_target_pairs={{1,0},{2,1},{3,2},{4,3},{5,4},{6,5},{7,6},{8,7},{9,8},{10,9},{11,1... | collective-permute-start | bytes 491528 | tf_op jit(solution)/shard_map/ppermute | solution.py:15
  30.4 4.4 %collective-permute-start.3 = (f32[5,1,32,256]{3,2,1,0:T(8,128)S(1)}, f32[5,1,32,256]{3,2,1,0:T(8,128)S(1)}, u32[]{:S(2)}, u32[]{:S(2)}) collective-permute-start(f32[5,1,32,256]{3,2,1,0:T(8,128)S(1)} %get-tuple-element.29), channel_id=1, source_target_pairs={{0,1},{1,2},{2,3},{3,4},{4,5},{5,6},{6,7},{7,8},{8,9},{9,10},{10,1... | collective-permute-start | bytes 491528 | tf_op jit(solution)/shard_map/ppermute | solution.py:12
  32.4 6.9 %collective-permute-start.2 = (f32[5,1,32,256]{3,2,1,0:T(8,128)S(1)}, f32[5,1,32,256]{3,2,1,0:T(8,128)S(1)}, u32[]{:S(2)}, u32[]{:S(2)}) collective-permute-start(f32[5,1,32,256]{3,2,1,0:T(8,128)S(1)} %get-tuple-element.28), channel_id=1, source_target_pairs={{1,0},{2,1},{3,2},{4,3},{5,4},{6,5},{7,6},{8,7},{9,8},{10,9},{11,1... | collective-permute-start | bytes 491528 | tf_op jit(solution)/shard_map/ppermute | solution.py:15
  42.5 4.4 %collective-permute-start.5 = (f32[5,1,32,256]{3,2,1,0:T(8,128)S(1)}, f32[5,1,32,256]{3,2,1,0:T(8,128)S(1)}, u32[]{:S(2)}, u32[]{:S(2)}) collective-permute-start(f32[5,1,32,256]{3,2,1,0:T(8,128)S(1)} %get-tuple-element.27), channel_id=1, source_target_pairs={{0,1},{1,2},{2,3},{3,4},{4,5},{5,6},{6,7},{7,8},{8,9},{9,10},{10,1... | collective-permute-start | bytes 491528 | tf_op jit(solution)/shard_map/ppermute | solution.py:12
  44.4 6.9 %collective-permute-start.4 = (f32[5,1,32,256]{3,2,1,0:T(8,128)S(1)}, f32[5,1,32,256]{3,2,1,0:T(8,128)S(1)}, u32[]{:S(2)}, u32[]{:S(2)}) collective-permute-start(f32[5,1,32,256]{3,2,1,0:T(8,128)S(1)} %get-tuple-element.26), channel_id=1, source_target_pairs={{1,0},{2,1},{3,2},{4,3},{5,4},{6,5},{7,6},{8,7},{9,8},{10,9},{11,1... | collective-permute-start | bytes 491528 | tf_op jit(solution)/shard_map/ppermute | solution.py:15
  46.9 42.8 %copy-start.11 = (s32[64]{0:T(128)S(1)}, s32[64]{0:T(128)}, u32[]{:S(2)}) copy-start(s32[64]{0:T(128)} %param.16) | copy-start | bytes 772
  52.0 4.4 %collective-permute-start.7 = (f32[5,1,32,256]{3,2,1,0:T(8,128)S(1)}, f32[5,1,32,256]{3,2,1,0:T(8,128)S(1)}, u32[]{:S(2)}, u32[]{:S(2)}) collective-permute-start(f32[5,1,32,256]{3,2,1,0:T(8,128)S(1)} %get-tuple-element.25), channel_id=1, source_target_pairs={{0,1},{1,2},{2,3},{3,4},{4,5},{5,6},{6,7},{7,8},{8,9},{9,10},{10,1... | collective-permute-start | bytes 491528 | tf_op jit(solution)/shard_map/ppermute | solution.py:12
  53.9 9.3 %collective-permute-start.6 = (f32[5,1,32,256]{3,2,1,0:T(8,128)S(1)}, f32[5,1,32,256]{3,2,1,0:T(8,128)S(1)}, u32[]{:S(2)}, u32[]{:S(2)}) collective-permute-start(f32[5,1,32,256]{3,2,1,0:T(8,128)S(1)} %get-tuple-element.24), channel_id=1, source_target_pairs={{1,0},{2,1},{3,2},{4,3},{5,4},{6,5},{7,6},{8,7},{9,8},{10,9},{11,1... | collective-permute-start | bytes 491528 | tf_op jit(solution)/shard_map/ppermute | solution.py:15
  63.9 4.4 %collective-permute-start.9 = (f32[5,1,32,256]{3,2,1,0:T(8,128)S(1)}, f32[5,1,32,256]{3,2,1,0:T(8,128)S(1)}, u32[]{:S(2)}, u32[]{:S(2)}) collective-permute-start(f32[5,1,32,256]{3,2,1,0:T(8,128)S(1)} %get-tuple-element.23), channel_id=1, source_target_pairs={{0,1},{1,2},{2,3},{3,4},{4,5},{5,6},{6,7},{7,8},{8,9},{9,10},{10,1... | collective-permute-start | bytes 491528 | tf_op jit(solution)/shard_map/ppermute | solution.py:12
  65.8 7.8 %collective-permute-start.8 = (f32[5,1,32,256]{3,2,1,0:T(8,128)S(1)}, f32[5,1,32,256]{3,2,1,0:T(8,128)S(1)}, u32[]{:S(2)}, u32[]{:S(2)}) collective-permute-start(f32[5,1,32,256]{3,2,1,0:T(8,128)S(1)} %get-tuple-element.22), channel_id=1, source_target_pairs={{1,0},{2,1},{3,2},{4,3},{5,4},{6,5},{7,6},{8,7},{9,8},{10,9},{11,1... | collective-permute-start | bytes 491528 | tf_op jit(solution)/shard_map/ppermute | solution.py:15
  74.3 4.4 %collective-permute-start.11 = (f32[5,1,32,256]{3,2,1,0:T(8,128)S(1)}, f32[5,1,32,256]{3,2,1,0:T(8,128)S(1)}, u32[]{:S(2)}, u32[]{:S(2)}) collective-permute-start(f32[5,1,32,256]{3,2,1,0:T(8,128)S(1)} %get-tuple-element.21), channel_id=1, source_target_pairs={{0,1},{1,2},{2,3},{3,4},{4,5},{5,6},{6,7},{7,8},{8,9},{9,10},{10,1... | collective-permute-start | bytes 491528 | tf_op jit(solution)/shard_map/ppermute | solution.py:12
  76.2 7.8 %collective-permute-start.10 = (f32[5,1,32,256]{3,2,1,0:T(8,128)S(1)}, f32[5,1,32,256]{3,2,1,0:T(8,128)S(1)}, u32[]{:S(2)}, u32[]{:S(2)}) collective-permute-start(f32[5,1,32,256]{3,2,1,0:T(8,128)S(1)} %get-tuple-element.20), channel_id=1, source_target_pairs={{1,0},{2,1},{3,2},{4,3},{5,4},{6,5},{7,6},{8,7},{9,8},{10,9},{11,1... | collective-permute-start | bytes 491528 | tf_op jit(solution)/shard_map/ppermute | solution.py:15
  78.6 21.6 %copy-start.10 = (f32[64]{0:T(128)S(1)}, f32[64]{0:T(128)}, u32[]{:S(2)}) copy-start(f32[64]{0:T(128)} %param.17) | copy-start | bytes 772
  85.3 4.4 %collective-permute-start.13 = (f32[5,1,32,256]{3,2,1,0:T(8,128)S(1)}, f32[5,1,32,256]{3,2,1,0:T(8,128)S(1)}, u32[]{:S(2)}, u32[]{:S(2)}) collective-permute-start(f32[5,1,32,256]{3,2,1,0:T(8,128)S(1)} %get-tuple-element.19), channel_id=1, source_target_pairs={{0,1},{1,2},{2,3},{3,4},{4,5},{5,6},{6,7},{7,8},{8,9},{9,10},{10,1... | collective-permute-start | bytes 491528 | tf_op jit(solution)/shard_map/ppermute | solution.py:12
  87.2 7.8 %collective-permute-start.12 = (f32[5,1,32,256]{3,2,1,0:T(8,128)S(1)}, f32[5,1,32,256]{3,2,1,0:T(8,128)S(1)}, u32[]{:S(2)}, u32[]{:S(2)}) collective-permute-start(f32[5,1,32,256]{3,2,1,0:T(8,128)S(1)} %get-tuple-element.18), channel_id=1, source_target_pairs={{1,0},{2,1},{3,2},{4,3},{5,4},{6,5},{7,6},{8,7},{9,8},{10,9},{11,1... | collective-permute-start | bytes 491528 | tf_op jit(solution)/shard_map/ppermute | solution.py:15
  111.7 19.8 %collective-permute-start.15 = (f32[4,1,32,256]{3,2,1,0:T(8,128)}, f32[4,1,32,256]{3,2,1,0:T(8,128)S(1)}, u32[]{:S(2)}, u32[]{:S(2)}) collective-permute-start(f32[4,1,32,256]{3,2,1,0:T(8,128)} %get-tuple-element.41), channel_id=1, source_target_pairs={{0,1},{1,2},{2,3},{3,4},{4,5},{5,6},{6,7},{7,8},{8,9},{9,10},{10,1... | collective-permute-start | bytes 393224 | tf_op jit(solution)/shard_map/ppermute | solution.py:12
  113.6 18.6 %collective-permute-start.14 = (f32[4,1,32,256]{3,2,1,0:T(8,128)S(1)}, f32[4,1,32,256]{3,2,1,0:T(8,128)}, u32[]{:S(2)}, u32[]{:S(2)}) collective-permute-start(f32[4,1,32,256]{3,2,1,0:T(8,128)S(1)} %get-tuple-element.40), channel_id=1, source_target_pairs={{1,0},{2,1},{3,2},{4,3},{5,4},{6,5},{7,6},{8,7},{9,8},{10,9},{11,1... | collective-permute-start | bytes 393224 | tf_op jit(solution)/shard_map/ppermute | solution.py:15
  133.4 22.0 %collective-permute-start.17 = (f32[4,1,32,256]{3,2,1,0:T(8,128)S(1)}, f32[4,1,32,256]{3,2,1,0:T(8,128)}, u32[]{:S(2)}, u32[]{:S(2)}) collective-permute-start(f32[4,1,32,256]{3,2,1,0:T(8,128)S(1)} %get-tuple-element.39), channel_id=1, source_target_pairs={{0,1},{1,2},{2,3},{3,4},{4,5},{5,6},{6,7},{7,8},{8,9},{9,10},{10,1... | collective-permute-start | bytes 393224 | tf_op jit(solution)/shard_map/ppermute | solution.py:12
  137.8 17.6 %collective-permute-start.16 = (f32[4,1,32,256]{3,2,1,0:T(8,128)S(1)}, f32[4,1,32,256]{3,2,1,0:T(8,128)}, u32[]{:S(2)}, u32[]{:S(2)}) collective-permute-start(f32[4,1,32,256]{3,2,1,0:T(8,128)S(1)} %get-tuple-element.38), channel_id=1, source_target_pairs={{1,0},{2,1},{3,2},{4,3},{5,4},{6,5},{7,6},{8,7},{9,8},{10,9},{11,1... | collective-permute-start | bytes 393224 | tf_op jit(solution)/shard_map/ppermute | solution.py:15
  157.4 21.1 %collective-permute-start.19 = (f32[4,1,32,256]{3,2,1,0:T(8,128)}, f32[4,1,32,256]{3,2,1,0:T(8,128)}, u32[]{:S(2)}, u32[]{:S(2)}) collective-permute-start(f32[4,1,32,256]{3,2,1,0:T(8,128)} %get-tuple-element.37), channel_id=1, source_target_pairs={{0,1},{1,2},{2,3},{3,4},{4,5},{5,6},{6,7},{7,8},{8,9},{9,10},{10,1... | collective-permute-start | bytes 393224 | tf_op jit(solution)/shard_map/ppermute | solution.py:12
  161.0 17.5 %collective-permute-start.18 = (f32[4,1,32,256]{3,2,1,0:T(8,128)}, f32[4,1,32,256]{3,2,1,0:T(8,128)}, u32[]{:S(2)}, u32[]{:S(2)}) collective-permute-start(f32[4,1,32,256]{3,2,1,0:T(8,128)} %get-tuple-element.36), channel_id=1, source_target_pairs={{1,0},{2,1},{3,2},{4,3},{5,4},{6,5},{7,6},{8,7},{9,8},{10,9},{11,1... | collective-permute-start | bytes 393224 | tf_op jit(solution)/shard_map/ppermute | solution.py:15
  180.4 21.1 %collective-permute-start.21 = (f32[4,1,32,256]{3,2,1,0:T(8,128)}, f32[4,1,32,256]{3,2,1,0:T(8,128)}, u32[]{:S(2)}, u32[]{:S(2)}) collective-permute-start(f32[4,1,32,256]{3,2,1,0:T(8,128)} %get-tuple-element.35), channel_id=1, source_target_pairs={{0,1},{1,2},{2,3},{3,4},{4,5},{5,6},{6,7},{7,8},{8,9},{9,10},{10,1... | collective-permute-start | bytes 393224 | tf_op jit(solution)/shard_map/ppermute | solution.py:12
  184.0 17.5 %collective-permute-start.20 = (f32[4,1,32,256]{3,2,1,0:T(8,128)}, f32[4,1,32,256]{3,2,1,0:T(8,128)}, u32[]{:S(2)}, u32[]{:S(2)}) collective-permute-start(f32[4,1,32,256]{3,2,1,0:T(8,128)} %get-tuple-element.34), channel_id=1, source_target_pairs={{1,0},{2,1},{3,2},{4,3},{5,4},{6,5},{7,6},{8,7},{9,8},{10,9},{11,1... | collective-permute-start | bytes 393224 | tf_op jit(solution)/shard_map/ppermute | solution.py:15
  202.7 21.1 %collective-permute-start.23 = (f32[4,1,32,256]{3,2,1,0:T(8,128)S(1)}, f32[4,1,32,256]{3,2,1,0:T(8,128)}, u32[]{:S(2)}, u32[]{:S(2)}) collective-permute-start(f32[4,1,32,256]{3,2,1,0:T(8,128)S(1)} %get-tuple-element.33), channel_id=1, source_target_pairs={{0,1},{1,2},{2,3},{3,4},{4,5},{5,6},{6,7},{7,8},{8,9},{9,10},{10,1... | collective-permute-start | bytes 393224 | tf_op jit(solution)/shard_map/ppermute | solution.py:12
  206.4 17.5 %collective-permute-start.22 = (f32[4,1,32,256]{3,2,1,0:T(8,128)S(1)}, f32[4,1,32,256]{3,2,1,0:T(8,128)}, u32[]{:S(2)}, u32[]{:S(2)}) collective-permute-start(f32[4,1,32,256]{3,2,1,0:T(8,128)S(1)} %get-tuple-element.32), channel_id=1, source_target_pairs={{1,0},{2,1},{3,2},{4,3},{5,4},{6,5},{7,6},{8,7},{9,8},{10,9},{11,1... | collective-permute-start | bytes 393224 | tf_op jit(solution)/shard_map/ppermute | solution.py:15
  225.1 21.4 %collective-permute-start.25 = (f32[4,1,32,256]{3,2,1,0:T(8,128)S(1)}, f32[4,1,32,256]{3,2,1,0:T(8,128)S(1)}, u32[]{:S(2)}, u32[]{:S(2)}) collective-permute-start(f32[4,1,32,256]{3,2,1,0:T(8,128)S(1)} %get-tuple-element.31), channel_id=1, source_target_pairs={{0,1},{1,2},{2,3},{3,4},{4,5},{5,6},{6,7},{7,8},{8,9},{9,10},{10,1... | collective-permute-start | bytes 393224 | tf_op jit(solution)/shard_map/ppermute | solution.py:12
  228.8 17.8 %collective-permute-start.24 = (f32[4,1,32,256]{3,2,1,0:T(8,128)S(1)}, f32[4,1,32,256]{3,2,1,0:T(8,128)}, u32[]{:S(2)}, u32[]{:S(2)}) collective-permute-start(f32[4,1,32,256]{3,2,1,0:T(8,128)S(1)} %get-tuple-element.30), channel_id=1, source_target_pairs={{1,0},{2,1},{3,2},{4,3},{5,4},{6,5},{7,6},{8,7},{9,8},{10,9},{11,1... | collective-permute-start | bytes 393224 | tf_op jit(solution)/shard_map/ppermute | solution.py:15
  248.5 180.0 %copy-start.2 = (f32[4,2,32,256]{3,2,1,0:T(8,128)}, f32[4,2,32,256]{3,2,1,0:T(8,128)S(1)}, u32[]{:S(2)}) copy-start(f32[4,2,32,256]{3,2,1,0:T(8,128)S(1)} %fusion.103) | copy-start | bytes 786436
  (7 other events, 30.2 us)
Sparse Core Ops, SparseCore 0:
  249.5 41.1 all-gather.2
where the time goes:
time: 438 us; the launch traced here: 435 us
  blocking collectives  129 us (29%)
  local copies, waits for them, and re-layouts  79.3 us (18%)
  waiting for transfers between devices  78 us (18%)
  starting transfers between devices  66.1 us (15%)
  other arithmetic  65.7 us (15%)
  between operations  15 us (3%)
    psum x1, blocking collectives, shards(): gram = lax.psum(inner_rows(rows), 'space') / total_cells  129 us
    all_gather x1, waiting for transfers between devices, shards(): rows = lax.all_gather(flat, 'probe', axis=0, tiled=True)  41.3 us
    scatter-add x7, other arithmetic, inject(): return flat.at[:, local_cells].add(values).reshape(field_shape)  38.7 us
    ppermute x13, starting transfers between devices, extended(): lax.ppermute(lax.slice_in_dim(block, block.shape[dim] - width, None, axis...  37.3 us
    reshape x7, local copies, waits for them, and re-layouts, inject(): return flat.at[:, local_cells].add(values).reshape(field_shape)  36.7 us
    ppermute x13, waiting for transfers between devices, extended(): lax.ppermute(lax.slice_in_dim(block, 0, width, axis=dim), axis, backward)  36.3 us
    slice x11, local copies, waits for them, and re-layouts, shards(): state_next[1:].reshape(groups, cells)  33.2 us
    ppermute x13, starting transfers between devices, extended(): lax.ppermute(lax.slice_in_dim(block, 0, width, axis=dim), axis, backward)  28.8 us
  transfers between devices with their start and end apart: 27, of which 9 were waited for; matrix products, arithmetic and copies ran while one was open for 21% of the time, Pallas kernels for 0%

commit v1 on v0

v1 whole, which is shorter than its diff:
```python
import jax
import jax.numpy as jnp
from jax import lax
from jax.experimental import pallas as pl
from jax.experimental.pallas import tpu as pltpu
from jax.sharding import PartitionSpec as P


F32 = jnp.float32
BF16 = jnp.bfloat16
NY, NZ = 32, 256
OWN = 4
EXT = 5 * OWN
LIST = 8
VMEM = pl.BlockSpec(memory_space=pltpu.VMEM)
SMEM = pl.BlockSpec(memory_space=pltpu.SMEM)
NT_DIMS = (((1,), (1,)), ((), ()))
NN_DIMS = (((1,), (0,)), ((), ()))


def call(kernel, outs, n_in, scratch=(), smem=(), name=None, flops=0):
    shapes = [jax.ShapeDtypeStruct(s, F32) for s in outs]
    return pl.pallas_call(
        kernel,
        out_shape=shapes if len(shapes) > 1 else shapes[0],
        in_specs=[SMEM if i in smem else VMEM for i in range(n_in)],
        out_specs=[VMEM] * len(shapes) if len(shapes) > 1 else VMEM,
        scratch_shapes=list(scratch),
        compiler_params=pltpu.CompilerParams(vmem_limit_bytes=56 << 20),
        name=name,
    )


def core_of():
    return lax.rem(lax.axis_index("space"), 2)


def halves(x):
    hi = x.astype(BF16)
    lo = (x - hi.astype(F32)).astype(BF16)
    return hi, lo


def dot(a, b, dims):
    return lax.dot_general(a, b, dims, preferred_element_type=F32)


def one_hots(cells):
    cell = cells.astype(jnp.int32)
    count = cell.shape[1]
    row = lax.shift_right_logical(cell, 8)
    col = lax.bitwise_and(cell, NZ - 1)
    in_row = lax.broadcasted_iota(jnp.int32, (OWN * NY, count), 0) == row
    in_col = lax.broadcasted_iota(jnp.int32, (NZ, count), 0) == col
    return in_row, in_col.astype(F32).astype(BF16)


def make_laplace():
    y = lax.broadcasted_iota(jnp.int32, (NY, NZ), 0)
    z = lax.broadcasted_iota(jnp.int32, (NY, NZ), 1)
    y_lo, y_hi, z_lo, z_hi = y > 0, y < NY - 1, z > 0, z < NZ - 1

    def laplace(below, f, above):
        total = below + above
        total = total + jnp.where(y_lo, pltpu.roll(f, 1, 0), 0.0)
        total = total + jnp.where(y_hi, pltpu.roll(f, NY - 1, 0), 0.0)
        total = total + jnp.where(z_lo, pltpu.roll(f, 1, 1), 0.0)
        total = total + jnp.where(z_hi, pltpu.roll(f, NZ - 1, 1), 0.0)
        return total - 6.0 * f

    return laplace


def pack_pair(p, courant, src, strength, rec, weight, out):
    other = 2 * (1 - core_of())
    for i in range(2):
        out[64 * i : 64 * (i + 1), :] = p[other + i].reshape(64, NZ)
    out[128:192, :] = courant[...].reshape(64, NZ)
    chip_cell = (lax.axis_index("space") // 2) * (OWN * NY * NZ)
    out[192:200, :] = jnp.zeros((LIST, NZ), F32)
    out[192:193, 64:128] = (src[...] - chip_cell).astype(F32)
    out[193:194, 64:128] = strength[...]
    out[194:195, 64:128] = (rec[...] - chip_cell).astype(F32)
    out[195:196, 64:128] = weight[...]


def pack_chip(p, courant, src, strength, rec, weight, got, own, right, left):
    core = core_of()
    mine = pl.multiple_of(core * 64, 64)
    theirs = pl.multiple_of((1 - core) * 64, 64)
    for i in range(2):
        own[pl.ds(128 * i + mine, 64), :] = p[2 * core + i].reshape(64, NZ)
        own[pl.ds(128 * i + theirs, 64), :] = got[64 * i : 64 * (i + 1), :]
    own[pl.ds(256 + mine, 64), :] = courant[...].reshape(64, NZ)
    own[pl.ds(256 + theirs, 64), :] = got[128:192, :]
    chip_cell = (lax.axis_index("space") // 2) * (OWN * NY * NZ)
    own[384:392, :] = got[192:200, :]
    own[384:385, 0:64] = (src[...] - chip_cell).astype(F32)
    own[385:386, 0:64] = strength[...]
    own[386:387, 0:64] = (rec[...] - chip_cell).astype(F32)
    own[387:388, 0:64] = weight[...]
    for i in range(3):
        left[64 * i : 64 * (i + 1), :] = own[128 * i : 128 * i + 64, :]
        right[64 * i : 64 * (i + 1), :] = own[128 * i + 64 : 128 * i + 128, :]
    left[192:200, :] = own[384:392, :]
    right[192:200, :] = own[384:392, :]


def forward(
    own, l1, r1, l2, r2, wavelet, drives, wrec, courant, cells, src, wave, born, probe, drive
):
    chip = lax.axis_index("space") // 2
    last = lax.axis_size("space") // 2 - 1
    keep = [
        jnp.where(ok, 1.0, 0.0).astype(F32)
        for ok in (chip >= 2, chip >= 1, chip >= 0, chip <= last - 1, chip <= last - 2)
    ]
    slots = (l2, l1, own, r1, r2)
    lists = (192, 384, 384, 384, 192)
    cells[...] = jnp.zeros((LIST, 128), F32)
    for m, (ref, base) in enumerate(zip(slots, lists)):
        listed = ref[base : base + LIST, 0:128]
        in_row, in_col = one_hots(listed[0:1])
        strength = listed[1:2] * keep[m]
        hi, lo = halves(jnp.where(in_row, strength, 0.0))
        field = dot(hi, in_col, NT_DIMS) + dot(lo, in_col, NT_DIMS)
        src[4 * m : 4 * m + 4] = field.reshape(OWN, NY, NZ)
        cells[m : m + 1, :] = listed[2:3]
    for m, ref in ((1, l1), (2, own), (3, r1)):
        for i in range(2):
            probe[i, 4 * m : 4 * m + 4] = ref[128 * i : 128 * (i + 1), :].reshape(OWN, NY, NZ)
        courant[4 * m : 4 * m + 4] = keep[m] * ref[256:384, :].reshape(OWN, NY, NZ)
    for m, at, ref in ((0, 2, l2), (4, 16, r2)):
        for i in range(2):
            probe[i, at : at + 2] = ref[64 * i : 64 * (i + 1), :].reshape(2, NY, NZ)
        courant[at : at + 2] = keep[m] * ref[128:192, :].reshape(2, NY, NZ)
    zero = jnp.zeros((NY, NZ), F32)
    for e in (0, 1, 18, 19):
        courant[e] = zero
    first = wavelet[0]

    def start(e, _):
        wave[1, e] = first * src[e]
        wave[0, e] = zero
        for i in range(2):
            born[0, i, e] = zero
            born[1, i, e] = zero
        return 0

    lax.fori_loop(0, EXT, start, 0)
    laplace = make_laplace()
    listed = own[384:392, 0:128]
    in_row, in_col = one_hots(listed[2:3])
    row_mask = jnp.where(in_row, 1.0, 0.0)
    weight = listed[3:4]
    wrec[...] = jnp.zeros((16, 128), F32)
    for t in range(1, 8):
        now, nxt = t % 2, (t + 1) % 2
        pulse = wavelet[t]

        def advance(e, _, now=now, nxt=nxt, pulse=pulse, t=t):
            c = courant[e]
            w = wave[now, e]
            d = c * laplace(wave[now, e - 1], w, wave[now, e + 1])
            drive[e] = d
            if t < 7:
                wave[nxt, e] = 2.0 * w - wave[nxt, e] + d + pulse * src[e]
            for i in range(2):
                force = probe[i, e] * d
                if t > 1:
                    b = born[now, i, e]
                    bent = laplace(born[now, i, e - 1], b, born[now, i, e + 1])
                    force = force + (2.0 * b - born[nxt, i, e] + c * bent)
                born[nxt, i, e] = force
            return 0

        lax.fori_loop(1 + t, 19 - t, advance, 0)
        drives[t - 1] = drive[8:12]
        for i in range(2):
            hi, lo = halves(born[nxt, i, 8:12].reshape(OWN * NY, NZ))
            picked = dot(hi, in_col, NN_DIMS) + dot(lo, in_col, NN_DIMS)
            value = jnp.sum(picked * row_mask, axis=0, keepdims=True)
            at = 2 * (t - 1) + i
            wrec[at : at + 1, :] = value * weight


def adjoint(courant, cells, w2l, w1l, w0, w1r, w2r, drives, mine, send, inj, adj, bent, hess):
    recs = (w2l, w1l, w0, w1r, w2r)
    for m, ref in enumerate(recs):
        in_row, in_col = one_hots(cells[m : m + 1, :])
        for k in range(8, 1, -1):
            lo_e, hi_e = 10 - k, 9 + k
            if 4 * m + 3 < lo_e or 4 * m > hi_e:
                continue
            for i in range(2):
                at = 2 * (k - 2) + i
                hi, lo = halves(ref[at : at + 1, :])
                a = jnp.where(in_row, hi.astype(F32), 0.0).astype(BF16)
                b = jnp.where(in_row, lo.astype(F32), 0.0).astype(BF16)
                field = dot(a, in_col, NT_DIMS) + dot(b, in_col, NT_DIMS)
                inj[k - 2, i, 4 * m : 4 * m + 4] = field.reshape(OWN, NY, NZ)
    laplace = make_laplace()

    def begin(e, _):
        for i in range(2):
            a = inj[6, i, e]
            adj[0, i, e] = a
            bent[0, i, e] = courant[e] * a
        return 0

    lax.fori_loop(2, 18, begin, 0)
    for i in range(2):
        for e in range(OWN):
            hess[i, e] = drives[6, e] * adj[0, i, 8 + e]
    for k in range(7, 1, -1):
        now, nxt = k % 2, (k + 1) % 2

        def advance(e, _, k=k, now=now, nxt=nxt):
            for i in range(2):
                a = 2.0 * adj[nxt, i, e] + inj[k - 2, i, e]
                a = a + laplace(bent[nxt, i, e - 1], bent[nxt, i, e], bent[nxt, i, e + 1])
                if k < 7:
                    a = a - adj[now, i, e]
                adj[now, i, e] = a
                if k > 2:
                    bent[now, i, e] = courant[e] * a
            return 0

        lax.fori_loop(10 - k, 10 + k, advance, 0)
        for i in range(2):
            for e in range(OWN):
                hess[i, e] = hess[i, e] + drives[k - 2, e] * adj[now, i, 8 + e]
    core = core_of()
    for i in range(2):
        for e in range(2):
            mine[i, e] = hess[i, 2 * core + e]
            send[i, e] = hess[i, 2 * (1 - core) + e]


def finish(p, prior, mine, got, out):
    core = core_of()
    for i in range(2):
        out[2 * core + i] = prior[...] * p[2 * core + i] + mine[i]
        out[2 * (1 - core) + i] = prior[...] * p[2 * (1 - core) + i] + got[i]


def gram_part(h0, h1, h2, h3, out, sums):
    group = lax.axis_index("probe")
    blocks = (h0, h1, h2, h3)
    start = [lax.rem(group + 4 - b, 4) * 4 for b in range(4)]
    for a in range(4):
        for b in range(a, 4):
            pairs = [(i, j) for i in range(4) for j in range(4) if a != b or i <= j]
            acc = [None] * len(pairs)
            for plane in range(2):
                for y in range(0, NY, 8):
                    left = [blocks[a][i, plane, y : y + 8, :] for i in range(4)]
                    right = [blocks[b][j, plane, y : y + 8, :] for j in range(4)] if a != b else left
                    for n, (i, j) in enumerate(pairs):
                        prod = left[i] * right[j]
                        prod = prod[:, :128] + prod[:, 128:]
                        acc[n] = prod if acc[n] is None else acc[n] + prod
            for n, (i, j) in enumerate(pairs):
                total = jnp.sum(acc[n], axis=0, keepdims=True)
                row, col = start[a] + i, start[b] + j
                sums[pl.ds(row * 16 + col, 1), :] = total
                sums[pl.ds(col * 16 + row, 1), :] = total
    flat = lax.dot_general(
        jnp.ones((8, 128), F32),
        sums[...],
        NT_DIMS,
        precision=lax.Precision.HIGHEST,
        preferred_element_type=F32,
    )
    pair = jnp.concatenate([flat[0:1, :128], flat[0:1, 128:]], axis=0)
    out[...] = jnp.broadcast_to(pair[None], out.shape)


def whiten(scale, parts, h0, h1, h2, h3, out, work):
    exact = dict(precision=lax.Precision.HIGHEST, preferred_element_type=F32)
    group = lax.axis_index("probe")
    total = jnp.sum(parts[...], axis=0) * scale
    row = lax.broadcasted_iota(jnp.int32, (16, 128), 0)
    lane = lax.broadcasted_iota(jnp.int32, (16, 128), 1)
    spread = jnp.where(
        row < 8,
        jnp.broadcast_to(total[0:1], (16, 128)),
        jnp.broadcast_to(total[1:2], (16, 128)),
    )
    spread = jnp.where(lax.shift_right_logical(lane, 4) == lax.bitwise_and(row, 7), spread, 0.0)
    from_lane = lax.broadcasted_iota(jnp.int32, (128, 128), 0)
    to_lane = lax.broadcasted_iota(jnp.int32, (128, 128), 1)
    select = jnp.where(lax.bitwise_and(from_lane, 15) == to_lane, 1.0, 0.0)
    x = lax.dot_general(spread, select, NN_DIMS, **exact)
    x = x + jnp.where(lane == row + 16, 1.0, 0.0)
    for k in range(16):
        column = jnp.broadcast_to(x[:, k : k + 1], (16, 128))
        pivot = jnp.broadcast_to(column[k : k + 1], (16, 128))
        ratio = jnp.broadcast_to(x[k : k + 1], (16, 128)) / pivot
        x = jnp.where(row > k, x - column * ratio, x)
        x = jnp.where(row == k, x * lax.rsqrt(pivot), x)
    work[...] = x
    rows = work[pl.ds(pl.multiple_of(group * 4, 4), 4), :]
    rows = jnp.concatenate([rows, rows], axis=0)
    block = lax.bitwise_and(group + 4 - lax.shift_right_logical(to_lane, 2), 3)
    source = 16 + block * 4 + lax.bitwise_and(to_lane, 3)
    order = jnp.where(jnp.logical_and(from_lane == source, to_lane < 16), 1.0, 0.0)
    coef = lax.dot_general(rows, order, NN_DIMS, **exact)
    blocks = (h0, h1, h2, h3)
    for r in range(4):
        c = [jnp.broadcast_to(coef[r : r + 1, s : s + 1], (8, NZ)) for s in range(16)]
        for plane in range(2):
            for y in range(0, NY, 8):
                acc = None
                for s in range(16):
                    term = c[s] * blocks[s // 4][s % 4, plane, y : y + 8, :]
                    acc = term if acc is None else acc + term
                out[r, plane, y : y + 8, :] = acc


def shards(
    courant_field,
    probe_fields,
    prior_weight,
    source_cells,
    source_strength,
    wavelet,
    receiver_cells,
    receiver_weight,
):
    count = lax.axis_size("space")
    lists = [
        v.reshape(1, -1) for v in (source_cells, source_strength, receiver_cells, receiver_weight)
    ]

    def swap(x):
        return lax.ppermute(x, "space", [(i, i ^ 1) for i in range(count)])

    def shift(x, by):
        return lax.ppermute(x, "space", [(i, (i + by) % count) for i in range(count)])

    pair = call(pack_pair, [(200, NZ)], 6, name="pack_pair")(probe_fields, courant_field, *lists)
    got = swap(pair)
    own, right, left = call(
        pack_chip, [(392, NZ), (200, NZ), (200, NZ)], 7, name="pack_chip"
    )(probe_fields, courant_field, *lists, got)
    l1, r1 = shift(own, 2), shift(own, -2)
    l2, r2 = shift(right, 4), shift(left, -4)
    plane = (NY, NZ)
    drives, wrec, courant, cells = call(
        forward,
        [(7, OWN) + plane, (16, 128), (EXT,) + plane, (LIST, 128)],
        6,
        scratch=[
            pltpu.VMEM((EXT,) + plane, F32),
            pltpu.VMEM((2, EXT) + plane, F32),
            pltpu.VMEM((2, 2, EXT) + plane, F32),
            pltpu.VMEM((2, EXT) + plane, F32),
            pltpu.VMEM((EXT,) + plane, F32),
        ],
        smem=(5,),
        name="forward",
    )(own, l1, r1, l2, r2, wavelet)
    w1l, w1r, w2l, w2r = shift(wrec, 2), shift(wrec, -2), shift(wrec, 4), shift(wrec, -4)
    half = (2, 2) + plane
    mine, send = call(
        adjoint,
        [half, half],
        8,
        scratch=[
            pltpu.VMEM((7, 2, EXT) + plane, F32),
            pltpu.VMEM((2, 2, EXT) + plane, F32),
            pltpu.VMEM((2, 2, EXT) + plane, F32),
            pltpu.VMEM((2, OWN) + plane, F32),
        ],
        name="adjoint",
    )(courant, cells, w2l, w1l, wrec, w1r, w2r, drives)
    hessian = call(finish, [(4, 2) + plane], 4, name="finish")(
        probe_fields, prior_weight, mine, swap(send)
    )
    groups = lax.axis_size("probe")
    others = [
        lax.ppermute(hessian, "probe", [(i, (i + b) % groups) for i in range(groups)])
        for b in (1, 2, 3)
    ]
    part = call(
        gram_part, [(count, 2, 128)], 4, scratch=[pltpu.VMEM((256, 128), F32)], name="gram"
    )(hessian, *others)
    parts = lax.all_to_all(part, "space", 0, 0, tiled=True)
    scale = 1.0 / (count * hessian[0].size)

    def whiten_scaled(*refs):
        whiten(scale, *refs)

    basis = call(
        whiten_scaled, [(4, 2) + plane], 5, scratch=[pltpu.VMEM((16, 128), F32)], name="whiten"
    )(parts, hessian, *others)
    return (hessian, basis)


def solution(mesh):
    in_specs = (
        P("space", None, None),
        P("probe", "space", None, None),
        P("space", None, None),
        P("space"),
        P("space"),
        P(),
        P("space"),
        P("space"),
    )
    out_specs = (P("probe", "space", None, None), P("probe", "space", None, None))
    return jax.shard_map(shards, mesh=mesh, in_specs=in_specs, out_specs=out_specs, check_vma=False)
```

time: 438 us -> 123 us (0.28)
  blocking collectives: 129 us -> 15.2 us
  local copies, waits for them, and re-layouts: 79.3 us -> 4.28 us
  other arithmetic: 65.7 us -> 0 us
  waiting for transfers between devices: 78 us -> 35.1 us
  Pallas kernels: 0 us -> 36.9 us
  starting transfers between devices: 66.1 us -> 30.2 us
  between operations: 15 us -> 0.68 us
    psum x1 -> x0, blocking collectives: 129 us -> none  [shards(): gram = lax.psum(inner_rows(rows), 'space') / total_cells]
    all_gather x1 -> x0, waiting for transfers between devices: 41.3 us -> none  [shards(): rows = lax.all_gather(flat, 'probe', axis=0, tiled=True)]
    scatter-add x8 -> x0, other arithmetic: 39.8 us -> none  [the longest x7 38.7 us: inject(): return flat.at[:, local_cells].add(values).reshape(field_shape)]
    slice x25 -> x0, local copies, waits for them, and re-layouts: 37.1 us -> none  [the longest x11 33.2 us: shards(): state_next[1:].reshape(groups, cells)]
    pallas_call x0 -> x7, Pallas kernels: none -> 36.9 us  [the longest x1 13.6 us: shards(): call(forward, [(7, OWN) + plane, (16, 128), (EXT,) + plane, (LIST, 128)],...]
    reshape x7 -> x0, local copies, waits for them, and re-layouts: 36.7 us -> none  [inject(): return flat.at[:, local_cells].add(values).reshape(field_shape)]
    ppermute x26 -> x13, starting transfers between devices: 66.1 us -> 30.2 us  [the longest x8 20.2 us: shift(): lax.ppermute(x, 'space', [(i, (i + by) % count) for i in range(count)])]
    all_to_all x0 -> x1, blocking collectives: none -> 15.2 us  [shards(): parts = lax.all_to_all(part, 'space', 0, 0, tiled=True)]
  transfers between devices with their start and end apart: 27 -> 13, of which waited for: 9 -> 8; matrix products, arithmetic and copies ran while one was open for 21% -> 0% of each run, Pallas kernels for 0% -> 0%
where the time goes in v1:
time: 123 us; the launch traced here: 122 us
  Pallas kernels  36.9 us (30%)
  waiting for transfers between devices  35.1 us (29%)
  starting transfers between devices  30.2 us (25%)
  blocking collectives  15.2 us (12%)
  local copies, waits for them, and re-layouts  4.28 us (3%)
    ppermute x8, starting transfers between devices, shift(): lax.ppermute(x, 'space', [(i, (i + by) % count) for i in range(count)])  20.2 us
    ppermute x8, waiting for transfers between devices, shift(): lax.ppermute(x, 'space', [(i, (i + by) % count) for i in range(count)])  18.1 us
    all_to_all x1, blocking collectives, shards(): parts = lax.all_to_all(part, 'space', 0, 0, tiled=True)  15.2 us
    ppermute x3, waiting for transfers between devices, shards(): lax.ppermute(hessian, 'probe', [(i, (i + b) % groups) for i in range(grou...  14.4 us
    pallas_call x1, Pallas kernels, shards(): call(forward, [(7, OWN) + plane, (16, 128), (EXT,) + plane, (LIST, 128)],...  13.6 us
    pallas_call x1, Pallas kernels, shards(): call(adjoint, [half, half], 8, scratch=[pltpu.VMEM((7, 2, EXT) + plane, F...  10.4 us
    ppermute x2, starting transfers between devices, swap(): return lax.ppermute(x, 'space', [(i, i ^ 1) for i in range(count)])  6.42 us
    pallas_call x1, Pallas kernels, shards(): call(whiten_scaled, [(4, 2) + plane], 5, scratch=[pltpu.VMEM((16, 128), F...  4.56 us
  transfers between devices with their start and end apart: 13, of which 8 were waited for; matrix products, arithmetic and copies ran while one was open for 0% of the time, Pallas kernels for 0%

profile of v1, /device:TPU:1, one launch (start us, length us, event | category | flops | bytes accessed | tf_op | source)
XLA Modules:
  0.0 122.4 jit_solution(14622235683322728338)
XLA Ops:
  0.6 1.8 %pack_pair.1 = f32[200,256]{1,0:T(8,128)} custom-call(f32[4,2,32,256]{3,2,1,0:T(8,128)} %p.5, f32[2,32,256]{2,1,0:T(8,128)} %courant.3, s32[1,64]{1,0:T(1,128)} %bitcast.4, f32[1,64]{1,0:T(1,128)} %bitcast.6, s32[1,64]{1,0:T(1,128)} %bitcast.8, f32[1,64]{1,0:T(1,128)} %bitcast.10), custom_call_target="tpu_custom_call" | custom-call | tf_op jit(solution)/shard_map/pack_pair/pallas_call | solution.py:342
  2.4 3.2 %collective-permute-start = (f32[200,256]{1,0:T(8,128)}, f32[200,256]{1,0:T(8,128)S(1)}, u32[]{:S(2)}, u32[]{:S(2)}) collective-permute-start(f32[200,256]{1,0:T(8,128)} %pack_pair.1), channel_id=1, source_target_pairs={{0,1},{1,0},{2,3},{3,2},{4,5},{5,4},{6,7},{7,6},{8,9},{9,8},{10,11... | collective-permute-start | bytes 614408 | tf_op jit(solution)/shard_map/ppermute | solution.py:337
  5.6 1.3 %collective-permute-done.got = f32[200,256]{1,0:T(8,128)S(1)} collective-permute-done((f32[200,256]{1,0:T(8,128)}, f32[200,256]{1,0:T(8,128)S(1)}, u32[]{:S(2)}, u32[]{:S(2)}) %collective-permute-start) | collective-permute-done | bytes 204832 | tf_op jit(solution)/shard_map/ppermute | solution.py:337
  6.9 0.7 copy-done.5
  7.6 2.0 %pack_chip.1 = (f32[392,256]{1,0:T(8,128)}, f32[200,256]{1,0:T(8,128)}, f32[200,256]{1,0:T(8,128)}) custom-call(f32[4,2,32,256]{3,2,1,0:T(8,128)} %p.5, f32[2,32,256]{2,1,0:T(8,128)} %courant.3, s32[1,64]{1,0:T(1,128)} %bitcast.5, f32[1,64]{1,0:T(1,128)} %bitcast.7, s32[1,64]{1,0:T(1,128)} %bitcast.9, f32[1,64]{1,0:T(1,128)} %bitcast.11, f32[200,256]{1,0:T(8,128)} %copy-done.5), custom_call_target="tpu_custom_call" | custom-call | tf_op jit(solution)/shard_map/pack_chip/pallas_call | solution.py:344
  9.6 6.3 %collective-permute-start.2 = (f32[392,256]{1,0:T(8,128)}, f32[392,256]{1,0:T(8,128)S(1)}, u32[]{:S(2)}, u32[]{:S(2)}) collective-permute-start(f32[392,256]{1,0:T(8,128)} %get-tuple-element.11.own), channel_id=1, source_target_pairs={{0,62},{1,63},{2,0},{3,1},{4,2},{5,3},{6,4},{7,5},{8,6},{9,7},{10,... | collective-permute-start | bytes 1204232 | tf_op jit(solution)/shard_map/ppermute | solution.py:340
  16.0 5.7 %collective-permute-start.4 = (f32[200,256]{1,0:T(8,128)}, f32[200,256]{1,0:T(8,128)S(1)}, u32[]{:S(2)}, u32[]{:S(2)}) collective-permute-start(f32[200,256]{1,0:T(8,128)} %get-tuple-element.13), channel_id=1, source_target_pairs={{0,60},{1,61},{2,62},{3,63},{4,0},{5,1},{6,2},{7,3},{8,4},{9,5},{1... | collective-permute-start | bytes 614408 | tf_op jit(solution)/shard_map/ppermute | solution.py:340
  21.6 12.2 %collective-permute-done.3.l2 = f32[200,256]{1,0:T(8,128)S(1)} collective-permute-done((f32[200,256]{1,0:T(8,128)}, f32[200,256]{1,0:T(8,128)S(1)}, u32[]{:S(2)}, u32[]{:S(2)}) %collective-permute-start.3) | collective-permute-done | bytes 204832 | tf_op jit(solution)/shard_map/ppermute | solution.py:340
  33.9 0.6 copy-done.6
  34.7 0.7 copy-done.4
  35.5 13.6 %forward.1 = (f32[7,4,32,256]{3,2,1,0:T(8,128)}, f32[16,128]{1,0:T(8,128)}, f32[20,32,256]{2,1,0:T(8,128)}, f32[8,128]{1,0:T(8,128)}) custom-call(f32[392,256]{1,0:T(8,128)} %get-tuple-element.11.own, f32[392,256]{1,0:T(8,128)} %copy-done.4, f32[392,256]{1,0:T(8,128)} %copy-done.3, f32[200,256]{1,0:T(8,128)} %copy-done.6, f32[200,256]{1,0:T(8,128)} %copy-done.7, ...), custom_call_target="tpu_custom_call" | custom-call | tf_op jit(solution)/shard_map/forward/pallas_call | solution.py:350
  49.1 5.7 %collective-permute-start.8 = (f32[16,128]{1,0:T(8,128)}, f32[16,128]{1,0:T(8,128)S(1)}, u32[]{:S(2)}, u32[]{:S(2)}) collective-permute-start(f32[16,128]{1,0:T(8,128)} %get-tuple-element.16.w0), channel_id=1, source_target_pairs={{0,60},{1,61},{2,62},{3,63},{4,0},{5,1},{6,2},{7,3},{8,4},{9,5},{1... | collective-permute-start | bytes 24584 | tf_op jit(solution)/shard_map/ppermute | solution.py:340
  54.8 1.5 %collective-permute-start.6 = (f32[16,128]{1,0:T(8,128)}, f32[16,128]{1,0:T(8,128)S(1)}, u32[]{:S(2)}, u32[]{:S(2)}) collective-permute-start(f32[16,128]{1,0:T(8,128)} %get-tuple-element.16.w0), channel_id=1, source_target_pairs={{0,2},{1,3},{2,4},{3,5},{4,6},{5,7},{6,8},{7,9},{8,10},{9,11},{10,... | collective-permute-start | bytes 24584 | tf_op jit(solution)/shard_map/ppermute | solution.py:340
  56.3 1.0 collective-permute-start.5
  57.2 0.3 collective-permute-done.7.w1r
  57.5 3.3 %collective-permute-done.6.w1l = f32[16,128]{1,0:T(8,128)S(1)} collective-permute-done((f32[16,128]{1,0:T(8,128)}, f32[16,128]{1,0:T(8,128)S(1)}, u32[]{:S(2)}, u32[]{:S(2)}) %collective-permute-start.6) | collective-permute-done | bytes 8224 | tf_op jit(solution)/shard_map/ppermute | solution.py:340
  60.8 2.4 %collective-permute-done.5.w2l = f32[16,128]{1,0:T(8,128)S(1)} collective-permute-done((f32[16,128]{1,0:T(8,128)}, f32[16,128]{1,0:T(8,128)S(1)}, u32[]{:S(2)}, u32[]{:S(2)}) %collective-permute-start.5) | collective-permute-done | bytes 8224 | tf_op jit(solution)/shard_map/ppermute | solution.py:340
  63.2 0.6 copy-done.12
  63.8 10.4 %adjoint.1 = (f32[2,2,32,256]{3,2,1,0:T(8,128)}, f32[2,2,32,256]{3,2,1,0:T(8,128)}) custom-call(f32[20,32,256]{2,1,0:T(8,128)} %get-tuple-element.14.courant, f32[8,128]{1,0:T(8,128)} %get-tuple-element.15.cells, f32[16,128]{1,0:T(8,128)} %copy-done.12, f32[16,128]{1,0:T(8,128)} %copy-done.11, f32[16,128]{1,0:T(8,128)} %get-tuple-element.16.w0, ...), custom_call_target="tpu_custom_call" | custom-call | tf_op jit(solution)/shard_map/adjoint/pallas_call | solution.py:366
  74.2 3.2 %collective-permute-start.9 = (f32[2,2,32,256]{3,2,1,0:T(8,128)}, f32[2,2,32,256]{3,2,1,0:T(8,128)S(1)}, u32[]{:S(2)}, u32[]{:S(2)}) collective-permute-start(f32[2,2,32,256]{3,2,1,0:T(8,128)} %get-tuple-element.19), channel_id=1, source_target_pairs={{0,1},{1,0},{2,3},{3,2},{4,5},{5,4},{6,7},{7,6},{8,9},{9,8},{10,11... | collective-permute-start | bytes 393224 | tf_op jit(solution)/shard_map/ppermute | solution.py:337
  77.5 1.2 collective-permute-done.9.got
  78.7 0.7 copy-done.8
  79.3 1.8 %finish.1.h0.refs_1_ = f32[4,2,32,256]{3,2,1,0:T(8,128)} custom-call(f32[4,2,32,256]{3,2,1,0:T(8,128)} %p.5, f32[2,32,256]{2,1,0:T(8,128)} %prior.1, f32[2,2,32,256]{3,2,1,0:T(8,128)} %get-tuple-element.18.mine, f32[2,2,32,256]{3,2,1,0:T(8,128)} %copy-done.8), custom_call_target="tpu_custom_call" | custom-call | tf_op jit(solution)/shard_map/finish/pallas_call | solution.py:378
  81.1 2.5 %collective-permute-start.12 = (f32[4,2,32,256]{3,2,1,0:T(8,128)}, f32[4,2,32,256]{3,2,1,0:T(8,128)S(1)}, u32[]{:S(2)}, u32[]{:S(2)}) collective-permute-start(f32[4,2,32,256]{3,2,1,0:T(8,128)} %finish.1.h0.refs_1_), channel_id=1, source_target_pairs={{0,192},{64,0},{128,64},{192,128},{1,193},{65,1},{129,65},{193,129... | collective-permute-start | bytes 786440 | tf_op jit(solution)/shard_map/ppermute | solution.py:383
  83.6 0.5 collective-permute-start.11
  84.1 0.6 collective-permute-start.10
  84.8 10.0 %collective-permute-done.12.h3.refs_4_ = f32[4,2,32,256]{3,2,1,0:T(8,128)S(1)} collective-permute-done((f32[4,2,32,256]{3,2,1,0:T(8,128)}, f32[4,2,32,256]{3,2,1,0:T(8,128)S(1)}, u32[]{:S(2)}, u32[]{:S(2)}) %collective-permute-start.12) | collective-permute-done | bytes 262176 | tf_op jit(solution)/shard_map/ppermute | solution.py:383
  94.7 4.5 %collective-permute-done.10.h1.refs_2_ = f32[4,2,32,256]{3,2,1,0:T(8,128)S(1)} collective-permute-done((f32[4,2,32,256]{3,2,1,0:T(8,128)}, f32[4,2,32,256]{3,2,1,0:T(8,128)S(1)}, u32[]{:S(2)}, u32[]{:S(2)}) %collective-permute-start.10) | collective-permute-done | bytes 262176 | tf_op jit(solution)/shard_map/ppermute | solution.py:383
  99.2 0.7 copy-done.2
  99.9 2.7 %gram.1 = f32[64,2,128]{2,1,0:T(2,128)} custom-call(f32[4,2,32,256]{3,2,1,0:T(8,128)} %finish.1.h0.refs_1_, f32[4,2,32,256]{3,2,1,0:T(8,128)} %copy-done.2, f32[4,2,32,256]{3,2,1,0:T(8,128)} %copy-done.1, f32[4,2,32,256]{3,2,1,0:T(8,128)} %copy-done), custom_call_target="tpu_custom_call" | custom-call | tf_op jit(solution)/shard_map/gram/pallas_call | solution.py:386
  102.6 15.2 %all_to_all.5.refs_0_ = f32[64,2,128]{2,1,0:T(2,128)} all-to-all(f32[64,2,128]{2,1,0:T(2,128)} %gram.1), channel_id=1, replica_groups=mesh['probe'=4,'space'=64] {'space'}, dimensions={0} | all-to-all | bytes 131072 | tf_op jit(solution)/shard_map/all_to_all | solution.py:389
  117.8 4.6 %whiten.1 = f32[4,2,32,256]{3,2,1,0:T(8,128)} custom-call(f32[64,2,128]{2,1,0:T(2,128)} %all_to_all.5.refs_0_, f32[4,2,32,256]{3,2,1,0:T(8,128)} %finish.1.h0.refs_1_, f32[4,2,32,256]{3,2,1,0:T(8,128)} %copy-done.2, f32[4,2,32,256]{3,2,1,0:T(8,128)} %copy-done.1, f32[4,2,32,256]{3,2,1,0:T(8,128)} %copy-done), custom_call_target="tpu_custom_call" | custom-call | tf_op jit(solution)/shard_map/whiten/pallas_call | solution.py:395
  (28 shorter events, 0.3 us)
Async XLA Ops:
  2.4 4.5 %collective-permute-start = (f32[200,256]{1,0:T(8,128)}, f32[200,256]{1,0:T(8,128)S(1)}, u32[]{:S(2)}, u32[]{:S(2)}) collective-permute-start(f32[200,256]{1,0:T(8,128)} %pack_pair.1), channel_id=1, source_target_pairs={{0,1},{1,0},{2,3},{3,2},{4,5},{5,4},{6,7},{7,6},{8,9},{9,8},{10,11... | collective-permute-start | bytes 614408 | tf_op jit(solution)/shard_map/ppermute | solution.py:337
  6.9 0.7 copy-start.5
  9.6 24.2 %collective-permute-start.2 = (f32[392,256]{1,0:T(8,128)}, f32[392,256]{1,0:T(8,128)S(1)}, u32[]{:S(2)}, u32[]{:S(2)}) collective-permute-start(f32[392,256]{1,0:T(8,128)} %get-tuple-element.11.own), channel_id=1, source_target_pairs={{0,62},{1,63},{2,0},{3,1},{4,2},{5,3},{6,4},{7,5},{8,6},{9,7},{10,... | collective-permute-start | bytes 1204232 | tf_op jit(solution)/shard_map/ppermute | solution.py:340
  15.9 17.9 %collective-permute-start.1 = (f32[392,256]{1,0:T(8,128)}, f32[392,256]{1,0:T(8,128)S(1)}, u32[]{:S(2)}, u32[]{:S(2)}) collective-permute-start(f32[392,256]{1,0:T(8,128)} %get-tuple-element.11.own), channel_id=1, source_target_pairs={{0,2},{1,3},{2,4},{3,5},{4,6},{5,7},{6,8},{7,9},{8,10},{9,11},{10,... | collective-permute-start | bytes 1204232 | tf_op jit(solution)/shard_map/ppermute | solution.py:340
  16.0 17.9 %collective-permute-start.3 = (f32[200,256]{1,0:T(8,128)}, f32[200,256]{1,0:T(8,128)S(1)}, u32[]{:S(2)}, u32[]{:S(2)}) collective-permute-start(f32[200,256]{1,0:T(8,128)} %get-tuple-element.12), channel_id=1, source_target_pairs={{0,4},{1,5},{2,6},{3,7},{4,8},{5,9},{6,10},{7,11},{8,12},{9,13},{1... | collective-permute-start | bytes 614408 | tf_op jit(solution)/shard_map/ppermute | solution.py:340
  16.0 17.9 %collective-permute-start.4 = (f32[200,256]{1,0:T(8,128)}, f32[200,256]{1,0:T(8,128)S(1)}, u32[]{:S(2)}, u32[]{:S(2)}) collective-permute-start(f32[200,256]{1,0:T(8,128)} %get-tuple-element.13), channel_id=1, source_target_pairs={{0,60},{1,61},{2,62},{3,63},{4,0},{5,1},{6,2},{7,3},{8,4},{9,5},{1... | collective-permute-start | bytes 614408 | tf_op jit(solution)/shard_map/ppermute | solution.py:340
  33.8 0.7 copy-start.6
  33.8 0.7 copy-start.7
  33.8 0.9 copy-start.3
  34.7 0.7 copy-start.4
  49.1 8.2 %collective-permute-start.8 = (f32[16,128]{1,0:T(8,128)}, f32[16,128]{1,0:T(8,128)S(1)}, u32[]{:S(2)}, u32[]{:S(2)}) collective-permute-start(f32[16,128]{1,0:T(8,128)} %get-tuple-element.16.w0), channel_id=1, source_target_pairs={{0,60},{1,61},{2,62},{3,63},{4,0},{5,1},{6,2},{7,3},{8,4},{9,5},{1... | collective-permute-start | bytes 24584 | tf_op jit(solution)/shard_map/ppermute | solution.py:340
  54.8 2.7 %collective-permute-start.7 = (f32[16,128]{1,0:T(8,128)}, f32[16,128]{1,0:T(8,128)S(1)}, u32[]{:S(2)}, u32[]{:S(2)}) collective-permute-start(f32[16,128]{1,0:T(8,128)} %get-tuple-element.16.w0), channel_id=1, source_target_pairs={{0,62},{1,63},{2,0},{3,1},{4,2},{5,3},{6,4},{7,5},{8,6},{9,7},{10,... | collective-permute-start | bytes 24584 | tf_op jit(solution)/shard_map/ppermute | solution.py:340
  54.8 6.0 %collective-permute-start.6 = (f32[16,128]{1,0:T(8,128)}, f32[16,128]{1,0:T(8,128)S(1)}, u32[]{:S(2)}, u32[]{:S(2)}) collective-permute-start(f32[16,128]{1,0:T(8,128)} %get-tuple-element.16.w0), channel_id=1, source_target_pairs={{0,2},{1,3},{2,4},{3,5},{4,6},{5,7},{6,8},{7,9},{8,10},{9,11},{10,... | collective-permute-start | bytes 24584 | tf_op jit(solution)/shard_map/ppermute | solution.py:340
  56.3 6.9 %collective-permute-start.5 = (f32[16,128]{1,0:T(8,128)}, f32[16,128]{1,0:T(8,128)S(1)}, u32[]{:S(2)}, u32[]{:S(2)}) collective-permute-start(f32[16,128]{1,0:T(8,128)} %get-tuple-element.16.w0), channel_id=1, source_target_pairs={{0,4},{1,5},{2,6},{3,7},{4,8},{5,9},{6,10},{7,11},{8,12},{9,13},{1... | collective-permute-start | bytes 24584 | tf_op jit(solution)/shard_map/ppermute | solution.py:340
  57.2 6.0 %copy-start.9 = (f32[16,128]{1,0:T(8,128)}, f32[16,128]{1,0:T(8,128)S(1)}, u32[]{:S(2)}) copy-start(f32[16,128]{1,0:T(8,128)S(1)} %collective-permute-done.8.w2r) | copy-start | bytes 24580
  57.5 5.7 %copy-start.10 = (f32[16,128]{1,0:T(8,128)}, f32[16,128]{1,0:T(8,128)S(1)}, u32[]{:S(2)}) copy-start(f32[16,128]{1,0:T(8,128)S(1)} %collective-permute-done.7.w1r) | copy-start | bytes 24580
  60.8 2.4 %copy-start.11 = (f32[16,128]{1,0:T(8,128)}, f32[16,128]{1,0:T(8,128)S(1)}, u32[]{:S(2)}) copy-start(f32[16,128]{1,0:T(8,128)S(1)} %collective-permute-done.6.w1l) | copy-start | bytes 24580
  63.2 0.6 copy-start.12
  74.2 4.4 %collective-permute-start.9 = (f32[2,2,32,256]{3,2,1,0:T(8,128)}, f32[2,2,32,256]{3,2,1,0:T(8,128)S(1)}, u32[]{:S(2)}, u32[]{:S(2)}) collective-permute-start(f32[2,2,32,256]{3,2,1,0:T(8,128)} %get-tuple-element.19), channel_id=1, source_target_pairs={{0,1},{1,0},{2,3},{3,2},{4,5},{5,4},{6,7},{7,6},{8,9},{9,8},{10,11... | collective-permute-start | bytes 393224 | tf_op jit(solution)/shard_map/ppermute | solution.py:337
  78.7 0.7 copy-start.8
  81.1 13.6 %collective-permute-start.12 = (f32[4,2,32,256]{3,2,1,0:T(8,128)}, f32[4,2,32,256]{3,2,1,0:T(8,128)S(1)}, u32[]{:S(2)}, u32[]{:S(2)}) collective-permute-start(f32[4,2,32,256]{3,2,1,0:T(8,128)} %finish.1.h0.refs_1_), channel_id=1, source_target_pairs={{0,192},{64,0},{128,64},{192,128},{1,193},{65,1},{129,65},{193,129... | collective-permute-start | bytes 786440 | tf_op jit(solution)/shard_map/ppermute | solution.py:383
  83.6 11.1 %collective-permute-start.11 = (f32[4,2,32,256]{3,2,1,0:T(8,128)}, f32[4,2,32,256]{3,2,1,0:T(8,128)S(1)}, u32[]{:S(2)}, u32[]{:S(2)}) collective-permute-start(f32[4,2,32,256]{3,2,1,0:T(8,128)} %finish.1.h0.refs_1_), channel_id=1, source_target_pairs={{0,128},{64,192},{128,0},{192,64},{1,129},{65,193},{129,1},{193,65... | collective-permute-start | bytes 786440 | tf_op jit(solution)/shard_map/ppermute | solution.py:383
  84.1 15.0 %collective-permute-start.10 = (f32[4,2,32,256]{3,2,1,0:T(8,128)}, f32[4,2,32,256]{3,2,1,0:T(8,128)S(1)}, u32[]{:S(2)}, u32[]{:S(2)}) collective-permute-start(f32[4,2,32,256]{3,2,1,0:T(8,128)} %finish.1.h0.refs_1_), channel_id=1, source_target_pairs={{0,64},{64,128},{128,192},{192,0},{1,65},{65,129},{129,193},{193,1... | collective-permute-start | bytes 786440 | tf_op jit(solution)/shard_map/ppermute | solution.py:383
  94.7 4.5 %copy-start = (f32[4,2,32,256]{3,2,1,0:T(8,128)}, f32[4,2,32,256]{3,2,1,0:T(8,128)S(1)}, u32[]{:S(2)}) copy-start(f32[4,2,32,256]{3,2,1,0:T(8,128)S(1)} %collective-permute-done.12.h3.refs_4_) | copy-start | bytes 786436
  94.7 4.5 %copy-start.1 = (f32[4,2,32,256]{3,2,1,0:T(8,128)}, f32[4,2,32,256]{3,2,1,0:T(8,128)S(1)}, u32[]{:S(2)}) copy-start(f32[4,2,32,256]{3,2,1,0:T(8,128)S(1)} %collective-permute-done.11.h2.refs_3_) | copy-start | bytes 786436
  99.2 0.7 copy-start.2

commit v2 on v1

--- a/solution.py
+++ b/solution.py
@@ -12,13 +12,14 @@
 OWN = 4
 EXT = 5 * OWN
 LIST = 8
+UNROLL = True
 VMEM = pl.BlockSpec(memory_space=pltpu.VMEM)
 SMEM = pl.BlockSpec(memory_space=pltpu.SMEM)
 NT_DIMS = (((1,), (1,)), ((), ()))
 NN_DIMS = (((1,), (0,)), ((), ()))
 
 
-def call(kernel, outs, n_in, scratch=(), smem=(), name=None, flops=0):
+def call(kernel, outs, n_in, scratch=(), smem=(), name=None, mib=8):
     shapes = [jax.ShapeDtypeStruct(s, F32) for s in outs]
     return pl.pallas_call(
         kernel,
@@ -26,7 +27,7 @@
         in_specs=[SMEM if i in smem else VMEM for i in range(n_in)],
         out_specs=[VMEM] * len(shapes) if len(shapes) > 1 else VMEM,
         scratch_shapes=list(scratch),
-        compiler_params=pltpu.CompilerParams(vmem_limit_bytes=56 << 20),
+        compiler_params=pltpu.CompilerParams(vmem_limit_bytes=mib << 20),
         name=name,
     )
 
@@ -55,92 +56,153 @@
     return in_row, in_col.astype(F32).astype(BF16)
 
 
+def tiles_of(ref, *index):
+    return [
+        [ref[index + (slice(y, y + 8), slice(z, z + 128))] for z in range(0, NZ, 128)]
+        for y in range(0, NY, 8)
+    ]
+
+
+def put_tile(ref, index, j, h, value):
+    ref[index + (slice(8 * j, 8 * j + 8), slice(128 * h, 128 * h + 128))] = value
+
+
 def make_laplace():
-    y = lax.broadcasted_iota(jnp.int32, (NY, NZ), 0)
-    z = lax.broadcasted_iota(jnp.int32, (NY, NZ), 1)
-    y_lo, y_hi, z_lo, z_hi = y > 0, y < NY - 1, z > 0, z < NZ - 1
+    y = lax.broadcasted_iota(jnp.int32, (8, 128), 0)
+    z = lax.broadcasted_iota(jnp.int32, (8, 128), 1)
+    y_lo, y_hi, z_lo, z_hi = y == 0, y == 7, z == 0, z == 127
+    zero = jnp.zeros((8, 128), F32)
 
     def laplace(below, f, above):
-        total = below + above
-        total = total + jnp.where(y_lo, pltpu.roll(f, 1, 0), 0.0)
-        total = total + jnp.where(y_hi, pltpu.roll(f, NY - 1, 0), 0.0)
-        total = total + jnp.where(z_lo, pltpu.roll(f, 1, 1), 0.0)
-        total = total + jnp.where(z_hi, pltpu.roll(f, NZ - 1, 1), 0.0)
-        return total - 6.0 * f
+        rows, cols = len(f), len(f[0])
+
+        def shifted(axis, by):
+            return [[pltpu.roll(v, by, axis) for v in line] for line in f]
+
+        up, down, left, right = shifted(0, 1), shifted(0, 7), shifted(1, 1), shifted(1, 127)
+        out = []
+        for j in range(rows):
+            line = []
+            for h in range(cols):
+                total = below[j][h] + above[j][h]
+                side = jnp.where(y_lo, up[j - 1][h] if j > 0 else zero, up[j][h])
+                total = total + side
+                side = jnp.where(y_hi, down[j + 1][h] if j + 1 < rows else zero, down[j][h])
+                total = total + side
+                side = jnp.where(z_lo, left[j][h - 1] if h > 0 else zero, left[j][h])
+                total = total + side
+                side = jnp.where(z_hi, right[j][h + 1] if h + 1 < cols else zero, right[j][h])
+                total = total + side
+                line.append(total - 6.0 * f[j][h])
+            out.append(line)
+        return out
 
     return laplace
 
 
-def pack_pair(p, courant, src, strength, rec, weight, out):
-    other = 2 * (1 - core_of())
-    for i in range(2):
-        out[64 * i : 64 * (i + 1), :] = p[other + i].reshape(64, NZ)
-    out[128:192, :] = courant[...].reshape(64, NZ)
+TILES = [(j, h) for j in range(NY // 8) for h in range(NZ // 128)]
+
+
+def pack(courant, src, strength, rec, weight, out):
     chip_cell = (lax.axis_index("space") // 2) * (OWN * NY * NZ)
-    out[192:200, :] = jnp.zeros((LIST, NZ), F32)
-    out[192:193, 64:128] = (src[...] - chip_cell).astype(F32)
-    out[193:194, 64:128] = strength[...]
-    out[194:195, 64:128] = (rec[...] - chip_cell).astype(F32)
-    out[195:196, 64:128] = weight[...]
-
-
-def pack_chip(p, courant, src, strength, rec, weight, got, own, right, left):
+    out[0:64, :] = courant[...].reshape(64, NZ)
+    out[64:72, :] = jnp.zeros((LIST, NZ), F32)
+    out[64:65, 0:64] = (src[...] - chip_cell).astype(F32)
+    out[65:66, 0:64] = strength[...]
+    out[66:67, 0:64] = (rec[...] - chip_cell).astype(F32)
+    out[67:68, 0:64] = weight[...]
+
+
+def both_lists(own, got, core):
+    first = core == 0
+    low = jnp.where(first, own, got)
+    high = jnp.where(first, got, own)
+    return low[:, 0:128] + pltpu.roll(high[:, 0:128], 64, 1)
+
+
+def forward(
+    p,
+    p_got,
+    cl,
+    cl_got,
+    near,
+    far,
+    near_got,
+    far_got,
+    wavelet,
+    drives,
+    wrec,
+    courant,
+    cells,
+    src,
+    wave,
+    born,
+    probe,
+    drive,
+    table,
+):
     core = core_of()
-    mine = pl.multiple_of(core * 64, 64)
-    theirs = pl.multiple_of((1 - core) * 64, 64)
-    for i in range(2):
-        own[pl.ds(128 * i + mine, 64), :] = p[2 * core + i].reshape(64, NZ)
-        own[pl.ds(128 * i + theirs, 64), :] = got[64 * i : 64 * (i + 1), :]
-    own[pl.ds(256 + mine, 64), :] = courant[...].reshape(64, NZ)
-    own[pl.ds(256 + theirs, 64), :] = got[128:192, :]
-    chip_cell = (lax.axis_index("space") // 2) * (OWN * NY * NZ)
-    own[384:392, :] = got[192:200, :]
-    own[384:385, 0:64] = (src[...] - chip_cell).astype(F32)
-    own[385:386, 0:64] = strength[...]
-    own[386:387, 0:64] = (rec[...] - chip_cell).astype(F32)
-    own[387:388, 0:64] = weight[...]
-    for i in range(3):
-        left[64 * i : 64 * (i + 1), :] = own[128 * i : 128 * i + 64, :]
-        right[64 * i : 64 * (i + 1), :] = own[128 * i + 64 : 128 * i + 128, :]
-    left[192:200, :] = own[384:392, :]
-    right[192:200, :] = own[384:392, :]
-
-
-def forward(
-    own, l1, r1, l2, r2, wavelet, drives, wrec, courant, cells, src, wave, born, probe, drive
-):
+    back = 1 - core
     chip = lax.axis_index("space") // 2
     last = lax.axis_size("space") // 2 - 1
-    keep = [
-        jnp.where(ok, 1.0, 0.0).astype(F32)
-        for ok in (chip >= 2, chip >= 1, chip >= 0, chip <= last - 1, chip <= last - 2)
-    ]
-    slots = (l2, l1, own, r1, r2)
-    lists = (192, 384, 384, 384, 192)
+    lo1, lo2 = chip >= 1, chip >= 2
+    hi1, hi2 = chip <= last - 1, chip <= last - 2
+    first = core == 0
+
+    def factor(ok):
+        return jnp.where(ok, 1.0, 0.0).astype(F32)
+
+    keep_near = factor(jnp.where(first, lo1, hi1))
+    keep_far = factor(jnp.where(first, lo2, hi2))
+    keep_near_got = factor(jnp.where(first, hi1, lo1))
+    keep_far_got = factor(jnp.where(first, hi2, lo2))
+    one = jnp.float32(1.0)
+
+    def put_list(slot, low, high, side, scale):
+        listed = both_lists(low, high, side)
+        at = pl.multiple_of(slot * LIST, LIST)
+        table[pl.ds(at, LIST), :] = listed
+        table[pl.ds(at + 1, 1), :] = scale * listed[1:2]
+
+    put_list(2, cl[64:72, :], cl_got[64:72, :], core, one)
+    put_list(1 + 2 * core, near[576:584, :], near[648:656, :], core, keep_near)
+    put_list(3 - 2 * core, near_got[576:584, :], near_got[648:656, :], back, keep_near_got)
+    put_list(4 * core, far[328:336, :], far[320:328, :], core, keep_far)
+    put_list(4 - 4 * core, far_got[328:336, :], far_got[320:328, :], back, keep_far_got)
+
+    def put_planes(at, ref, p_row, c_row, scale):
+        for i in range(2):
+            row = pl.multiple_of(p_row + 128 * core + 64 * i, 64)
+            probe[i, pl.ds(at, 2)] = ref[pl.ds(row, 64), :].reshape(2, NY, NZ)
+        courant[pl.ds(at, 2)] = scale * ref[c_row : c_row + 64, :].reshape(2, NY, NZ)
+
+    for i in range(2):
+        probe[i, pl.ds(8 + 2 * core, 2)] = p[2 * core + i]
+        probe[i, pl.ds(8 + 2 * back, 2)] = p_got[2 * core + i]
+    courant[pl.ds(8 + 2 * core, 2)] = cl[0:64, :].reshape(2, NY, NZ)
+    courant[pl.ds(8 + 2 * back, 2)] = cl_got[0:64, :].reshape(2, NY, NZ)
+    base, base_got = 4 + 8 * core, 12 - 8 * core
+    put_planes(base + 2 * core, near, 0, 512, keep_near)
+    put_planes(base + 2 * back, near, 256, 584, keep_near)
+    put_planes(base_got + 2 * back, near_got, 0, 512, keep_near_got)
+    put_planes(base_got + 2 * core, near_got, 256, 584, keep_near_got)
+    put_planes(2 + 14 * core, far, 0, 256, keep_far)
+    put_planes(16 - 14 * core, far_got, 0, 256, keep_far_got)
+    zero = jnp.zeros((NY, NZ), F32)
+    for e in (0, 1, 18, 19):
+        courant[e] = zero
     cells[...] = jnp.zeros((LIST, 128), F32)
-    for m, (ref, base) in enumerate(zip(slots, lists)):
-        listed = ref[base : base + LIST, 0:128]
+    for m in range(5):
+        listed = table[LIST * m : LIST * (m + 1), :]
         in_row, in_col = one_hots(listed[0:1])
-        strength = listed[1:2] * keep[m]
-        hi, lo = halves(jnp.where(in_row, strength, 0.0))
+        hi, lo = halves(jnp.where(in_row, listed[1:2], 0.0))
         field = dot(hi, in_col, NT_DIMS) + dot(lo, in_col, NT_DIMS)
         src[4 * m : 4 * m + 4] = field.reshape(OWN, NY, NZ)
         cells[m : m + 1, :] = listed[2:3]
-    for m, ref in ((1, l1), (2, own), (3, r1)):
-        for i in range(2):
-            probe[i, 4 * m : 4 * m + 4] = ref[128 * i : 128 * (i + 1), :].reshape(OWN, NY, NZ)
-        courant[4 * m : 4 * m + 4] = keep[m] * ref[256:384, :].reshape(OWN, NY, NZ)
-    for m, at, ref in ((0, 2, l2), (4, 16, r2)):
-        for i in range(2):
-            probe[i, at : at + 2] = ref[64 * i : 64 * (i + 1), :].reshape(2, NY, NZ)
-        courant[at : at + 2] = keep[m] * ref[128:192, :].reshape(2, NY, NZ)
-    zero = jnp.zeros((NY, NZ), F32)
-    for e in (0, 1, 18, 19):
-        courant[e] = zero
-    first = wavelet[0]
+    pulse_0 = wavelet[0]
 
     def start(e, _):
-        wave[1, e] = first * src[e]
+        wave[1, e] = pulse_0 * src[e]
         wave[0, e] = zero
         for i in range(2):
             born[0, i, e] = zero
@@ -149,7 +211,7 @@
 
     lax.fori_loop(0, EXT, start, 0)
     laplace = make_laplace()
-    listed = own[384:392, 0:128]
+    listed = table[2 * LIST : 3 * LIST, :]
     in_row, in_col = one_hots(listed[2:3])
     row_mask = jnp.where(in_row, 1.0, 0.0)
     weight = listed[3:4]
@@ -159,22 +221,34 @@
         pulse = wavelet[t]
 
         def advance(e, _, now=now, nxt=nxt, pulse=pulse, t=t):
-            c = courant[e]
-            w = wave[now, e]
-            d = c * laplace(wave[now, e - 1], w, wave[now, e + 1])
-            drive[e] = d
+            c = tiles_of(courant, e)
+            w = tiles_of(wave, now, e)
+            d = laplace(tiles_of(wave, now, e - 1), w, tiles_of(wave, now, e + 1))
+            for j, h in TILES:
+                d[j][h] = c[j][h] * d[j][h]
+                put_tile(drive, (e,), j, h, d[j][h])
             if t < 7:
-                wave[nxt, e] = 2.0 * w - wave[nxt, e] + d + pulse * src[e]
+                w_old, s = tiles_of(wave, nxt, e), tiles_of(src, e)
+                for j, h in TILES:
+                    w_new = 2.0 * w[j][h] - w_old[j][h] + d[j][h] + pulse * s[j][h]
+                    put_tile(wave, (nxt, e), j, h, w_new)
             for i in range(2):
-                force = probe[i, e] * d
+                q = tiles_of(probe, i, e)
                 if t > 1:
-                    b = born[now, i, e]
-                    bent = laplace(born[now, i, e - 1], b, born[now, i, e + 1])
-                    force = force + (2.0 * b - born[nxt, i, e] + c * bent)
-                born[nxt, i, e] = force
+                    b = tiles_of(born, now, i, e)
+                    bent = laplace(
+                        tiles_of(born, now, i, e - 1), b, tiles_of(born, now, i, e + 1)
+                    )
+                    b_old = tiles_of(born, nxt, i, e)
+                for j, h in TILES:
+                    b_new = q[j][h] * d[j][h]
+                    if t > 1:
+                        moved = 2.0 * b[j][h] - b_old[j][h] + c[j][h] * bent[j][h]
+                        b_new = b_new + moved
+                    put_tile(born, (nxt, i, e), j, h, b_new)
             return 0
 
-        lax.fori_loop(1 + t, 19 - t, advance, 0)
+        lax.fori_loop(1 + t, 19 - t, advance, 0, unroll=UNROLL)
         drives[t - 1] = drive[8:12]
         for i in range(2):
             hi, lo = halves(born[nxt, i, 8:12].reshape(OWN * NY, NZ))
@@ -184,9 +258,19 @@
             wrec[at : at + 1, :] = value * weight
 
 
-def adjoint(courant, cells, w2l, w1l, w0, w1r, w2r, drives, mine, send, inj, adj, bent, hess):
-    recs = (w2l, w1l, w0, w1r, w2r)
-    for m, ref in enumerate(recs):
+def adjoint(
+    courant, cells, w0, near, far, near_got, far_got, drives, mine, send, inj, adj, bent, hess
+):
+    first = core_of() == 0
+    side = [near[0:16, :], near_got[16:32, :], far[0:16, :], far_got[16:32, :]]
+    recs = (
+        jnp.where(first, side[2], side[3]),
+        jnp.where(first, side[0], side[1]),
+        w0[...],
+        jnp.where(first, side[1], side[0]),
+        jnp.where(first, side[3], side[2]),
+    )
+    for m, rec in enumerate(recs):
         in_row, in_col = one_hots(cells[m : m + 1, :])
         for k in range(8, 1, -1):
             lo_e, hi_e = 10 - k, 9 + k
@@ -194,7 +278,7 @@
                 continue
             for i in range(2):
                 at = 2 * (k - 2) + i
-                hi, lo = halves(ref[at : at + 1, :])
+                hi, lo = halves(rec[at : at + 1, :])
                 a = jnp.where(in_row, hi.astype(F32), 0.0).astype(BF16)
                 b = jnp.where(in_row, lo.astype(F32), 0.0).astype(BF16)
                 field = dot(a, in_col, NT_DIMS) + dot(b, in_col, NT_DIMS)
@@ -216,17 +300,25 @@
         now, nxt = k % 2, (k + 1) % 2
 
         def advance(e, _, k=k, now=now, nxt=nxt):
+            c = tiles_of(courant, e)
             for i in range(2):
-                a = 2.0 * adj[nxt, i, e] + inj[k - 2, i, e]
-                a = a + laplace(bent[nxt, i, e - 1], bent[nxt, i, e], bent[nxt, i, e + 1])
-                if k < 7:
-                    a = a - adj[now, i, e]
-                adj[now, i, e] = a
-                if k > 2:
-                    bent[now, i, e] = courant[e] * a
+                a_new = laplace(
+                    tiles_of(bent, nxt, i, e - 1),
+                    tiles_of(bent, nxt, i, e),
+                    tiles_of(bent, nxt, i, e + 1),
+                )
+                a, a_old = tiles_of(adj, nxt, i, e), tiles_of(adj, now, i, e)
+                pushed = tiles_of(inj, k - 2, i, e)
+                for j, h in TILES:
+                    value = a_new[j][h] + (2.0 * a[j][h] + pushed[j][h])
+                    if k < 7:
+                        value = value - a_old[j][h]
+                    put_tile(adj, (now, i, e), j, h, value)
+                    if k > 2:
+                        put_tile(bent, (now, i, e), j, h, c[j][h] * value)
             return 0
 
-        lax.fori_loop(10 - k, 10 + k, advance, 0)
+        lax.fori_loop(10 - k, 10 + k, advance, 0, unroll=UNROLL)
         for i in range(2):
             for e in range(OWN):
                 hess[i, e] = hess[i, e] + drives[k - 2, e] * adj[now, i, 8 + e]
@@ -329,39 +421,43 @@
     receiver_weight,
 ):
     count = lax.axis_size("space")
+    def swap(x):
+        return lax.ppermute(x, "space", [(i, i ^ 1) for i in range(count)])
+
+    def inward(x, by):
+        pairs = [(i, (i + (by if i % 2 == 0 else -by)) % count) for i in range(count)]
+        return lax.ppermute(x, "space", pairs)
+
+    p = probe_fields
     lists = [
         v.reshape(1, -1) for v in (source_cells, source_strength, receiver_cells, receiver_weight)
     ]
-
-    def swap(x):
-        return lax.ppermute(x, "space", [(i, i ^ 1) for i in range(count)])
-
-    def shift(x, by):
-        return lax.ppermute(x, "space", [(i, (i + by) % count) for i in range(count)])
-
-    pair = call(pack_pair, [(200, NZ)], 6, name="pack_pair")(probe_fields, courant_field, *lists)
-    got = swap(pair)
-    own, right, left = call(
-        pack_chip, [(392, NZ), (200, NZ), (200, NZ)], 7, name="pack_chip"
-    )(probe_fields, courant_field, *lists, got)
-    l1, r1 = shift(own, 2), shift(own, -2)
-    l2, r2 = shift(right, 4), shift(left, -4)
+    cl = call(pack, [(72, NZ)], 5, name="pack")(courant_field, *lists)
+    p_got, cl_got = swap(p), swap(cl)
+    flat = p_got.reshape(256, NZ)
+    near = inward(jnp.concatenate([p.reshape(256, NZ), flat, cl, cl_got], axis=0), 2)
+    far = inward(jnp.concatenate([flat, cl_got, cl[64:72]], axis=0), 4)
+    near_got, far_got = swap(near), swap(far)
     plane = (NY, NZ)
     drives, wrec, courant, cells = call(
         forward,
         [(7, OWN) + plane, (16, 128), (EXT,) + plane, (LIST, 128)],
-        6,
+        9,
         scratch=[
             pltpu.VMEM((EXT,) + plane, F32),
             pltpu.VMEM((2, EXT) + plane, F32),
             pltpu.VMEM((2, 2, EXT) + plane, F32),
             pltpu.VMEM((2, EXT) + plane, F32),
             pltpu.VMEM((EXT,) + plane, F32),
+            pltpu.VMEM((5 * LIST, 128), F32),
         ],
-        smem=(5,),
+        smem=(8,),
         name="forward",
-    )(own, l1, r1, l2, r2, wavelet)
-    w1l, w1r, w2l, w2r = shift(wrec, 2), shift(wrec, -2), shift(wrec, 4), shift(wrec, -4)
+        mib=16,
+    )(p, p_got, cl, cl_got, near, far, near_got, far_got, wavelet)
+    all_rec = jnp.concatenate([wrec, swap(wrec)], axis=0)
+    rec_near, rec_far = inward(all_rec, 2), inward(all_rec, 4)
+    rec_near_got, rec_far_got = swap(rec_near), swap(rec_far)
     half = (2, 2) + plane
     mine, send = call(
         adjoint,
@@ -374,7 +470,8 @@
             pltpu.VMEM((2, OWN) + plane, F32),
         ],
         name="adjoint",
-    )(courant, cells, w2l, w1l, wrec, w1r, w2r, drives)
+        mib=24,
+    )(courant, cells, wrec, rec_near, rec_far, rec_near_got, rec_far_got, drives)
     hessian = call(finish, [(4, 2) + plane], 4, name="finish")(
         probe_fields, prior_weight, mine, swap(send)
     )

time: 123 us -> 94.6 us (0.77)
  Pallas kernels: 36.9 us -> 15.1 us
  starting transfers between devices: 30.2 us -> 23.3 us
  local copies, waits for them, and re-layouts: 4.28 us -> 2.5 us
    pallas_call x1, Pallas kernels: 13.6 us -> 5.93 us  [shards(): call(forward, [(7, OWN) + plane, (16, 128), (EXT,) + plane, (LIST, 128)],...]
    ppermute x8 -> x4, starting transfers between devices: 20.2 us -> 13.8 us  [inward(): return lax.ppermute(x, 'space', pairs)]
    pallas_call x1, Pallas kernels: 10.4 us -> 4.2 us  [shards(): call(adjoint, [half, half], 8, scratch=[pltpu.VMEM((7, 2, EXT) + plane, F...]
    pallas_call x2 -> x1, Pallas kernels: 3.82 us -> 0.01 us  [shards(): cl = call(pack, [(72, NZ)], 5, name='pack')(courant_field, *lists)]
    ppermute x2 -> x8, waiting for transfers between devices: 2.49 us -> 5.79 us  [swap(): return lax.ppermute(x, 'space', [(i, i ^ 1) for i in range(count)])]
    ppermute x8 -> x4, waiting for transfers between devices: 18.1 us -> 15.4 us  [inward(): return lax.ppermute(x, 'space', pairs)]
    pallas_call x1, Pallas kernels: 2.72 us -> 0.9 us  [shards(): call(gram_part, [(count, 2, 128)], 4, scratch=[pltpu.VMEM((256, 128), F32...]
    unnamed x26 -> x19, local copies, waits for them, and re-layouts: 4.28 us -> 2.5 us
  transfers between devices with their start and end apart: 13 -> 15, of which waited for: 8 -> 11; matrix products, arithmetic and copies ran while one was open for 0% -> 0% of each run, Pallas kernels for 0% -> 0%
where the time goes in v2:
time: 94.6 us; the launch traced here: 94.4 us
  waiting for transfers between devices  35.6 us (38%)
  starting transfers between devices  23.3 us (25%)
  blocking collectives  16.2 us (17%)
  Pallas kernels  15.1 us (16%)
  local copies, waits for them, and re-layouts  2.5 us (3%)
  other arithmetic  1.02 us (1%)
    all_to_all x1, blocking collectives, shards(): parts = lax.all_to_all(part, 'space', 0, 0, tiled=True)  16.2 us
    ppermute x4, waiting for transfers between devices, inward(): return lax.ppermute(x, 'space', pairs)  15.4 us
    ppermute x3, waiting for transfers between devices, shards(): lax.ppermute(hessian, 'probe', [(i, (i + b) % groups) for i in range(grou...  14.4 us
    ppermute x4, starting transfers between devices, inward(): return lax.ppermute(x, 'space', pairs)  13.8 us
    ppermute x8, starting transfers between devices, swap(): return lax.ppermute(x, 'space', [(i, i ^ 1) for i in range(count)])  5.93 us
    pallas_call x1, Pallas kernels, shards(): call(forward, [(7, OWN) + plane, (16, 128), (EXT,) + plane, (LIST, 128)],...  5.93 us
    ppermute x8, waiting for transfers between devices, swap(): return lax.ppermute(x, 'space', [(i, i ^ 1) for i in range(count)])  5.79 us
    pallas_call x1, Pallas kernels, shards(): call(adjoint, [half, half], 8, scratch=[pltpu.VMEM((7, 2, EXT) + plane, F...  4.2 us
  transfers between devices with their start and end apart: 15, of which 11 were waited for; matrix products, arithmetic and copies ran while one was open for 0% of the time, Pallas kernels for 0%

profile of v2, /device:TPU:1, one launch (start us, length us, event | category | flops | bytes accessed | tf_op | source)
XLA Modules:
  0.0 94.4 jit_solution(4594989896153195541)
XLA Ops:
  0.6 3.3 %collective-permute-start = (f32[4,2,32,256]{3,2,1,0:T(8,128)}, f32[4,2,32,256]{3,2,1,0:T(8,128)S(1)}, u32[]{:S(2)}, u32[]{:S(2)}) collective-permute-start(f32[4,2,32,256]{3,2,1,0:T(8,128)} %p.3), channel_id=1, source_target_pairs={{0,1},{1,0},{2,3},{3,2},{4,5},{5,4},{6,7},{7,6},{8,9},{9,8},{10,11... | collective-permute-start | bytes 786440 | tf_op jit(solution)/shard_map/ppermute | solution.py:425
  3.9 0.6 copy-done.7
  4.6 0.8 copy-done.2
  5.6 1.2 %collective-permute-done.1.cl_got = f32[72,256]{1,0:T(8,128)S(1)} collective-permute-done((f32[72,256]{1,0:T(8,128)S(1)}, f32[72,256]{1,0:T(8,128)S(1)}, u32[]{:S(2)}, u32[]{:S(2)}) %collective-permute-start.1) | collective-permute-done | bytes 73760 | tf_op jit(solution)/shard_map/ppermute | solution.py:425
  6.8 1.0 %pad_maximum_fusion = f32[656,256]{1,0:T(8,128)S(1)} fusion(f32[72,256]{1,0:T(8,128)S(1)} %collective-permute-done.1.cl_got, f32[72,256]{1,0:T(8,128)S(1)} %pack.1.cl, f32[256,256]{1,0:T(8,128)S(1)} %bitcast.7, f32[256,256]{1,0:T(8,128)} %bitcast.6), kind=kLoop, calls=%fused_computation | loop fusion | flops 503808 | bytes 1343488 | tf_op jit(solution)/shard_map/concatenate | solution.py:438
  7.8 6.4 %collective-permute-start.2 = (f32[656,256]{1,0:T(8,128)S(1)}, f32[656,256]{1,0:T(8,128)S(1)}, u32[]{:S(2)}, u32[]{:S(2)}) collective-permute-start(f32[656,256]{1,0:T(8,128)S(1)} %pad_maximum_fusion), channel_id=1, source_target_pairs={{0,2},{1,63},{2,4},{3,1},{4,6},{5,3},{6,8},{7,5},{8,10},{9,7},{10,... | collective-permute-start | bytes 2015240 | tf_op jit(solution)/shard_map/ppermute | solution.py:429
  14.3 1.2 %collective-permute-start.3 = (f32[336,256]{1,0:T(8,128)S(1)}, f32[336,256]{1,0:T(8,128)S(1)}, u32[]{:S(2)}, u32[]{:S(2)}) collective-permute-start(f32[336,256]{1,0:T(8,128)S(1)} %pad_maximum_fusion.1), channel_id=1, source_target_pairs={{0,4},{1,61},{2,6},{3,63},{4,8},{5,1},{6,10},{7,3},{8,12},{9,5},{1... | collective-permute-start | bytes 1032200 | tf_op jit(solution)/shard_map/ppermute | solution.py:429
  15.5 10.1 %collective-permute-done.2.near = f32[656,256]{1,0:T(8,128)S(1)} collective-permute-done((f32[656,256]{1,0:T(8,128)S(1)}, f32[656,256]{1,0:T(8,128)S(1)}, u32[]{:S(2)}, u32[]{:S(2)}) %collective-permute-start.2) | collective-permute-done | bytes 671776 | tf_op jit(solution)/shard_map/ppermute | solution.py:429
  25.6 3.7 %collective-permute-done.3.far = f32[336,256]{1,0:T(8,128)S(1)} collective-permute-done((f32[336,256]{1,0:T(8,128)S(1)}, f32[336,256]{1,0:T(8,128)S(1)}, u32[]{:S(2)}, u32[]{:S(2)}) %collective-permute-start.3) | collective-permute-done | bytes 344096 | tf_op jit(solution)/shard_map/ppermute | solution.py:429
  29.3 1.6 %collective-permute-done.5.far_got = f32[336,256]{1,0:T(8,128)S(1)} collective-permute-done((f32[336,256]{1,0:T(8,128)S(1)}, f32[336,256]{1,0:T(8,128)S(1)}, u32[]{:S(2)}, u32[]{:S(2)}) %collective-permute-start.5) | collective-permute-done | bytes 344096 | tf_op jit(solution)/shard_map/ppermute | solution.py:425
  31.0 5.9 %forward.1 = (f32[7,4,32,256]{3,2,1,0:T(8,128)S(1)}, f32[16,128]{1,0:T(8,128)S(1)}, f32[20,32,256]{2,1,0:T(8,128)S(1)}, f32[8,128]{1,0:T(8,128)S(1)}) custom-call(f32[4,2,32,256]{3,2,1,0:T(8,128)S(1)} %copy-done, f32[4,2,32,256]{3,2,1,0:T(8,128)S(1)} %collective-permute-done.p_got, f32[72,256]{1,0:T(8,128)S(1)} %pack.1.cl, ...), custom_call_target="tpu_custom_call" | custom-call | tf_op jit(solution)/shard_map/forward/pallas_call | solution.py:442
  36.9 0.2 collective-permute-start.6
  37.1 1.0 %collective-permute-done.6 = f32[16,128]{1,0:T(8,128)S(1)} collective-permute-done((f32[16,128]{1,0:T(8,128)S(1)}, f32[16,128]{1,0:T(8,128)S(1)}, u32[]{:S(2)}, u32[]{:S(2)}) %collective-permute-start.6) | collective-permute-done | bytes 8224 | tf_op jit(solution)/shard_map/ppermute | solution.py:425
  38.2 6.1 %collective-permute-start.8 = (f32[32,128]{1,0:T(8,128)S(1)}, f32[32,128]{1,0:T(8,128)S(1)}, u32[]{:S(2)}, u32[]{:S(2)}) collective-permute-start(f32[32,128]{1,0:T(8,128)S(1)} %constant_dynamic-update-slice_fusion), channel_id=1, source_target_pairs={{0,4},{1,61},{2,6},{3,63},{4,8},{5,1},{6,10},{7,3},{8,12},{9,5},{1... | collective-permute-start | bytes 49160 | tf_op jit(solution)/shard_map/ppermute | solution.py:429
  44.3 0.9 collective-permute-done.8.far
  45.2 1.3 %collective-permute-start.10 = (f32[32,128]{1,0:T(8,128)S(1)}, f32[32,128]{1,0:T(8,128)S(1)}, u32[]{:S(2)}, u32[]{:S(2)}) collective-permute-start(f32[32,128]{1,0:T(8,128)S(1)} %collective-permute-done.8.far), channel_id=1, source_target_pairs={{0,1},{1,0},{2,3},{3,2},{4,5},{5,4},{6,7},{7,6},{8,9},{9,8},{10,11... | collective-permute-start | bytes 49160 | tf_op jit(solution)/shard_map/ppermute | solution.py:425
  46.4 0.7 collective-permute-done.7.near
  47.2 0.6 collective-permute-start.9
  47.8 0.8 collective-permute-done.9.near_got
  48.6 4.2 %adjoint.1 = (f32[2,2,32,256]{3,2,1,0:T(8,128)S(1)}, f32[2,2,32,256]{3,2,1,0:T(8,128)S(1)}) custom-call(f32[20,32,256]{2,1,0:T(8,128)S(1)} %get-tuple-element.8.courant, f32[8,128]{1,0:T(8,128)S(1)} %get-tuple-element.9.cells, f32[16,128]{1,0:T(8,128)S(1)} %get-tuple-element.10.w0, f32[32,128]{1,0:T(8,128)S(1)} %collective-permute-done.7.near, ...), custom_call_target="tpu_custom_call" | custom-call | tf_op jit(solution)/shard_map/adjoint/pallas_call | solution.py:462
  52.8 0.4 collective-permute-start.11
  53.2 1.0 %collective-permute-done.11.got = f32[2,2,32,256]{3,2,1,0:T(8,128)S(1)} collective-permute-done((f32[2,2,32,256]{3,2,1,0:T(8,128)S(1)}, f32[2,2,32,256]{3,2,1,0:T(8,128)S(1)}, u32[]{:S(2)}, u32[]{:S(2)}) %collective-permute-start.11) | collective-permute-done | bytes 131104 | tf_op jit(solution)/shard_map/ppermute | solution.py:425
  54.2 0.7 finish.1.h0.refs_1_
  55.0 2.5 %collective-permute-start.14 = (f32[4,2,32,256]{3,2,1,0:T(8,128)}, f32[4,2,32,256]{3,2,1,0:T(8,128)S(1)}, u32[]{:S(2)}, u32[]{:S(2)}) collective-permute-start(f32[4,2,32,256]{3,2,1,0:T(8,128)} %finish.1.h0.refs_1_), channel_id=1, source_target_pairs={{0,192},{64,0},{128,64},{192,128},{1,193},{65,1},{129,65},{193,129... | collective-permute-start | bytes 786440 | tf_op jit(solution)/shard_map/ppermute | solution.py:480
  57.5 0.5 collective-permute-start.13
  58.0 0.6 collective-permute-start.12
  58.6 10.0 %collective-permute-done.14.h3.refs_4_ = f32[4,2,32,256]{3,2,1,0:T(8,128)S(1)} collective-permute-done((f32[4,2,32,256]{3,2,1,0:T(8,128)}, f32[4,2,32,256]{3,2,1,0:T(8,128)S(1)}, u32[]{:S(2)}, u32[]{:S(2)}) %collective-permute-start.14) | collective-permute-done | bytes 262176 | tf_op jit(solution)/shard_map/ppermute | solution.py:480
  68.6 4.4 %collective-permute-done.12.h1.refs_2_ = f32[4,2,32,256]{3,2,1,0:T(8,128)S(1)} collective-permute-done((f32[4,2,32,256]{3,2,1,0:T(8,128)}, f32[4,2,32,256]{3,2,1,0:T(8,128)S(1)}, u32[]{:S(2)}, u32[]{:S(2)}) %collective-permute-start.12) | collective-permute-done | bytes 262176 | tf_op jit(solution)/shard_map/ppermute | solution.py:480
  73.0 0.9 %copy-done.1 = f32[4,2,32,256]{3,2,1,0:T(8,128)S(1)} copy-done((f32[4,2,32,256]{3,2,1,0:T(8,128)S(1)}, f32[4,2,32,256]{3,2,1,0:T(8,128)}, u32[]{:S(2)}) %copy-start.1) | copy-done | bytes 262168
  74.0 0.9 gram.1
  74.9 16.2 %all_to_all.5.refs_0_ = f32[64,2,128]{2,1,0:T(2,128)S(1)} all-to-all(f32[64,2,128]{2,1,0:T(2,128)S(1)} %gram.1), channel_id=1, replica_groups=mesh['probe'=4,'space'=64] {'space'}, dimensions={0} | all-to-all | bytes 131072 | tf_op jit(solution)/shard_map/all_to_all | solution.py:486
  91.0 3.4 %whiten.1 = f32[4,2,32,256]{3,2,1,0:T(8,128)} custom-call(f32[64,2,128]{2,1,0:T(2,128)S(1)} %all_to_all.5.refs_0_, f32[4,2,32,256]{3,2,1,0:T(8,128)S(1)} %copy-done.1, f32[4,2,32,256]{3,2,1,0:T(8,128)S(1)} %collective-permute-done.12.h1.refs_2_, f32[4,2,32,256]{3,2,1,0:T(8,128)S(1)} %collective-permute-done.13.h2.refs_3_, ...), custom_call_target="tpu_custom_call" | custom-call | tf_op jit(solution)/shard_map/whiten/pallas_call | solution.py:492
  (28 shorter events, 0.2 us)
Async XLA Ops:
  0.6 6.2 %collective-permute-start = (f32[4,2,32,256]{3,2,1,0:T(8,128)}, f32[4,2,32,256]{3,2,1,0:T(8,128)S(1)}, u32[]{:S(2)}, u32[]{:S(2)}) collective-permute-start(f32[4,2,32,256]{3,2,1,0:T(8,128)} %p.3), channel_id=1, source_target_pairs={{0,1},{1,0},{2,3},{3,2},{4,5},{5,4},{6,7},{7,6},{8,9},{9,8},{10,11... | collective-permute-start | bytes 786440 | tf_op jit(solution)/shard_map/ppermute | solution.py:425
  3.9 0.7 copy-start.7
  3.9 0.7 copy-start.4
  3.9 0.7 copy-start.5
  3.9 0.7 copy-start.6
  4.6 0.8 copy-start.2
  5.5 1.4 %collective-permute-start.1 = (f32[72,256]{1,0:T(8,128)S(1)}, f32[72,256]{1,0:T(8,128)S(1)}, u32[]{:S(2)}, u32[]{:S(2)}) collective-permute-start(f32[72,256]{1,0:T(8,128)S(1)} %pack.1.cl), channel_id=1, source_target_pairs={{0,1},{1,0},{2,3},{3,2},{4,5},{5,4},{6,7},{7,6},{8,9},{9,8},{10,11... | collective-permute-start | bytes 221192 | tf_op jit(solution)/shard_map/ppermute | solution.py:425
  7.8 17.8 %collective-permute-start.2 = (f32[656,256]{1,0:T(8,128)S(1)}, f32[656,256]{1,0:T(8,128)S(1)}, u32[]{:S(2)}, u32[]{:S(2)}) collective-permute-start(f32[656,256]{1,0:T(8,128)S(1)} %pad_maximum_fusion), channel_id=1, source_target_pairs={{0,2},{1,63},{2,4},{3,1},{4,6},{5,3},{6,8},{7,5},{8,10},{9,7},{10,... | collective-permute-start | bytes 2015240 | tf_op jit(solution)/shard_map/ppermute | solution.py:429
  14.2 16.7 %copy-start = (f32[4,2,32,256]{3,2,1,0:T(8,128)S(1)}, f32[4,2,32,256]{3,2,1,0:T(8,128)}, u32[]{:S(2)}) copy-start(f32[4,2,32,256]{3,2,1,0:T(8,128)} %p.3) | copy-start | bytes 786436
  14.2 16.7 %copy-start.8 = (f32[8]{0:T(128)S(1)}, f32[8]{0:T(128)}, u32[]{:S(2)}) copy-start(f32[8]{0:T(128)} %wavelet.1) | copy-start | bytes 100
  14.3 15.0 %collective-permute-start.3 = (f32[336,256]{1,0:T(8,128)S(1)}, f32[336,256]{1,0:T(8,128)S(1)}, u32[]{:S(2)}, u32[]{:S(2)}) collective-permute-start(f32[336,256]{1,0:T(8,128)S(1)} %pad_maximum_fusion.1), channel_id=1, source_target_pairs={{0,4},{1,61},{2,6},{3,63},{4,8},{5,1},{6,10},{7,3},{8,12},{9,5},{1... | collective-permute-start | bytes 1032200 | tf_op jit(solution)/shard_map/ppermute | solution.py:429
  25.6 5.3 %collective-permute-start.4 = (f32[656,256]{1,0:T(8,128)S(1)}, f32[656,256]{1,0:T(8,128)S(1)}, u32[]{:S(2)}, u32[]{:S(2)}) collective-permute-start(f32[656,256]{1,0:T(8,128)S(1)} %collective-permute-done.2.near), channel_id=1, source_target_pairs={{0,1},{1,0},{2,3},{3,2},{4,5},{5,4},{6,7},{7,6},{8,9},{9,8},{10,11... | collective-permute-start | bytes 2015240 | tf_op jit(solution)/shard_map/ppermute | solution.py:425
  29.3 1.7 %collective-permute-start.5 = (f32[336,256]{1,0:T(8,128)S(1)}, f32[336,256]{1,0:T(8,128)S(1)}, u32[]{:S(2)}, u32[]{:S(2)}) collective-permute-start(f32[336,256]{1,0:T(8,128)S(1)} %collective-permute-done.3.far), channel_id=1, source_target_pairs={{0,1},{1,0},{2,3},{3,2},{4,5},{5,4},{6,7},{7,6},{8,9},{9,8},{10,11... | collective-permute-start | bytes 1032200 | tf_op jit(solution)/shard_map/ppermute | solution.py:425
  36.9 1.3 %collective-permute-start.6 = (f32[16,128]{1,0:T(8,128)S(1)}, f32[16,128]{1,0:T(8,128)S(1)}, u32[]{:S(2)}, u32[]{:S(2)}) collective-permute-start(f32[16,128]{1,0:T(8,128)S(1)} %get-tuple-element.10.w0), channel_id=1, source_target_pairs={{0,1},{1,0},{2,3},{3,2},{4,5},{5,4},{6,7},{7,6},{8,9},{9,8},{10,11... | collective-permute-start | bytes 24584 | tf_op jit(solution)/shard_map/ppermute | solution.py:425
  38.2 7.0 %collective-permute-start.8 = (f32[32,128]{1,0:T(8,128)S(1)}, f32[32,128]{1,0:T(8,128)S(1)}, u32[]{:S(2)}, u32[]{:S(2)}) collective-permute-start(f32[32,128]{1,0:T(8,128)S(1)} %constant_dynamic-update-slice_fusion), channel_id=1, source_target_pairs={{0,4},{1,61},{2,6},{3,63},{4,8},{5,1},{6,10},{7,3},{8,12},{9,5},{1... | collective-permute-start | bytes 49160 | tf_op jit(solution)/shard_map/ppermute | solution.py:429
  44.3 2.9 %collective-permute-start.7 = (f32[32,128]{1,0:T(8,128)S(1)}, f32[32,128]{1,0:T(8,128)S(1)}, u32[]{:S(2)}, u32[]{:S(2)}) collective-permute-start(f32[32,128]{1,0:T(8,128)S(1)} %constant_dynamic-update-slice_fusion), channel_id=1, source_target_pairs={{0,2},{1,63},{2,4},{3,1},{4,6},{5,3},{6,8},{7,5},{8,10},{9,7},{10,... | collective-permute-start | bytes 49160 | tf_op jit(solution)/shard_map/ppermute | solution.py:429
  45.2 2.6 %collective-permute-start.10 = (f32[32,128]{1,0:T(8,128)S(1)}, f32[32,128]{1,0:T(8,128)S(1)}, u32[]{:S(2)}, u32[]{:S(2)}) collective-permute-start(f32[32,128]{1,0:T(8,128)S(1)} %collective-permute-done.8.far), channel_id=1, source_target_pairs={{0,1},{1,0},{2,3},{3,2},{4,5},{5,4},{6,7},{7,6},{8,9},{9,8},{10,11... | collective-permute-start | bytes 49160 | tf_op jit(solution)/shard_map/ppermute | solution.py:425
  47.2 1.4 %collective-permute-start.9 = (f32[32,128]{1,0:T(8,128)S(1)}, f32[32,128]{1,0:T(8,128)S(1)}, u32[]{:S(2)}, u32[]{:S(2)}) collective-permute-start(f32[32,128]{1,0:T(8,128)S(1)} %collective-permute-done.7.near), channel_id=1, source_target_pairs={{0,1},{1,0},{2,3},{3,2},{4,5},{5,4},{6,7},{7,6},{8,9},{9,8},{10,11... | collective-permute-start | bytes 49160 | tf_op jit(solution)/shard_map/ppermute | solution.py:425
  48.6 5.6 %copy-start.3 = (f32[2,32,256]{2,1,0:T(8,128)S(1)}, f32[2,32,256]{2,1,0:T(8,128)}, u32[]{:S(2)}) copy-start(f32[2,32,256]{2,1,0:T(8,128)} %prior.1) | copy-start | bytes 196612
  52.8 1.4 %collective-permute-start.11 = (f32[2,2,32,256]{3,2,1,0:T(8,128)S(1)}, f32[2,2,32,256]{3,2,1,0:T(8,128)S(1)}, u32[]{:S(2)}, u32[]{:S(2)}) collective-permute-start(f32[2,2,32,256]{3,2,1,0:T(8,128)S(1)} %get-tuple-element.13), channel_id=1, source_target_pairs={{0,1},{1,0},{2,3},{3,2},{4,5},{5,4},{6,7},{7,6},{8,9},{9,8},{10,11... | collective-permute-start | bytes 393224 | tf_op jit(solution)/shard_map/ppermute | solution.py:425
  55.0 13.6 %collective-permute-start.14 = (f32[4,2,32,256]{3,2,1,0:T(8,128)}, f32[4,2,32,256]{3,2,1,0:T(8,128)S(1)}, u32[]{:S(2)}, u32[]{:S(2)}) collective-permute-start(f32[4,2,32,256]{3,2,1,0:T(8,128)} %finish.1.h0.refs_1_), channel_id=1, source_target_pairs={{0,192},{64,0},{128,64},{192,128},{1,193},{65,1},{129,65},{193,129... | collective-permute-start | bytes 786440 | tf_op jit(solution)/shard_map/ppermute | solution.py:480
  57.5 11.1 %collective-permute-start.13 = (f32[4,2,32,256]{3,2,1,0:T(8,128)}, f32[4,2,32,256]{3,2,1,0:T(8,128)S(1)}, u32[]{:S(2)}, u32[]{:S(2)}) collective-permute-start(f32[4,2,32,256]{3,2,1,0:T(8,128)} %finish.1.h0.refs_1_), channel_id=1, source_target_pairs={{0,128},{64,192},{128,0},{192,64},{1,129},{65,193},{129,1},{193,65... | collective-permute-start | bytes 786440 | tf_op jit(solution)/shard_map/ppermute | solution.py:480
  58.0 15.0 %collective-permute-start.12 = (f32[4,2,32,256]{3,2,1,0:T(8,128)}, f32[4,2,32,256]{3,2,1,0:T(8,128)S(1)}, u32[]{:S(2)}, u32[]{:S(2)}) collective-permute-start(f32[4,2,32,256]{3,2,1,0:T(8,128)} %finish.1.h0.refs_1_), channel_id=1, source_target_pairs={{0,64},{64,128},{128,192},{192,0},{1,65},{65,129},{129,193},{193,1... | collective-permute-start | bytes 786440 | tf_op jit(solution)/shard_map/ppermute | solution.py:480
  73.0 1.0 %copy-start.1 = (f32[4,2,32,256]{3,2,1,0:T(8,128)S(1)}, f32[4,2,32,256]{3,2,1,0:T(8,128)}, u32[]{:S(2)}) copy-start(f32[4,2,32,256]{3,2,1,0:T(8,128)} %finish.1.h0.refs_1_) | copy-start | bytes 786436

commit v3 on v2

--- a/solution.py
+++ b/solution.py
@@ -19,7 +19,7 @@
 NN_DIMS = (((1,), (0,)), ((), ()))
 
 
-def call(kernel, outs, n_in, scratch=(), smem=(), name=None, mib=8):
+def call(kernel, outs, n_in, scratch=(), smem=(), mib=8):
     shapes = [jax.ShapeDtypeStruct(s, F32) for s in outs]
     return pl.pallas_call(
         kernel,
@@ -28,7 +28,6 @@
         out_specs=[VMEM] * len(shapes) if len(shapes) > 1 else VMEM,
         scratch_shapes=list(scratch),
         compiler_params=pltpu.CompilerParams(vmem_limit_bytes=mib << 20),
-        name=name,
     )
 
 
@@ -103,14 +102,13 @@
 TILES = [(j, h) for j in range(NY // 8) for h in range(NZ // 128)]
 
 
-def pack(courant, src, strength, rec, weight, out):
+def pack(src, strength, rec, weight, out):
     chip_cell = (lax.axis_index("space") // 2) * (OWN * NY * NZ)
-    out[0:64, :] = courant[...].reshape(64, NZ)
-    out[64:72, :] = jnp.zeros((LIST, NZ), F32)
-    out[64:65, 0:64] = (src[...] - chip_cell).astype(F32)
-    out[65:66, 0:64] = strength[...]
-    out[66:67, 0:64] = (rec[...] - chip_cell).astype(F32)
-    out[67:68, 0:64] = weight[...]
+    out[...] = jnp.zeros((LIST, NZ), F32)
+    out[0:1, 0:64] = (src[...] - chip_cell).astype(F32)
+    out[1:2, 0:64] = strength[...]
+    out[2:3, 0:64] = (rec[...] - chip_cell).astype(F32)
+    out[3:4, 0:64] = weight[...]
 
 
 def both_lists(own, got, core):
@@ -123,12 +121,16 @@
 def forward(
     p,
     p_got,
-    cl,
-    cl_got,
+    c_own,
+    c_got,
+    lists,
+    lists_got,
     near,
     far,
     near_got,
     far_got,
+    near_p,
+    far_p,
     wavelet,
     drives,
     wrec,
@@ -164,30 +166,38 @@
         table[pl.ds(at, LIST), :] = listed
         table[pl.ds(at + 1, 1), :] = scale * listed[1:2]
 
-    put_list(2, cl[64:72, :], cl_got[64:72, :], core, one)
-    put_list(1 + 2 * core, near[576:584, :], near[648:656, :], core, keep_near)
-    put_list(3 - 2 * core, near_got[576:584, :], near_got[648:656, :], back, keep_near_got)
-    put_list(4 * core, far[328:336, :], far[320:328, :], core, keep_far)
-    put_list(4 - 4 * core, far_got[328:336, :], far_got[320:328, :], back, keep_far_got)
-
-    def put_planes(at, ref, p_row, c_row, scale):
+    put_list(2, lists[...], lists_got[...], core, one)
+    put_list(1 + 2 * core, near[384:392, :], near[392:400, :], core, keep_near)
+    put_list(3 - 2 * core, near_got[384:392, :], near_got[392:400, :], back, keep_near_got)
+    put_list(4 * core, far[192:200, :], far[200:208, :], core, keep_far)
+    put_list(4 - 4 * core, far_got[192:200, :], far_got[200:208, :], back, keep_far_got)
+
+    def put_probe(at, ref, row):
         for i in range(2):
-            row = pl.multiple_of(p_row + 128 * core + 64 * i, 64)
-            probe[i, pl.ds(at, 2)] = ref[pl.ds(row, 64), :].reshape(2, NY, NZ)
-        courant[pl.ds(at, 2)] = scale * ref[c_row : c_row + 64, :].reshape(2, NY, NZ)
+            piece = ref[row + 64 * i : row + 64 * (i + 1), :]
+            probe[i, pl.ds(at, 2)] = piece.reshape(2, NY, NZ)
+
+    def put_courant(at, ref, row, scale):
+        courant[pl.ds(at, 2)] = scale * ref[row : row + 64, :].reshape(2, NY, NZ)
 
     for i in range(2):
         probe[i, pl.ds(8 + 2 * core, 2)] = p[2 * core + i]
         probe[i, pl.ds(8 + 2 * back, 2)] = p_got[2 * core + i]
-    courant[pl.ds(8 + 2 * core, 2)] = cl[0:64, :].reshape(2, NY, NZ)
-    courant[pl.ds(8 + 2 * back, 2)] = cl_got[0:64, :].reshape(2, NY, NZ)
+    courant[pl.ds(8 + 2 * core, 2)] = c_own[...]
+    courant[pl.ds(8 + 2 * back, 2)] = c_got[...]
     base, base_got = 4 + 8 * core, 12 - 8 * core
-    put_planes(base + 2 * core, near, 0, 512, keep_near)
-    put_planes(base + 2 * back, near, 256, 584, keep_near)
-    put_planes(base_got + 2 * back, near_got, 0, 512, keep_near_got)
-    put_planes(base_got + 2 * core, near_got, 256, 584, keep_near_got)
-    put_planes(2 + 14 * core, far, 0, 256, keep_far)
-    put_planes(16 - 14 * core, far_got, 0, 256, keep_far_got)
+    put_probe(base + 2 * core, near_p, 0)
+    put_probe(base + 2 * back, near_p, 128)
+    put_probe(base_got + 2 * back, near_got, 0)
+    put_probe(base_got + 2 * core, near_got, 128)
+    put_probe(2 + 14 * core, far_p, 0)
+    put_probe(16 - 14 * core, far_got, 0)
+    put_courant(base + 2 * core, near, 256, keep_near)
+    put_courant(base + 2 * back, near, 320, keep_near)
+    put_courant(base_got + 2 * back, near_got, 256, keep_near_got)
+    put_courant(base_got + 2 * core, near_got, 320, keep_near_got)
+    put_courant(2 + 14 * core, far, 128, keep_far)
+    put_courant(16 - 14 * core, far_got, 128, keep_far_got)
     zero = jnp.zeros((NY, NZ), F32)
     for e in (0, 1, 18, 19):
         courant[e] = zero
@@ -329,16 +339,18 @@
             send[i, e] = hess[i, 2 * (1 - core) + e]
 
 
-def finish(p, prior, mine, got, out):
+def finish(p, prior, mine, got, out, low, high):
     core = core_of()
     for i in range(2):
         out[2 * core + i] = prior[...] * p[2 * core + i] + mine[i]
         out[2 * (1 - core) + i] = prior[...] * p[2 * (1 - core) + i] + got[i]
-
-
-def gram_part(h0, h1, h2, h3, out, sums):
+    low[...] = out[0:2]
+    high[...] = out[2:4]
+
+
+def gram_part(*refs):
+    *rows, out, sums = refs
     group = lax.axis_index("probe")
-    blocks = (h0, h1, h2, h3)
     start = [lax.rem(group + 4 - b, 4) * 4 for b in range(4)]
     for a in range(4):
         for b in range(a, 4):
@@ -346,8 +358,8 @@
             acc = [None] * len(pairs)
             for plane in range(2):
                 for y in range(0, NY, 8):
-                    left = [blocks[a][i, plane, y : y + 8, :] for i in range(4)]
-                    right = [blocks[b][j, plane, y : y + 8, :] for j in range(4)] if a != b else left
+                    left = [rows[2 * a + i // 2][i % 2, plane, y : y + 8, :] for i in range(4)]
+                    right = [rows[2 * b + j // 2][j % 2, plane, y : y + 8, :] for j in range(4)]
                     for n, (i, j) in enumerate(pairs):
                         prod = left[i] * right[j]
                         prod = prod[:, :128] + prod[:, 128:]
@@ -368,7 +380,8 @@
     out[...] = jnp.broadcast_to(pair[None], out.shape)
 
 
-def whiten(scale, parts, h0, h1, h2, h3, out, work):
+def whiten(scale, parts, *refs):
+    *rows, out, work = refs
     exact = dict(precision=lax.Precision.HIGHEST, preferred_element_type=F32)
     group = lax.axis_index("probe")
     total = jnp.sum(parts[...], axis=0) * scale
@@ -392,20 +405,19 @@
         x = jnp.where(row > k, x - column * ratio, x)
         x = jnp.where(row == k, x * lax.rsqrt(pivot), x)
     work[...] = x
-    rows = work[pl.ds(pl.multiple_of(group * 4, 4), 4), :]
-    rows = jnp.concatenate([rows, rows], axis=0)
+    picked = work[pl.ds(pl.multiple_of(group * 4, 4), 4), :]
+    picked = jnp.concatenate([picked, picked], axis=0)
     block = lax.bitwise_and(group + 4 - lax.shift_right_logical(to_lane, 2), 3)
     source = 16 + block * 4 + lax.bitwise_and(to_lane, 3)
     order = jnp.where(jnp.logical_and(from_lane == source, to_lane < 16), 1.0, 0.0)
-    coef = lax.dot_general(rows, order, NN_DIMS, **exact)
-    blocks = (h0, h1, h2, h3)
+    coef = lax.dot_general(picked, order, NN_DIMS, **exact)
     for r in range(4):
         c = [jnp.broadcast_to(coef[r : r + 1, s : s + 1], (8, NZ)) for s in range(16)]
         for plane in range(2):
             for y in range(0, NY, 8):
                 acc = None
                 for s in range(16):
-                    term = c[s] * blocks[s // 4][s % 4, plane, y : y + 8, :]
+                    term = c[s] * rows[s // 2][s % 2, plane, y : y + 8, :]
                     acc = term if acc is None else acc + term
                 out[r, plane, y : y + 8, :] = acc
 
@@ -421,6 +433,7 @@
     receiver_weight,
 ):
     count = lax.axis_size("space")
+
     def swap(x):
         return lax.ppermute(x, "space", [(i, i ^ 1) for i in range(count)])
 
@@ -429,20 +442,43 @@
         return lax.ppermute(x, "space", pairs)
 
     p = probe_fields
-    lists = [
-        v.reshape(1, -1) for v in (source_cells, source_strength, receiver_cells, receiver_weight)
-    ]
-    cl = call(pack, [(72, NZ)], 5, name="pack")(courant_field, *lists)
-    p_got, cl_got = swap(p), swap(cl)
-    flat = p_got.reshape(256, NZ)
-    near = inward(jnp.concatenate([p.reshape(256, NZ), flat, cl, cl_got], axis=0), 2)
-    far = inward(jnp.concatenate([flat, cl_got, cl[64:72]], axis=0), 4)
-    near_got, far_got = swap(near), swap(far)
+    core = core_of()
+    p_got, c_got = swap(p), swap(courant_field)
+    lists = call(pack, [(LIST, NZ)], 4)(
+        *[
+            v.reshape(1, -1)
+            for v in (source_cells, source_strength, receiver_cells, receiver_weight)
+        ]
+    )
+    lists_got = swap(lists)
+
+    def pair_of(x, side):
+        return lax.dynamic_slice_in_dim(x, 2 * side, 2, 0).reshape(128, NZ)
+
+    c_rows, c_got_rows = courant_field.reshape(64, NZ), c_got.reshape(64, NZ)
+    rest = jnp.concatenate([pair_of(p, core), pair_of(p_got, core)], axis=0)
+    near = inward(
+        jnp.concatenate(
+            [pair_of(p, 1 - core), pair_of(p_got, 1 - core), c_rows, c_got_rows, lists, lists_got],
+            axis=0,
+        ),
+        2,
+    )
+    far = inward(
+        jnp.concatenate(
+            [pair_of(p_got, 1 - core), c_got_rows, lists, lists_got], axis=0
+        ),
+        4,
+    )
+    near_p = inward(rest, 2)
+    far_p = inward(pair_of(p_got, core), 4)
+    near_got = swap(near)
+    far_got = swap(far)
     plane = (NY, NZ)
     drives, wrec, courant, cells = call(
         forward,
         [(7, OWN) + plane, (16, 128), (EXT,) + plane, (LIST, 128)],
-        9,
+        13,
         scratch=[
             pltpu.VMEM((EXT,) + plane, F32),
             pltpu.VMEM((2, EXT) + plane, F32),
@@ -451,10 +487,23 @@
             pltpu.VMEM((EXT,) + plane, F32),
             pltpu.VMEM((5 * LIST, 128), F32),
         ],
-        smem=(8,),
-        name="forward",
+        smem=(12,),
         mib=16,
-    )(p, p_got, cl, cl_got, near, far, near_got, far_got, wavelet)
+    )(
+        p,
+        p_got,
+        courant_field,
+        c_got,
+        lists,
+        lists_got,
+        near,
+        far,
+        near_got,
+        far_got,
+        near_p,
+        far_p,
+        wavelet,
+    )
     all_rec = jnp.concatenate([wrec, swap(wrec)], axis=0)
     rec_near, rec_far = inward(all_rec, 2), inward(all_rec, 4)
     rec_near_got, rec_far_got = swap(rec_near), swap(rec_far)
@@ -469,20 +518,21 @@
             pltpu.VMEM((2, 2, EXT) + plane, F32),
             pltpu.VMEM((2, OWN) + plane, F32),
         ],
-        name="adjoint",
         mib=24,
     )(courant, cells, wrec, rec_near, rec_far, rec_near_got, rec_far_got, drives)
-    hessian = call(finish, [(4, 2) + plane], 4, name="finish")(
+    hessian, low, high = call(finish, [(4, 2) + plane, half, half], 4)(
         probe_fields, prior_weight, mine, swap(send)
     )
     groups = lax.axis_size("probe")
-    others = [
-        lax.ppermute(hessian, "probe", [(i, (i + b) % groups) for i in range(groups)])
-        for b in (1, 2, 3)
-    ]
-    part = call(
-        gram_part, [(count, 2, 128)], 4, scratch=[pltpu.VMEM((256, 128), F32)], name="gram"
-    )(hessian, *others)
+
+    def turn(x, by):
+        return lax.ppermute(x, "probe", [(i, (i + by) % groups) for i in range(groups)])
+
+    low_1, high_3 = turn(low, 1), turn(high, -1)
+    high_1, low_3 = turn(high, 1), turn(low, -1)
+    low_2, high_2 = turn(low_1, 1), turn(high_3, -1)
+    rows = [low, high, low_1, high_1, low_2, high_2, low_3, high_3]
+    part = call(gram_part, [(count, 2, 128)], 8, scratch=[pltpu.VMEM((256, 128), F32)])(*rows)
     parts = lax.all_to_all(part, "space", 0, 0, tiled=True)
     scale = 1.0 / (count * hessian[0].size)
 
@@ -490,8 +540,8 @@
         whiten(scale, *refs)
 
     basis = call(
-        whiten_scaled, [(4, 2) + plane], 5, scratch=[pltpu.VMEM((16, 128), F32)], name="whiten"
-    )(parts, hessian, *others)
+        whiten_scaled, [(4, 2) + plane], 9, scratch=[pltpu.VMEM((16, 128), F32)]
+    )(parts, *rows)
     return (hessian, basis)
 
 

time: 94.6 us -> 90.7 us (0.959)
  waiting for transfers between devices: 35.6 us -> 18.9 us
  starting transfers between devices: 23.3 us -> 38.2 us
  blocking collectives: 16.2 us -> 14.7 us
  other arithmetic: 1.02 us -> 0.03 us
    ppermute x3 -> x6, waiting for transfers between devices: 14.4 us -> 5.94 us  [turn(): lax.ppermute(x, 'probe', [(i, (i + by) % groups) for i in range(groups)])]
    ppermute x8 -> x9, starting transfers between devices: 5.93 us -> 12.3 us  [swap(): return lax.ppermute(x, 'space', [(i, i ^ 1) for i in range(count)])]
    ppermute x4 -> x6, waiting for transfers between devices: 15.4 us -> 9.73 us  [inward(): return lax.ppermute(x, 'space', pairs)]
    ppermute x4 -> x6, starting transfers between devices: 13.8 us -> 19 us  [inward(): return lax.ppermute(x, 'space', pairs)]
    ppermute x3 -> x6, starting transfers between devices: 3.61 us -> 6.82 us  [turn(): lax.ppermute(x, 'probe', [(i, (i + by) % groups) for i in range(groups)])]
    ppermute x8 -> x9, waiting for transfers between devices: 5.79 us -> 3.21 us  [swap(): return lax.ppermute(x, 'space', [(i, i ^ 1) for i in range(count)])]
    all_to_all x1, blocking collectives: 16.2 us -> 14.7 us  [shards(): parts = lax.all_to_all(part, 'space', 0, 0, tiled=True)]
    dynamic_slice x0 -> x2, local copies, waits for them, and re-layouts: none -> 1.01 us  [pair_of(): return lax.dynamic_slice_in_dim(x, 2 * side, 2, 0).reshape(128, NZ)]
  transfers between devices with their start and end apart: 15 -> 21, of which waited for: 11 -> 10; matrix products, arithmetic and copies ran while one was open for 0% -> 1% of each run, Pallas kernels for 0% -> 0%
where the time goes in v3:
time: 90.7 us; the launch traced here: 90.5 us
  starting transfers between devices  38.2 us (42%)
  waiting for transfers between devices  18.9 us (21%)
  Pallas kernels  15.3 us (17%)
  blocking collectives  14.7 us (16%)
  local copies, waits for them, and re-layouts  2.58 us (3%)
    ppermute x6, starting transfers between devices, inward(): return lax.ppermute(x, 'space', pairs)  19 us
    all_to_all x1, blocking collectives, shards(): parts = lax.all_to_all(part, 'space', 0, 0, tiled=True)  14.7 us
    ppermute x9, starting transfers between devices, swap(): return lax.ppermute(x, 'space', [(i, i ^ 1) for i in range(count)])  12.3 us
    ppermute x6, waiting for transfers between devices, inward(): return lax.ppermute(x, 'space', pairs)  9.73 us
    ppermute x6, starting transfers between devices, turn(): lax.ppermute(x, 'probe', [(i, (i + by) % groups) for i in range(groups)])  6.82 us
    pallas_call x1, Pallas kernels, shards(): call(forward, [(7, OWN) + plane, (16, 128), (EXT,) + plane, (LIST, 128)],...  6 us
    ppermute x6, waiting for transfers between devices, turn(): lax.ppermute(x, 'probe', [(i, (i + by) % groups) for i in range(groups)])  5.94 us
    pallas_call x1, Pallas kernels, shards(): call(adjoint, [half, half], 8, scratch=[pltpu.VMEM((7, 2, EXT) + plane, F...  4.29 us
  transfers between devices with their start and end apart: 21, of which 10 were waited for; matrix products, arithmetic and copies ran while one was open for 1% of the time, Pallas kernels for 0%

profile of v3, /device:TPU:1, one launch (start us, length us, event | category | flops | bytes accessed | tf_op | source)
XLA Modules:
  0.0 90.5 jit_solution(11657186318749235098)
XLA Ops:
  0.6 3.3 %collective-permute-start = (f32[4,2,32,256]{3,2,1,0:T(8,128)}, f32[4,2,32,256]{3,2,1,0:T(8,128)S(1)}, u32[]{:S(2)}, u32[]{:S(2)}) collective-permute-start(f32[4,2,32,256]{3,2,1,0:T(8,128)} %p.3), channel_id=1, source_target_pairs={{0,1},{1,0},{2,3},{3,2},{4,5},{5,4},{6,7},{7,6},{8,9},{9,8},{10,11... | collective-permute-start | bytes 786440 | tf_op jit(solution)/shard_map/ppermute | solution.py:438
  3.9 0.6 copy-done.7
  4.7 0.5 collective-permute-start.1
  5.2 1.0 %constant_dynamic-slice_fusion.1 = (f32[2,2,32,256]{3,2,1,0:T(8,128)S(1)}, f32[2,2,32,256]{3,2,1,0:T(8,128)S(1)}) fusion(f32[4,2,32,256]{3,2,1,0:T(8,128)} %p.3, s32[]{:T(128)S(6)} %select_n.5, s32[]{:T(128)S(6)} %select_n.4), kind=kLoop, calls=%fused_computation.11 | loop fusion | bytes 524296 | tf_op jit(solution)/shard_map/dynamic_slice | solution.py:456
  6.3 0.8 copy-done.1
  7.2 6.4 %collective-permute-start.3 = (f32[400,256]{1,0:T(8,128)S(1)}, f32[400,256]{1,0:T(8,128)S(1)}, u32[]{:S(2)}, u32[]{:S(2)}) collective-permute-start(f32[400,256]{1,0:T(8,128)S(1)} %constant_dynamic-update-slice_fusion), channel_id=1, source_target_pairs={{0,2},{1,63},{2,4},{3,1},{4,6},{5,3},{6,8},{7,5},{8,10},{9,7},{10,... | collective-permute-start | bytes 1228808 | tf_op jit(solution)/shard_map/ppermute | solution.py:442
  13.6 1.2 %collective-permute-start.4 = (f32[208,256]{1,0:T(8,128)S(1)}, f32[208,256]{1,0:T(8,128)S(1)}, u32[]{:S(2)}, u32[]{:S(2)}) collective-permute-start(f32[208,256]{1,0:T(8,128)S(1)} %pad_maximum_fusion.1), channel_id=1, source_target_pairs={{0,4},{1,61},{2,6},{3,63},{4,8},{5,1},{6,10},{7,3},{8,12},{9,5},{1... | collective-permute-start | bytes 638984 | tf_op jit(solution)/shard_map/ppermute | solution.py:442
  14.8 5.9 %collective-permute-done.3.near = f32[400,256]{1,0:T(8,128)S(1)} collective-permute-done((f32[400,256]{1,0:T(8,128)S(1)}, f32[400,256]{1,0:T(8,128)S(1)}, u32[]{:S(2)}, u32[]{:S(2)}) %collective-permute-start.3) | collective-permute-done | bytes 409632 | tf_op jit(solution)/shard_map/ppermute | solution.py:442
  20.8 5.3 %collective-permute-start.7 = (f32[256,256]{1,0:T(8,128)S(1)}, f32[256,256]{1,0:T(8,128)S(1)}, u32[]{:S(2)}, u32[]{:S(2)}) collective-permute-start(f32[256,256]{1,0:T(8,128)S(1)} %pad_maximum_fusion), channel_id=1, source_target_pairs={{0,2},{1,63},{2,4},{3,1},{4,6},{5,3},{6,8},{7,5},{8,10},{9,7},{10,... | collective-permute-start | bytes 786440 | tf_op jit(solution)/shard_map/ppermute | solution.py:442
  26.1 3.2 %collective-permute-start.8 = (f32[128,256]{1,0:T(8,128)S(1)}, f32[128,256]{1,0:T(8,128)S(1)}, u32[]{:S(2)}, u32[]{:S(2)}) collective-permute-start(f32[128,256]{1,0:T(8,128)S(1)} %bitcast.21), channel_id=1, source_target_pairs={{0,4},{1,61},{2,6},{3,63},{4,8},{5,1},{6,10},{7,3},{8,12},{9,5},{1... | collective-permute-start | bytes 393224 | tf_op jit(solution)/shard_map/ppermute | solution.py:442
  29.3 2.9 %collective-permute-done.8.far_p = f32[128,256]{1,0:T(8,128)S(1)} collective-permute-done((f32[128,256]{1,0:T(8,128)S(1)}, f32[128,256]{1,0:T(8,128)S(1)}, u32[]{:S(2)}, u32[]{:S(2)}) %collective-permute-start.8) | collective-permute-done | bytes 131104 | tf_op jit(solution)/shard_map/ppermute | solution.py:442
  32.2 6.0 %shard_map.96 = (f32[7,4,32,256]{3,2,1,0:T(8,128)S(1)}, f32[16,128]{1,0:T(8,128)S(1)}, f32[20,32,256]{2,1,0:T(8,128)S(1)}, f32[8,128]{1,0:T(8,128)S(1)}) custom-call(f32[4,2,32,256]{3,2,1,0:T(8,128)S(1)} %copy-done, f32[4,2,32,256]{3,2,1,0:T(8,128)S(1)} %collective-permute-done.p_got, f32[2,32,256]{2,1,0:T(8,128)S(1)} %copy-done.1, ...), custom_call_target="tpu_custom_call" | custom-call | tf_op jit(solution)/shard_map/pallas_call | solution.py:478
  38.2 3.7 %collective-permute-start.9 = (f32[16,128]{1,0:T(8,128)S(1)}, f32[16,128]{1,0:T(8,128)S(1)}, u32[]{:S(2)}, u32[]{:S(2)}) collective-permute-start(f32[16,128]{1,0:T(8,128)S(1)} %get-tuple-element.13.w0), channel_id=1, source_target_pairs={{0,1},{1,0},{2,3},{3,2},{4,5},{5,4},{6,7},{7,6},{8,9},{9,8},{10,11... | collective-permute-start | bytes 24584 | tf_op jit(solution)/shard_map/ppermute | solution.py:438
  41.9 0.8 collective-permute-done.9
  42.7 2.9 %collective-permute-start.11 = (f32[32,128]{1,0:T(8,128)S(1)}, f32[32,128]{1,0:T(8,128)S(1)}, u32[]{:S(2)}, u32[]{:S(2)}) collective-permute-start(f32[32,128]{1,0:T(8,128)S(1)} %constant_dynamic-update-slice_fusion.6), channel_id=1, source_target_pairs={{0,4},{1,61},{2,6},{3,63},{4,8},{5,1},{6,10},{7,3},{8,12},{9,5},{1... | collective-permute-start | bytes 49160 | tf_op jit(solution)/shard_map/ppermute | solution.py:442
  45.6 0.9 collective-permute-done.11.far
  46.5 4.5 %collective-permute-start.13 = (f32[32,128]{1,0:T(8,128)S(1)}, f32[32,128]{1,0:T(8,128)S(1)}, u32[]{:S(2)}, u32[]{:S(2)}) collective-permute-start(f32[32,128]{1,0:T(8,128)S(1)} %collective-permute-done.11.far), channel_id=1, source_target_pairs={{0,1},{1,0},{2,3},{3,2},{4,5},{5,4},{6,7},{7,6},{8,9},{9,8},{10,11... | collective-permute-start | bytes 49160 | tf_op jit(solution)/shard_map/ppermute | solution.py:438
  51.0 0.8 collective-permute-done.13.far_got
  51.9 0.3 collective-permute-done.12.near_got
  52.2 4.3 %shard_map.97 = (f32[2,2,32,256]{3,2,1,0:T(8,128)S(1)}, f32[2,2,32,256]{3,2,1,0:T(8,128)S(1)}) custom-call(f32[20,32,256]{2,1,0:T(8,128)S(1)} %get-tuple-element.11.courant, f32[8,128]{1,0:T(8,128)S(1)} %get-tuple-element.12.cells, f32[16,128]{1,0:T(8,128)S(1)} %get-tuple-element.13.w0, f32[32,128]{1,0:T(8,128)S(1)} %collective-permute-done.10.near, ...), custom_call_target="tpu_custom_call" | custom-call | tf_op jit(solution)/shard_map/pallas_call | solution.py:511
  56.5 0.2 collective-permute-start.14
  56.8 1.2 %collective-permute-done.14.got = f32[2,2,32,256]{3,2,1,0:T(8,128)S(1)} collective-permute-done((f32[2,2,32,256]{3,2,1,0:T(8,128)S(1)}, f32[2,2,32,256]{3,2,1,0:T(8,128)S(1)}, u32[]{:S(2)}, u32[]{:S(2)}) %collective-permute-start.14) | collective-permute-done | bytes 131104 | tf_op jit(solution)/shard_map/ppermute | solution.py:438
  57.9 0.7 shard_map.98
  58.7 1.2 %collective-permute-start.15 = (f32[2,2,32,256]{3,2,1,0:T(8,128)S(1)}, f32[2,2,32,256]{3,2,1,0:T(8,128)S(1)}, u32[]{:S(2)}, u32[]{:S(2)}) collective-permute-start(f32[2,2,32,256]{3,2,1,0:T(8,128)S(1)} %get-tuple-element.18.refs_0_.refs_1_), channel_id=1, source_target_pairs={{0,64},{64,128},{128,192},{192,0},{1,65},{65,129},{129,193},{193,1... | collective-permute-start | bytes 393224 | tf_op jit(solution)/shard_map/ppermute | solution.py:529
  59.9 1.5 %collective-permute-start.18 = (f32[2,2,32,256]{3,2,1,0:T(8,128)S(1)}, f32[2,2,32,256]{3,2,1,0:T(8,128)S(1)}, u32[]{:S(2)}, u32[]{:S(2)}) collective-permute-start(f32[2,2,32,256]{3,2,1,0:T(8,128)S(1)} %get-tuple-element.19.refs_1_.refs_2_), channel_id=1, source_target_pairs={{0,192},{64,0},{128,64},{192,128},{1,193},{65,1},{129,65},{193,129... | collective-permute-start | bytes 393224 | tf_op jit(solution)/shard_map/ppermute | solution.py:529
  61.4 1.3 %collective-permute-start.20 = (f32[2,2,32,256]{3,2,1,0:T(8,128)S(1)}, f32[2,2,32,256]{3,2,1,0:T(8,128)S(1)}, u32[]{:S(2)}, u32[]{:S(2)}) collective-permute-start(f32[2,2,32,256]{3,2,1,0:T(8,128)S(1)} %get-tuple-element.18.refs_0_.refs_1_), channel_id=1, source_target_pairs={{0,192},{64,0},{128,64},{192,128},{1,193},{65,1},{129,65},{193,129... | collective-permute-start | bytes 393224 | tf_op jit(solution)/shard_map/ppermute | solution.py:529
  62.8 2.0 %collective-permute-done.15.refs_2_.refs_3_ = f32[2,2,32,256]{3,2,1,0:T(8,128)S(1)} collective-permute-done((f32[2,2,32,256]{3,2,1,0:T(8,128)S(1)}, f32[2,2,32,256]{3,2,1,0:T(8,128)S(1)}, u32[]{:S(2)}, u32[]{:S(2)}) %collective-permute-start.15) | collective-permute-done | bytes 131104 | tf_op jit(solution)/shard_map/ppermute | solution.py:529
  64.8 2.7 %collective-permute-start.19 = (f32[2,2,32,256]{3,2,1,0:T(8,128)S(1)}, f32[2,2,32,256]{3,2,1,0:T(8,128)S(1)}, u32[]{:S(2)}, u32[]{:S(2)}) collective-permute-start(f32[2,2,32,256]{3,2,1,0:T(8,128)S(1)} %collective-permute-done.18.refs_7_.refs_8_), channel_id=1, source_target_pairs={{0,192},{64,0},{128,64},{192,128},{1,193},{65,1},{129,65},{193,129... | collective-permute-start | bytes 393224 | tf_op jit(solution)/shard_map/ppermute | solution.py:529
  67.7 3.8 %collective-permute-done.17.refs_4_.refs_5_ = f32[2,2,32,256]{3,2,1,0:T(8,128)S(1)} collective-permute-done((f32[2,2,32,256]{3,2,1,0:T(8,128)S(1)}, f32[2,2,32,256]{3,2,1,0:T(8,128)S(1)}, u32[]{:S(2)}, u32[]{:S(2)}) %collective-permute-start.17) | collective-permute-done | bytes 131104 | tf_op jit(solution)/shard_map/ppermute | solution.py:529
  71.5 0.9 shard_map.99
  72.4 14.7 %all_to_all.5.refs_0_ = f32[64,2,128]{2,1,0:T(2,128)S(1)} all-to-all(f32[64,2,128]{2,1,0:T(2,128)S(1)} %shard_map.99), channel_id=1, replica_groups=mesh['probe'=4,'space'=64] {'space'}, dimensions={0} | all-to-all | bytes 131072 | tf_op jit(solution)/shard_map/all_to_all | solution.py:536
  87.1 3.4 %shard_map.100 = f32[4,2,32,256]{3,2,1,0:T(8,128)} custom-call(f32[64,2,128]{2,1,0:T(2,128)S(1)} %all_to_all.5.refs_0_, f32[2,2,32,256]{3,2,1,0:T(8,128)S(1)} %get-tuple-element.18.refs_0_.refs_1_, f32[2,2,32,256]{3,2,1,0:T(8,128)S(1)} %get-tuple-element.19.refs_1_.refs_2_, f32[2,2,32,256]{3,2,1,0:T(8,128)S(1)} %collective-permute-done.15.refs_2_.refs_3_, ...), custom_call_target="tpu_custom_call" | custom-call | tf_op jit(solution)/shard_map/pallas_call | solution.py:542
  (45 shorter events, 0.7 us)
Async XLA Ops:
  0.6 5.6 %collective-permute-start = (f32[4,2,32,256]{3,2,1,0:T(8,128)}, f32[4,2,32,256]{3,2,1,0:T(8,128)S(1)}, u32[]{:S(2)}, u32[]{:S(2)}) collective-permute-start(f32[4,2,32,256]{3,2,1,0:T(8,128)} %p.3), channel_id=1, source_target_pairs={{0,1},{1,0},{2,3},{3,2},{4,5},{5,4},{6,7},{7,6},{8,9},{9,8},{10,11... | collective-permute-start | bytes 786440 | tf_op jit(solution)/shard_map/ppermute | solution.py:438
  3.9 0.7 copy-start.7
  3.9 0.7 copy-start.4
  3.9 0.7 copy-start.5
  3.9 0.7 copy-start.6
  4.6 2.5 %collective-permute-start.2 = (f32[8,256]{1,0:T(8,128)S(1)}, f32[8,256]{1,0:T(8,128)S(1)}, u32[]{:S(2)}, u32[]{:S(2)}) collective-permute-start(f32[8,256]{1,0:T(8,128)S(1)} %shard_map.95.lists), channel_id=1, source_target_pairs={{0,1},{1,0},{2,3},{3,2},{4,5},{5,4},{6,7},{7,6},{8,9},{9,8},{10,11... | collective-permute-start | bytes 24584 | tf_op jit(solution)/shard_map/ppermute | solution.py:438
  4.7 2.4 %collective-permute-start.1 = (f32[2,32,256]{2,1,0:T(8,128)}, f32[2,32,256]{2,1,0:T(8,128)S(1)}, u32[]{:S(2)}, u32[]{:S(2)}) collective-permute-start(f32[2,32,256]{2,1,0:T(8,128)} %c_own.1), channel_id=1, source_target_pairs={{0,1},{1,0},{2,3},{3,2},{4,5},{5,4},{6,7},{7,6},{8,9},{9,8},{10,11... | collective-permute-start | bytes 196616 | tf_op jit(solution)/shard_map/ppermute | solution.py:438
  6.3 0.8 copy-start.1
  7.2 13.6 %collective-permute-start.3 = (f32[400,256]{1,0:T(8,128)S(1)}, f32[400,256]{1,0:T(8,128)S(1)}, u32[]{:S(2)}, u32[]{:S(2)}) collective-permute-start(f32[400,256]{1,0:T(8,128)S(1)} %constant_dynamic-update-slice_fusion), channel_id=1, source_target_pairs={{0,2},{1,63},{2,4},{3,1},{4,6},{5,3},{6,8},{7,5},{8,10},{9,7},{10,... | collective-permute-start | bytes 1228808 | tf_op jit(solution)/shard_map/ppermute | solution.py:442
  13.6 12.5 %collective-permute-start.4 = (f32[208,256]{1,0:T(8,128)S(1)}, f32[208,256]{1,0:T(8,128)S(1)}, u32[]{:S(2)}, u32[]{:S(2)}) collective-permute-start(f32[208,256]{1,0:T(8,128)S(1)} %pad_maximum_fusion.1), channel_id=1, source_target_pairs={{0,4},{1,61},{2,6},{3,63},{4,8},{5,1},{6,10},{7,3},{8,12},{9,5},{1... | collective-permute-start | bytes 638984 | tf_op jit(solution)/shard_map/ppermute | solution.py:442
  20.7 11.5 %collective-permute-start.5 = (f32[400,256]{1,0:T(8,128)S(1)}, f32[400,256]{1,0:T(8,128)S(1)}, u32[]{:S(2)}, u32[]{:S(2)}) collective-permute-start(f32[400,256]{1,0:T(8,128)S(1)} %collective-permute-done.3.near), channel_id=1, source_target_pairs={{0,1},{1,0},{2,3},{3,2},{4,5},{5,4},{6,7},{7,6},{8,9},{9,8},{10,11... | collective-permute-start | bytes 1228808 | tf_op jit(solution)/shard_map/ppermute | solution.py:438
  20.7 11.5 %copy-start = (f32[4,2,32,256]{3,2,1,0:T(8,128)S(1)}, f32[4,2,32,256]{3,2,1,0:T(8,128)}, u32[]{:S(2)}) copy-start(f32[4,2,32,256]{3,2,1,0:T(8,128)} %p.3) | copy-start | bytes 786436
  20.7 11.5 %copy-start.3 = (f32[8]{0:T(128)S(1)}, f32[8]{0:T(128)}, u32[]{:S(2)}) copy-start(f32[8]{0:T(128)} %wavelet.1) | copy-start | bytes 100
  20.8 11.4 %collective-permute-start.7 = (f32[256,256]{1,0:T(8,128)S(1)}, f32[256,256]{1,0:T(8,128)S(1)}, u32[]{:S(2)}, u32[]{:S(2)}) collective-permute-start(f32[256,256]{1,0:T(8,128)S(1)} %pad_maximum_fusion), channel_id=1, source_target_pairs={{0,2},{1,63},{2,4},{3,1},{4,6},{5,3},{6,8},{7,5},{8,10},{9,7},{10,... | collective-permute-start | bytes 786440 | tf_op jit(solution)/shard_map/ppermute | solution.py:442
  26.1 6.1 %collective-permute-start.6 = (f32[208,256]{1,0:T(8,128)S(1)}, f32[208,256]{1,0:T(8,128)S(1)}, u32[]{:S(2)}, u32[]{:S(2)}) collective-permute-start(f32[208,256]{1,0:T(8,128)S(1)} %collective-permute-done.4.far), channel_id=1, source_target_pairs={{0,1},{1,0},{2,3},{3,2},{4,5},{5,4},{6,7},{7,6},{8,9},{9,8},{10,11... | collective-permute-start | bytes 638984 | tf_op jit(solution)/shard_map/ppermute | solution.py:438
  26.1 6.1 %collective-permute-start.8 = (f32[128,256]{1,0:T(8,128)S(1)}, f32[128,256]{1,0:T(8,128)S(1)}, u32[]{:S(2)}, u32[]{:S(2)}) collective-permute-start(f32[128,256]{1,0:T(8,128)S(1)} %bitcast.21), channel_id=1, source_target_pairs={{0,4},{1,61},{2,6},{3,63},{4,8},{5,1},{6,10},{7,3},{8,12},{9,5},{1... | collective-permute-start | bytes 393224 | tf_op jit(solution)/shard_map/ppermute | solution.py:442
  38.2 4.5 %collective-permute-start.9 = (f32[16,128]{1,0:T(8,128)S(1)}, f32[16,128]{1,0:T(8,128)S(1)}, u32[]{:S(2)}, u32[]{:S(2)}) collective-permute-start(f32[16,128]{1,0:T(8,128)S(1)} %get-tuple-element.13.w0), channel_id=1, source_target_pairs={{0,1},{1,0},{2,3},{3,2},{4,5},{5,4},{6,7},{7,6},{8,9},{9,8},{10,11... | collective-permute-start | bytes 24584 | tf_op jit(solution)/shard_map/ppermute | solution.py:438
  42.7 3.8 %collective-permute-start.11 = (f32[32,128]{1,0:T(8,128)S(1)}, f32[32,128]{1,0:T(8,128)S(1)}, u32[]{:S(2)}, u32[]{:S(2)}) collective-permute-start(f32[32,128]{1,0:T(8,128)S(1)} %constant_dynamic-update-slice_fusion.6), channel_id=1, source_target_pairs={{0,4},{1,61},{2,6},{3,63},{4,8},{5,1},{6,10},{7,3},{8,12},{9,5},{1... | collective-permute-start | bytes 49160 | tf_op jit(solution)/shard_map/ppermute | solution.py:442
  45.6 5.4 %collective-permute-start.10 = (f32[32,128]{1,0:T(8,128)S(1)}, f32[32,128]{1,0:T(8,128)S(1)}, u32[]{:S(2)}, u32[]{:S(2)}) collective-permute-start(f32[32,128]{1,0:T(8,128)S(1)} %constant_dynamic-update-slice_fusion.6), channel_id=1, source_target_pairs={{0,2},{1,63},{2,4},{3,1},{4,6},{5,3},{6,8},{7,5},{8,10},{9,7},{10,... | collective-permute-start | bytes 49160 | tf_op jit(solution)/shard_map/ppermute | solution.py:442
  46.5 5.4 %collective-permute-start.13 = (f32[32,128]{1,0:T(8,128)S(1)}, f32[32,128]{1,0:T(8,128)S(1)}, u32[]{:S(2)}, u32[]{:S(2)}) collective-permute-start(f32[32,128]{1,0:T(8,128)S(1)} %collective-permute-done.11.far), channel_id=1, source_target_pairs={{0,1},{1,0},{2,3},{3,2},{4,5},{5,4},{6,7},{7,6},{8,9},{9,8},{10,11... | collective-permute-start | bytes 49160 | tf_op jit(solution)/shard_map/ppermute | solution.py:438
  51.0 1.2 %collective-permute-start.12 = (f32[32,128]{1,0:T(8,128)S(1)}, f32[32,128]{1,0:T(8,128)S(1)}, u32[]{:S(2)}, u32[]{:S(2)}) collective-permute-start(f32[32,128]{1,0:T(8,128)S(1)} %collective-permute-done.10.near), channel_id=1, source_target_pairs={{0,1},{1,0},{2,3},{3,2},{4,5},{5,4},{6,7},{7,6},{8,9},{9,8},{10,11... | collective-permute-start | bytes 49160 | tf_op jit(solution)/shard_map/ppermute | solution.py:438
  52.2 5.7 %copy-start.2 = (f32[2,32,256]{2,1,0:T(8,128)S(1)}, f32[2,32,256]{2,1,0:T(8,128)}, u32[]{:S(2)}) copy-start(f32[2,32,256]{2,1,0:T(8,128)} %prior.1) | copy-start | bytes 196612
  56.5 1.4 %collective-permute-start.14 = (f32[2,2,32,256]{3,2,1,0:T(8,128)S(1)}, f32[2,2,32,256]{3,2,1,0:T(8,128)S(1)}, u32[]{:S(2)}, u32[]{:S(2)}) collective-permute-start(f32[2,2,32,256]{3,2,1,0:T(8,128)S(1)} %get-tuple-element.16), channel_id=1, source_target_pairs={{0,1},{1,0},{2,3},{3,2},{4,5},{5,4},{6,7},{7,6},{8,9},{9,8},{10,11... | collective-permute-start | bytes 393224 | tf_op jit(solution)/shard_map/ppermute | solution.py:438
  58.7 6.1 %collective-permute-start.15 = (f32[2,2,32,256]{3,2,1,0:T(8,128)S(1)}, f32[2,2,32,256]{3,2,1,0:T(8,128)S(1)}, u32[]{:S(2)}, u32[]{:S(2)}) collective-permute-start(f32[2,2,32,256]{3,2,1,0:T(8,128)S(1)} %get-tuple-element.18.refs_0_.refs_1_), channel_id=1, source_target_pairs={{0,64},{64,128},{128,192},{192,0},{1,65},{65,129},{129,193},{193,1... | collective-permute-start | bytes 393224 | tf_op jit(solution)/shard_map/ppermute | solution.py:529
  59.9 4.9 %collective-permute-start.18 = (f32[2,2,32,256]{3,2,1,0:T(8,128)S(1)}, f32[2,2,32,256]{3,2,1,0:T(8,128)S(1)}, u32[]{:S(2)}, u32[]{:S(2)}) collective-permute-start(f32[2,2,32,256]{3,2,1,0:T(8,128)S(1)} %get-tuple-element.19.refs_1_.refs_2_), channel_id=1, source_target_pairs={{0,192},{64,0},{128,64},{192,128},{1,193},{65,1},{129,65},{193,129... | collective-permute-start | bytes 393224 | tf_op jit(solution)/shard_map/ppermute | solution.py:529
  61.4 6.1 %collective-permute-start.20 = (f32[2,2,32,256]{3,2,1,0:T(8,128)S(1)}, f32[2,2,32,256]{3,2,1,0:T(8,128)S(1)}, u32[]{:S(2)}, u32[]{:S(2)}) collective-permute-start(f32[2,2,32,256]{3,2,1,0:T(8,128)S(1)} %get-tuple-element.18.refs_0_.refs_1_), channel_id=1, source_target_pairs={{0,192},{64,0},{128,64},{192,128},{1,193},{65,1},{129,65},{193,129... | collective-permute-start | bytes 393224 | tf_op jit(solution)/shard_map/ppermute | solution.py:529
  62.6 5.0 %collective-permute-start.16 = (f32[2,2,32,256]{3,2,1,0:T(8,128)S(1)}, f32[2,2,32,256]{3,2,1,0:T(8,128)S(1)}, u32[]{:S(2)}, u32[]{:S(2)}) collective-permute-start(f32[2,2,32,256]{3,2,1,0:T(8,128)S(1)} %get-tuple-element.19.refs_1_.refs_2_), channel_id=1, source_target_pairs={{0,64},{64,128},{128,192},{192,0},{1,65},{65,129},{129,193},{193,1... | collective-permute-start | bytes 393224 | tf_op jit(solution)/shard_map/ppermute | solution.py:529
  64.8 6.6 %collective-permute-start.17 = (f32[2,2,32,256]{3,2,1,0:T(8,128)S(1)}, f32[2,2,32,256]{3,2,1,0:T(8,128)S(1)}, u32[]{:S(2)}, u32[]{:S(2)}) collective-permute-start(f32[2,2,32,256]{3,2,1,0:T(8,128)S(1)} %collective-permute-done.15.refs_2_.refs_3_), channel_id=1, source_target_pairs={{0,64},{64,128},{128,192},{192,0},{1,65},{65,129},{129,193},{193,1... | collective-permute-start | bytes 393224 | tf_op jit(solution)/shard_map/ppermute | solution.py:529
  64.8 6.6 %collective-permute-start.19 = (f32[2,2,32,256]{3,2,1,0:T(8,128)S(1)}, f32[2,2,32,256]{3,2,1,0:T(8,128)S(1)}, u32[]{:S(2)}, u32[]{:S(2)}) collective-permute-start(f32[2,2,32,256]{3,2,1,0:T(8,128)S(1)} %collective-permute-done.18.refs_7_.refs_8_), channel_id=1, source_target_pairs={{0,192},{64,0},{128,64},{192,128},{1,193},{65,1},{129,65},{193,129... | collective-permute-start | bytes 393224 | tf_op jit(solution)/shard_map/ppermute | solution.py:529

commit v4 on v3

--- a/solution.py
+++ b/solution.py
@@ -398,11 +398,17 @@
     select = jnp.where(lax.bitwise_and(from_lane, 15) == to_lane, 1.0, 0.0)
     x = lax.dot_general(spread, select, NN_DIMS, **exact)
     x = x + jnp.where(lane == row + 16, 1.0, 0.0)
+    columns = [jnp.broadcast_to(x[:, k : k + 1], (16, 128)) for k in range(16)]
+
+    def spread_row(v, k):
+        return jnp.broadcast_to(v[k : k + 1], (16, 128))
+
     for k in range(16):
-        column = jnp.broadcast_to(x[:, k : k + 1], (16, 128))
-        pivot = jnp.broadcast_to(column[k : k + 1], (16, 128))
-        ratio = jnp.broadcast_to(x[k : k + 1], (16, 128)) / pivot
-        x = jnp.where(row > k, x - column * ratio, x)
+        pivot = spread_row(columns[k], k)
+        ratio = jnp.where(row > k, columns[k] / pivot, 0.0)
+        for j in range(k + 1, 16):
+            columns[j] = columns[j] - ratio * spread_row(columns[k], j)
+        x = x - ratio * spread_row(x, k)
         x = jnp.where(row == k, x * lax.rsqrt(pivot), x)
     work[...] = x
     picked = work[pl.ds(pl.multiple_of(group * 4, 4), 4), :]
@@ -505,8 +511,10 @@
         wavelet,
     )
     all_rec = jnp.concatenate([wrec, swap(wrec)], axis=0)
-    rec_near, rec_far = inward(all_rec, 2), inward(all_rec, 4)
-    rec_near_got, rec_far_got = swap(rec_near), swap(rec_far)
+    rec_near = inward(all_rec, 2)
+    rec_far = inward(all_rec, 4)
+    rec_near_got = swap(rec_near)
+    rec_far_got = swap(rec_far)
     half = (2, 2) + plane
     mine, send = call(
         adjoint,

time: 90.7 us -> 89.1 us (0.982)
  Pallas kernels: 15.3 us -> 13.8 us
    pallas_call x1, Pallas kernels: 3.36 us -> 1.81 us  [shards(): call(whiten_scaled, [(4, 2) + plane], 9, scratch=[pltpu.VMEM((16, 128), F...]
where the time goes in v4:
time: 89.1 us; the launch traced here: 88.9 us
  starting transfers between devices  38.2 us (43%)
  waiting for transfers between devices  18.9 us (21%)
  blocking collectives  14.7 us (16%)
  Pallas kernels  13.8 us (15%)
  local copies, waits for them, and re-layouts  2.58 us (3%)
    ppermute x6, starting transfers between devices, inward(): return lax.ppermute(x, 'space', pairs)  19 us
    all_to_all x1, blocking collectives, shards(): parts = lax.all_to_all(part, 'space', 0, 0, tiled=True)  14.7 us
    ppermute x9, starting transfers between devices, swap(): return lax.ppermute(x, 'space', [(i, i ^ 1) for i in range(count)])  12.3 us
    ppermute x6, waiting for transfers between devices, inward(): return lax.ppermute(x, 'space', pairs)  9.73 us
    ppermute x6, starting transfers between devices, turn(): lax.ppermute(x, 'probe', [(i, (i + by) % groups) for i in range(groups)])  6.82 us
    pallas_call x1, Pallas kernels, shards(): call(forward, [(7, OWN) + plane, (16, 128), (EXT,) + plane, (LIST, 128)],...  6 us
    ppermute x6, waiting for transfers between devices, turn(): lax.ppermute(x, 'probe', [(i, (i + by) % groups) for i in range(groups)])  5.94 us
    pallas_call x1, Pallas kernels, shards(): call(adjoint, [half, half], 8, scratch=[pltpu.VMEM((7, 2, EXT) + plane, F...  4.29 us
  transfers between devices with their start and end apart: 21, of which 10 were waited for; matrix products, arithmetic and copies ran while one was open for 1% of the time, Pallas kernels for 0%

profile of v4, /device:TPU:1, one launch (start us, length us, event | category | flops | bytes accessed | tf_op | source)
XLA Modules:
  0.0 88.9 jit_solution(7421757146541436535)
XLA Ops:
  0.6 3.3 %collective-permute-start = (f32[4,2,32,256]{3,2,1,0:T(8,128)}, f32[4,2,32,256]{3,2,1,0:T(8,128)S(1)}, u32[]{:S(2)}, u32[]{:S(2)}) collective-permute-start(f32[4,2,32,256]{3,2,1,0:T(8,128)} %p.3), channel_id=1, source_target_pairs={{0,1},{1,0},{2,3},{3,2},{4,5},{5,4},{6,7},{7,6},{8,9},{9,8},{10,11... | collective-permute-start | bytes 786440 | tf_op jit(solution)/shard_map/ppermute | solution.py:444
  3.9 0.6 copy-done.7
  4.7 0.5 collective-permute-start.1
  5.2 1.0 %constant_dynamic-slice_fusion.1 = (f32[2,2,32,256]{3,2,1,0:T(8,128)S(1)}, f32[2,2,32,256]{3,2,1,0:T(8,128)S(1)}) fusion(f32[4,2,32,256]{3,2,1,0:T(8,128)} %p.3, s32[]{:T(128)S(6)} %select_n.5, s32[]{:T(128)S(6)} %select_n.4), kind=kLoop, calls=%fused_computation.11 | loop fusion | bytes 524296 | tf_op jit(solution)/shard_map/dynamic_slice | solution.py:462
  6.3 0.8 copy-done.1
  7.2 6.4 %collective-permute-start.3 = (f32[400,256]{1,0:T(8,128)S(1)}, f32[400,256]{1,0:T(8,128)S(1)}, u32[]{:S(2)}, u32[]{:S(2)}) collective-permute-start(f32[400,256]{1,0:T(8,128)S(1)} %constant_dynamic-update-slice_fusion), channel_id=1, source_target_pairs={{0,2},{1,63},{2,4},{3,1},{4,6},{5,3},{6,8},{7,5},{8,10},{9,7},{10,... | collective-permute-start | bytes 1228808 | tf_op jit(solution)/shard_map/ppermute | solution.py:448
  13.6 1.2 %collective-permute-start.4 = (f32[208,256]{1,0:T(8,128)S(1)}, f32[208,256]{1,0:T(8,128)S(1)}, u32[]{:S(2)}, u32[]{:S(2)}) collective-permute-start(f32[208,256]{1,0:T(8,128)S(1)} %pad_maximum_fusion.1), channel_id=1, source_target_pairs={{0,4},{1,61},{2,6},{3,63},{4,8},{5,1},{6,10},{7,3},{8,12},{9,5},{1... | collective-permute-start | bytes 638984 | tf_op jit(solution)/shard_map/ppermute | solution.py:448
  14.8 5.9 %collective-permute-done.3.near = f32[400,256]{1,0:T(8,128)S(1)} collective-permute-done((f32[400,256]{1,0:T(8,128)S(1)}, f32[400,256]{1,0:T(8,128)S(1)}, u32[]{:S(2)}, u32[]{:S(2)}) %collective-permute-start.3) | collective-permute-done | bytes 409632 | tf_op jit(solution)/shard_map/ppermute | solution.py:448
  20.8 5.3 %collective-permute-start.7 = (f32[256,256]{1,0:T(8,128)S(1)}, f32[256,256]{1,0:T(8,128)S(1)}, u32[]{:S(2)}, u32[]{:S(2)}) collective-permute-start(f32[256,256]{1,0:T(8,128)S(1)} %pad_maximum_fusion), channel_id=1, source_target_pairs={{0,2},{1,63},{2,4},{3,1},{4,6},{5,3},{6,8},{7,5},{8,10},{9,7},{10,... | collective-permute-start | bytes 786440 | tf_op jit(solution)/shard_map/ppermute | solution.py:448
  26.1 3.2 %collective-permute-start.8 = (f32[128,256]{1,0:T(8,128)S(1)}, f32[128,256]{1,0:T(8,128)S(1)}, u32[]{:S(2)}, u32[]{:S(2)}) collective-permute-start(f32[128,256]{1,0:T(8,128)S(1)} %bitcast.21), channel_id=1, source_target_pairs={{0,4},{1,61},{2,6},{3,63},{4,8},{5,1},{6,10},{7,3},{8,12},{9,5},{1... | collective-permute-start | bytes 393224 | tf_op jit(solution)/shard_map/ppermute | solution.py:448
  29.3 2.9 %collective-permute-done.8.far_p = f32[128,256]{1,0:T(8,128)S(1)} collective-permute-done((f32[128,256]{1,0:T(8,128)S(1)}, f32[128,256]{1,0:T(8,128)S(1)}, u32[]{:S(2)}, u32[]{:S(2)}) %collective-permute-start.8) | collective-permute-done | bytes 131104 | tf_op jit(solution)/shard_map/ppermute | solution.py:448
  32.2 6.0 %shard_map.96 = (f32[7,4,32,256]{3,2,1,0:T(8,128)S(1)}, f32[16,128]{1,0:T(8,128)S(1)}, f32[20,32,256]{2,1,0:T(8,128)S(1)}, f32[8,128]{1,0:T(8,128)S(1)}) custom-call(f32[4,2,32,256]{3,2,1,0:T(8,128)S(1)} %copy-done, f32[4,2,32,256]{3,2,1,0:T(8,128)S(1)} %collective-permute-done.p_got, f32[2,32,256]{2,1,0:T(8,128)S(1)} %copy-done.1, ...), custom_call_target="tpu_custom_call" | custom-call | tf_op jit(solution)/shard_map/pallas_call | solution.py:484
  38.2 3.7 %collective-permute-start.9 = (f32[16,128]{1,0:T(8,128)S(1)}, f32[16,128]{1,0:T(8,128)S(1)}, u32[]{:S(2)}, u32[]{:S(2)}) collective-permute-start(f32[16,128]{1,0:T(8,128)S(1)} %get-tuple-element.13.w0), channel_id=1, source_target_pairs={{0,1},{1,0},{2,3},{3,2},{4,5},{5,4},{6,7},{7,6},{8,9},{9,8},{10,11... | collective-permute-start | bytes 24584 | tf_op jit(solution)/shard_map/ppermute | solution.py:444
  41.9 0.8 collective-permute-done.9
  42.7 2.9 %collective-permute-start.11 = (f32[32,128]{1,0:T(8,128)S(1)}, f32[32,128]{1,0:T(8,128)S(1)}, u32[]{:S(2)}, u32[]{:S(2)}) collective-permute-start(f32[32,128]{1,0:T(8,128)S(1)} %constant_dynamic-update-slice_fusion.6), channel_id=1, source_target_pairs={{0,4},{1,61},{2,6},{3,63},{4,8},{5,1},{6,10},{7,3},{8,12},{9,5},{1... | collective-permute-start | bytes 49160 | tf_op jit(solution)/shard_map/ppermute | solution.py:448
  45.6 0.9 collective-permute-done.11.far
  46.5 4.5 %collective-permute-start.13 = (f32[32,128]{1,0:T(8,128)S(1)}, f32[32,128]{1,0:T(8,128)S(1)}, u32[]{:S(2)}, u32[]{:S(2)}) collective-permute-start(f32[32,128]{1,0:T(8,128)S(1)} %collective-permute-done.11.far), channel_id=1, source_target_pairs={{0,1},{1,0},{2,3},{3,2},{4,5},{5,4},{6,7},{7,6},{8,9},{9,8},{10,11... | collective-permute-start | bytes 49160 | tf_op jit(solution)/shard_map/ppermute | solution.py:444
  51.0 0.8 collective-permute-done.13.far_got
  51.9 0.3 collective-permute-done.12.near_got
  52.2 4.3 %shard_map.97 = (f32[2,2,32,256]{3,2,1,0:T(8,128)S(1)}, f32[2,2,32,256]{3,2,1,0:T(8,128)S(1)}) custom-call(f32[20,32,256]{2,1,0:T(8,128)S(1)} %get-tuple-element.11.courant, f32[8,128]{1,0:T(8,128)S(1)} %get-tuple-element.12.cells, f32[16,128]{1,0:T(8,128)S(1)} %get-tuple-element.13.w0, f32[32,128]{1,0:T(8,128)S(1)} %collective-permute-done.10.near, ...), custom_call_target="tpu_custom_call" | custom-call | tf_op jit(solution)/shard_map/pallas_call | solution.py:519
  56.5 0.2 collective-permute-start.14
  56.8 1.2 %collective-permute-done.14.got = f32[2,2,32,256]{3,2,1,0:T(8,128)S(1)} collective-permute-done((f32[2,2,32,256]{3,2,1,0:T(8,128)S(1)}, f32[2,2,32,256]{3,2,1,0:T(8,128)S(1)}, u32[]{:S(2)}, u32[]{:S(2)}) %collective-permute-start.14) | collective-permute-done | bytes 131104 | tf_op jit(solution)/shard_map/ppermute | solution.py:444
  57.9 0.7 shard_map.98
  58.7 1.2 %collective-permute-start.15 = (f32[2,2,32,256]{3,2,1,0:T(8,128)S(1)}, f32[2,2,32,256]{3,2,1,0:T(8,128)S(1)}, u32[]{:S(2)}, u32[]{:S(2)}) collective-permute-start(f32[2,2,32,256]{3,2,1,0:T(8,128)S(1)} %get-tuple-element.18.refs_0_.refs_1_), channel_id=1, source_target_pairs={{0,64},{64,128},{128,192},{192,0},{1,65},{65,129},{129,193},{193,1... | collective-permute-start | bytes 393224 | tf_op jit(solution)/shard_map/ppermute | solution.py:537
  59.9 1.5 %collective-permute-start.18 = (f32[2,2,32,256]{3,2,1,0:T(8,128)S(1)}, f32[2,2,32,256]{3,2,1,0:T(8,128)S(1)}, u32[]{:S(2)}, u32[]{:S(2)}) collective-permute-start(f32[2,2,32,256]{3,2,1,0:T(8,128)S(1)} %get-tuple-element.19.refs_1_.refs_2_), channel_id=1, source_target_pairs={{0,192},{64,0},{128,64},{192,128},{1,193},{65,1},{129,65},{193,129... | collective-permute-start | bytes 393224 | tf_op jit(solution)/shard_map/ppermute | solution.py:537
  61.4 1.3 %collective-permute-start.20 = (f32[2,2,32,256]{3,2,1,0:T(8,128)S(1)}, f32[2,2,32,256]{3,2,1,0:T(8,128)S(1)}, u32[]{:S(2)}, u32[]{:S(2)}) collective-permute-start(f32[2,2,32,256]{3,2,1,0:T(8,128)S(1)} %get-tuple-element.18.refs_0_.refs_1_), channel_id=1, source_target_pairs={{0,192},{64,0},{128,64},{192,128},{1,193},{65,1},{129,65},{193,129... | collective-permute-start | bytes 393224 | tf_op jit(solution)/shard_map/ppermute | solution.py:537
  62.8 2.0 %collective-permute-done.15.refs_2_.refs_3_ = f32[2,2,32,256]{3,2,1,0:T(8,128)S(1)} collective-permute-done((f32[2,2,32,256]{3,2,1,0:T(8,128)S(1)}, f32[2,2,32,256]{3,2,1,0:T(8,128)S(1)}, u32[]{:S(2)}, u32[]{:S(2)}) %collective-permute-start.15) | collective-permute-done | bytes 131104 | tf_op jit(solution)/shard_map/ppermute | solution.py:537
  64.8 2.7 %collective-permute-start.19 = (f32[2,2,32,256]{3,2,1,0:T(8,128)S(1)}, f32[2,2,32,256]{3,2,1,0:T(8,128)S(1)}, u32[]{:S(2)}, u32[]{:S(2)}) collective-permute-start(f32[2,2,32,256]{3,2,1,0:T(8,128)S(1)} %collective-permute-done.18.refs_7_.refs_8_), channel_id=1, source_target_pairs={{0,192},{64,0},{128,64},{192,128},{1,193},{65,1},{129,65},{193,129... | collective-permute-start | bytes 393224 | tf_op jit(solution)/shard_map/ppermute | solution.py:537
  67.7 3.8 %collective-permute-done.17.refs_4_.refs_5_ = f32[2,2,32,256]{3,2,1,0:T(8,128)S(1)} collective-permute-done((f32[2,2,32,256]{3,2,1,0:T(8,128)S(1)}, f32[2,2,32,256]{3,2,1,0:T(8,128)S(1)}, u32[]{:S(2)}, u32[]{:S(2)}) %collective-permute-start.17) | collective-permute-done | bytes 131104 | tf_op jit(solution)/shard_map/ppermute | solution.py:537
  71.5 0.9 %shard_map.99 = f32[64,2,128]{2,1,0:T(2,128)S(1)} custom-call(f32[2,2,32,256]{3,2,1,0:T(8,128)S(1)} %get-tuple-element.18.refs_0_.refs_1_, f32[2,2,32,256]{3,2,1,0:T(8,128)S(1)} %get-tuple-element.19.refs_1_.refs_2_, f32[2,2,32,256]{3,2,1,0:T(8,128)S(1)} %collective-permute-done.15.refs_2_.refs_3_, ...), custom_call_target="tpu_custom_call" | custom-call | tf_op jit(solution)/shard_map/pallas_call | solution.py:543
  72.4 14.7 %all_to_all.5.refs_0_ = f32[64,2,128]{2,1,0:T(2,128)S(1)} all-to-all(f32[64,2,128]{2,1,0:T(2,128)S(1)} %shard_map.99), channel_id=1, replica_groups=mesh['probe'=4,'space'=64] {'space'}, dimensions={0} | all-to-all | bytes 131072 | tf_op jit(solution)/shard_map/all_to_all | solution.py:544
  87.1 1.8 %shard_map.100 = f32[4,2,32,256]{3,2,1,0:T(8,128)} custom-call(f32[64,2,128]{2,1,0:T(2,128)S(1)} %all_to_all.5.refs_0_, f32[2,2,32,256]{3,2,1,0:T(8,128)S(1)} %get-tuple-element.18.refs_0_.refs_1_, f32[2,2,32,256]{3,2,1,0:T(8,128)S(1)} %get-tuple-element.19.refs_1_.refs_2_, f32[2,2,32,256]{3,2,1,0:T(8,128)S(1)} %collective-permute-done.15.refs_2_.refs_3_, ...), custom_call_target="tpu_custom_call" | custom-call | tf_op jit(solution)/shard_map/pallas_call | solution.py:550
  (45 shorter events, 0.7 us)
Async XLA Ops:
  0.6 5.6 %collective-permute-start = (f32[4,2,32,256]{3,2,1,0:T(8,128)}, f32[4,2,32,256]{3,2,1,0:T(8,128)S(1)}, u32[]{:S(2)}, u32[]{:S(2)}) collective-permute-start(f32[4,2,32,256]{3,2,1,0:T(8,128)} %p.3), channel_id=1, source_target_pairs={{0,1},{1,0},{2,3},{3,2},{4,5},{5,4},{6,7},{7,6},{8,9},{9,8},{10,11... | collective-permute-start | bytes 786440 | tf_op jit(solution)/shard_map/ppermute | solution.py:444
  3.9 0.7 copy-start.7
  3.9 0.7 copy-start.4
  3.9 0.7 copy-start.5
  3.9 0.7 copy-start.6
  4.6 2.5 %collective-permute-start.2 = (f32[8,256]{1,0:T(8,128)S(1)}, f32[8,256]{1,0:T(8,128)S(1)}, u32[]{:S(2)}, u32[]{:S(2)}) collective-permute-start(f32[8,256]{1,0:T(8,128)S(1)} %shard_map.95.lists), channel_id=1, source_target_pairs={{0,1},{1,0},{2,3},{3,2},{4,5},{5,4},{6,7},{7,6},{8,9},{9,8},{10,11... | collective-permute-start | bytes 24584 | tf_op jit(solution)/shard_map/ppermute | solution.py:444
  4.7 2.4 %collective-permute-start.1 = (f32[2,32,256]{2,1,0:T(8,128)}, f32[2,32,256]{2,1,0:T(8,128)S(1)}, u32[]{:S(2)}, u32[]{:S(2)}) collective-permute-start(f32[2,32,256]{2,1,0:T(8,128)} %c_own.1), channel_id=1, source_target_pairs={{0,1},{1,0},{2,3},{3,2},{4,5},{5,4},{6,7},{7,6},{8,9},{9,8},{10,11... | collective-permute-start | bytes 196616 | tf_op jit(solution)/shard_map/ppermute | solution.py:444
  6.3 0.8 copy-start.1
  7.2 13.6 %collective-permute-start.3 = (f32[400,256]{1,0:T(8,128)S(1)}, f32[400,256]{1,0:T(8,128)S(1)}, u32[]{:S(2)}, u32[]{:S(2)}) collective-permute-start(f32[400,256]{1,0:T(8,128)S(1)} %constant_dynamic-update-slice_fusion), channel_id=1, source_target_pairs={{0,2},{1,63},{2,4},{3,1},{4,6},{5,3},{6,8},{7,5},{8,10},{9,7},{10,... | collective-permute-start | bytes 1228808 | tf_op jit(solution)/shard_map/ppermute | solution.py:448
  13.6 12.5 %collective-permute-start.4 = (f32[208,256]{1,0:T(8,128)S(1)}, f32[208,256]{1,0:T(8,128)S(1)}, u32[]{:S(2)}, u32[]{:S(2)}) collective-permute-start(f32[208,256]{1,0:T(8,128)S(1)} %pad_maximum_fusion.1), channel_id=1, source_target_pairs={{0,4},{1,61},{2,6},{3,63},{4,8},{5,1},{6,10},{7,3},{8,12},{9,5},{1... | collective-permute-start | bytes 638984 | tf_op jit(solution)/shard_map/ppermute | solution.py:448
  20.7 11.5 %collective-permute-start.5 = (f32[400,256]{1,0:T(8,128)S(1)}, f32[400,256]{1,0:T(8,128)S(1)}, u32[]{:S(2)}, u32[]{:S(2)}) collective-permute-start(f32[400,256]{1,0:T(8,128)S(1)} %collective-permute-done.3.near), channel_id=1, source_target_pairs={{0,1},{1,0},{2,3},{3,2},{4,5},{5,4},{6,7},{7,6},{8,9},{9,8},{10,11... | collective-permute-start | bytes 1228808 | tf_op jit(solution)/shard_map/ppermute | solution.py:444
  20.7 11.5 %copy-start = (f32[4,2,32,256]{3,2,1,0:T(8,128)S(1)}, f32[4,2,32,256]{3,2,1,0:T(8,128)}, u32[]{:S(2)}) copy-start(f32[4,2,32,256]{3,2,1,0:T(8,128)} %p.3) | copy-start | bytes 786436
  20.7 11.5 %copy-start.3 = (f32[8]{0:T(128)S(1)}, f32[8]{0:T(128)}, u32[]{:S(2)}) copy-start(f32[8]{0:T(128)} %wavelet.1) | copy-start | bytes 100
  20.8 11.4 %collective-permute-start.7 = (f32[256,256]{1,0:T(8,128)S(1)}, f32[256,256]{1,0:T(8,128)S(1)}, u32[]{:S(2)}, u32[]{:S(2)}) collective-permute-start(f32[256,256]{1,0:T(8,128)S(1)} %pad_maximum_fusion), channel_id=1, source_target_pairs={{0,2},{1,63},{2,4},{3,1},{4,6},{5,3},{6,8},{7,5},{8,10},{9,7},{10,... | collective-permute-start | bytes 786440 | tf_op jit(solution)/shard_map/ppermute | solution.py:448
  26.1 6.1 %collective-permute-start.6 = (f32[208,256]{1,0:T(8,128)S(1)}, f32[208,256]{1,0:T(8,128)S(1)}, u32[]{:S(2)}, u32[]{:S(2)}) collective-permute-start(f32[208,256]{1,0:T(8,128)S(1)} %collective-permute-done.4.far), channel_id=1, source_target_pairs={{0,1},{1,0},{2,3},{3,2},{4,5},{5,4},{6,7},{7,6},{8,9},{9,8},{10,11... | collective-permute-start | bytes 638984 | tf_op jit(solution)/shard_map/ppermute | solution.py:444
  26.1 6.1 %collective-permute-start.8 = (f32[128,256]{1,0:T(8,128)S(1)}, f32[128,256]{1,0:T(8,128)S(1)}, u32[]{:S(2)}, u32[]{:S(2)}) collective-permute-start(f32[128,256]{1,0:T(8,128)S(1)} %bitcast.21), channel_id=1, source_target_pairs={{0,4},{1,61},{2,6},{3,63},{4,8},{5,1},{6,10},{7,3},{8,12},{9,5},{1... | collective-permute-start | bytes 393224 | tf_op jit(solution)/shard_map/ppermute | solution.py:448
  38.2 4.5 %collective-permute-start.9 = (f32[16,128]{1,0:T(8,128)S(1)}, f32[16,128]{1,0:T(8,128)S(1)}, u32[]{:S(2)}, u32[]{:S(2)}) collective-permute-start(f32[16,128]{1,0:T(8,128)S(1)} %get-tuple-element.13.w0), channel_id=1, source_target_pairs={{0,1},{1,0},{2,3},{3,2},{4,5},{5,4},{6,7},{7,6},{8,9},{9,8},{10,11... | collective-permute-start | bytes 24584 | tf_op jit(solution)/shard_map/ppermute | solution.py:444
  42.7 3.8 %collective-permute-start.11 = (f32[32,128]{1,0:T(8,128)S(1)}, f32[32,128]{1,0:T(8,128)S(1)}, u32[]{:S(2)}, u32[]{:S(2)}) collective-permute-start(f32[32,128]{1,0:T(8,128)S(1)} %constant_dynamic-update-slice_fusion.6), channel_id=1, source_target_pairs={{0,4},{1,61},{2,6},{3,63},{4,8},{5,1},{6,10},{7,3},{8,12},{9,5},{1... | collective-permute-start | bytes 49160 | tf_op jit(solution)/shard_map/ppermute | solution.py:448
  45.6 5.4 %collective-permute-start.10 = (f32[32,128]{1,0:T(8,128)S(1)}, f32[32,128]{1,0:T(8,128)S(1)}, u32[]{:S(2)}, u32[]{:S(2)}) collective-permute-start(f32[32,128]{1,0:T(8,128)S(1)} %constant_dynamic-update-slice_fusion.6), channel_id=1, source_target_pairs={{0,2},{1,63},{2,4},{3,1},{4,6},{5,3},{6,8},{7,5},{8,10},{9,7},{10,... | collective-permute-start | bytes 49160 | tf_op jit(solution)/shard_map/ppermute | solution.py:448
  46.5 5.4 %collective-permute-start.13 = (f32[32,128]{1,0:T(8,128)S(1)}, f32[32,128]{1,0:T(8,128)S(1)}, u32[]{:S(2)}, u32[]{:S(2)}) collective-permute-start(f32[32,128]{1,0:T(8,128)S(1)} %collective-permute-done.11.far), channel_id=1, source_target_pairs={{0,1},{1,0},{2,3},{3,2},{4,5},{5,4},{6,7},{7,6},{8,9},{9,8},{10,11... | collective-permute-start | bytes 49160 | tf_op jit(solution)/shard_map/ppermute | solution.py:444
  51.0 1.2 %collective-permute-start.12 = (f32[32,128]{1,0:T(8,128)S(1)}, f32[32,128]{1,0:T(8,128)S(1)}, u32[]{:S(2)}, u32[]{:S(2)}) collective-permute-start(f32[32,128]{1,0:T(8,128)S(1)} %collective-permute-done.10.near), channel_id=1, source_target_pairs={{0,1},{1,0},{2,3},{3,2},{4,5},{5,4},{6,7},{7,6},{8,9},{9,8},{10,11... | collective-permute-start | bytes 49160 | tf_op jit(solution)/shard_map/ppermute | solution.py:444
  52.2 5.7 %copy-start.2 = (f32[2,32,256]{2,1,0:T(8,128)S(1)}, f32[2,32,256]{2,1,0:T(8,128)}, u32[]{:S(2)}) copy-start(f32[2,32,256]{2,1,0:T(8,128)} %prior.1) | copy-start | bytes 196612
  56.5 1.4 %collective-permute-start.14 = (f32[2,2,32,256]{3,2,1,0:T(8,128)S(1)}, f32[2,2,32,256]{3,2,1,0:T(8,128)S(1)}, u32[]{:S(2)}, u32[]{:S(2)}) collective-permute-start(f32[2,2,32,256]{3,2,1,0:T(8,128)S(1)} %get-tuple-element.16), channel_id=1, source_target_pairs={{0,1},{1,0},{2,3},{3,2},{4,5},{5,4},{6,7},{7,6},{8,9},{9,8},{10,11... | collective-permute-start | bytes 393224 | tf_op jit(solution)/shard_map/ppermute | solution.py:444
  58.7 6.1 %collective-permute-start.15 = (f32[2,2,32,256]{3,2,1,0:T(8,128)S(1)}, f32[2,2,32,256]{3,2,1,0:T(8,128)S(1)}, u32[]{:S(2)}, u32[]{:S(2)}) collective-permute-start(f32[2,2,32,256]{3,2,1,0:T(8,128)S(1)} %get-tuple-element.18.refs_0_.refs_1_), channel_id=1, source_target_pairs={{0,64},{64,128},{128,192},{192,0},{1,65},{65,129},{129,193},{193,1... | collective-permute-start | bytes 393224 | tf_op jit(solution)/shard_map/ppermute | solution.py:537
  59.9 4.9 %collective-permute-start.18 = (f32[2,2,32,256]{3,2,1,0:T(8,128)S(1)}, f32[2,2,32,256]{3,2,1,0:T(8,128)S(1)}, u32[]{:S(2)}, u32[]{:S(2)}) collective-permute-start(f32[2,2,32,256]{3,2,1,0:T(8,128)S(1)} %get-tuple-element.19.refs_1_.refs_2_), channel_id=1, source_target_pairs={{0,192},{64,0},{128,64},{192,128},{1,193},{65,1},{129,65},{193,129... | collective-permute-start | bytes 393224 | tf_op jit(solution)/shard_map/ppermute | solution.py:537
  61.4 6.1 %collective-permute-start.20 = (f32[2,2,32,256]{3,2,1,0:T(8,128)S(1)}, f32[2,2,32,256]{3,2,1,0:T(8,128)S(1)}, u32[]{:S(2)}, u32[]{:S(2)}) collective-permute-start(f32[2,2,32,256]{3,2,1,0:T(8,128)S(1)} %get-tuple-element.18.refs_0_.refs_1_), channel_id=1, source_target_pairs={{0,192},{64,0},{128,64},{192,128},{1,193},{65,1},{129,65},{193,129... | collective-permute-start | bytes 393224 | tf_op jit(solution)/shard_map/ppermute | solution.py:537
  62.6 5.0 %collective-permute-start.16 = (f32[2,2,32,256]{3,2,1,0:T(8,128)S(1)}, f32[2,2,32,256]{3,2,1,0:T(8,128)S(1)}, u32[]{:S(2)}, u32[]{:S(2)}) collective-permute-start(f32[2,2,32,256]{3,2,1,0:T(8,128)S(1)} %get-tuple-element.19.refs_1_.refs_2_), channel_id=1, source_target_pairs={{0,64},{64,128},{128,192},{192,0},{1,65},{65,129},{129,193},{193,1... | collective-permute-start | bytes 393224 | tf_op jit(solution)/shard_map/ppermute | solution.py:537
  64.8 6.6 %collective-permute-start.17 = (f32[2,2,32,256]{3,2,1,0:T(8,128)S(1)}, f32[2,2,32,256]{3,2,1,0:T(8,128)S(1)}, u32[]{:S(2)}, u32[]{:S(2)}) collective-permute-start(f32[2,2,32,256]{3,2,1,0:T(8,128)S(1)} %collective-permute-done.15.refs_2_.refs_3_), channel_id=1, source_target_pairs={{0,64},{64,128},{128,192},{192,0},{1,65},{65,129},{129,193},{193,1... | collective-permute-start | bytes 393224 | tf_op jit(solution)/shard_map/ppermute | solution.py:537
  64.8 6.6 %collective-permute-start.19 = (f32[2,2,32,256]{3,2,1,0:T(8,128)S(1)}, f32[2,2,32,256]{3,2,1,0:T(8,128)S(1)}, u32[]{:S(2)}, u32[]{:S(2)}) collective-permute-start(f32[2,2,32,256]{3,2,1,0:T(8,128)S(1)} %collective-permute-done.18.refs_7_.refs_8_), channel_id=1, source_target_pairs={{0,192},{64,0},{128,64},{192,128},{1,193},{65,1},{129,65},{193,129... | collective-permute-start | bytes 393224 | tf_op jit(solution)/shard_map/ppermute | solution.py:537
